TPU v7x, 256 devices: a whole 4x4x8 slice. The times are simulated.
256 devices in a mesh: blk: 64 (over x, y_hi, z), sub: 4 (over y_lo, core).
Axes of the slice: x: 4, y: 4 (y_hi: 2, y_lo: 2; y = y_hi * 2 + y_lo), z: 8, core: 2. Of those that a mesh axis runs over, the one named last changes fastest.
Arguments:
- queries: bfloat16 [524288, 512], P(('blk', 'sub')), may hold values from -100 to 100
- keys: bfloat16 [524288, 512], P(('blk', 'sub')), may hold values from -6 to 6
- values: bfloat16 [524288, 512], P(('blk', 'sub')), may hold values from -6 to 6
- global_ids: int32 [2], replicated, may hold values from 0 to 4095
- rand_pick: int32 [4096, 3], P(('blk', 'sub')), may hold values from 0 to 15
Outputs:
- attended: bfloat16 [524288, 512], P(('blk', 'sub'))
Inputs may be any that keep to these rules, and one draw needn't show every extreme that they name: `global_ids`: two block numbers below 4096, possibly equal.
All inputs are finite; a program needn't handle non-finite values.
Results may differ from a plain program's by a relative error of at most 0.0047.
Values may be sent and summed in bfloat16 or wider, within the bound.
No kernel may reach another device: no remote copies, remote signals or barrier semaphores. Data moves between devices by JAX's collectives and lax.ppermute only.
A program may use at most 128 MiB of HBM per device.

v0:
```python
import math

import jax
import jax.numpy as jnp
from jax import lax
from jax.sharding import PartitionSpec as P

H = 4
DH = 128
BS = 128


def padded_2(block, sides, width):
    for axis, dim in sides:
        count = lax.axis_size(axis)
        forward = [(i, i + 1) for i in range(count - 1)]
        forward.append((count - 1, 0))
        backward = [(target, source) for source, target in forward]
        low = lax.ppermute(
            lax.slice_in_dim(block, block.shape[dim] - width, None, axis=dim), axis, forward
        )
        high = lax.ppermute(lax.slice_in_dim(block, 0, width, axis=dim), axis, backward)
        block = jnp.concatenate([low, block, high], axis=dim)
    return block


def spread(shard, axis, root):
    mine = lax.axis_index(axis) == root
    return lax.psum(jnp.where(mine, shard, jnp.zeros_like(shard)), axis)


def from_behind(value, axis, steps):
    count = lax.axis_size(axis)
    pairs = [(source, (source + steps) % count) for source in range(count)]
    return lax.ppermute(value, axis, pairs)


def attend(query_rows, key_rows, value_rows):
    group_count = query_rows.shape[0]
    score_scale = 1.0 / math.sqrt(DH)
    query_heads = query_rows.reshape(group_count, BS, H, DH)
    key_heads = key_rows.reshape(group_count, -1, H, DH)
    value_heads = value_rows.reshape(group_count, -1, H, DH)
    scores = (
        jnp.einsum("gqhd,gkhd->ghqk", query_heads, key_heads, preferred_element_type=jnp.float32)
        * score_scale
    )
    row_max = jnp.max(scores, axis=-1, keepdims=True)
    weights = jnp.exp(scores - row_max)
    totals = jnp.sum(weights, axis=-1)
    rounded = weights.astype(jnp.bfloat16)
    mixed = jnp.einsum("ghqk,gkhd->gqhd", rounded, value_heads, preferred_element_type=jnp.float32)
    mixed = mixed / jnp.transpose(totals, (0, 2, 1))[..., None]
    return mixed.astype(jnp.bfloat16).reshape(group_count, BS, H * DH)


def own_piece(key_value, global_block, blocks):
    return lax.dynamic_slice_in_dim(key_value, global_block % blocks * BS, BS, 0)


def per_device(queries, keys, values, global_ids, rand_pick):
    row_count, feature_width = queries.shape
    blocks = row_count // BS
    key_value = jnp.concatenate([keys, values], axis=1)
    padded = padded_2(key_value, ((("blk", "sub"), 0),), BS)
    cycle_size = lax.axis_size("blk")
    quarter = cycle_size // 4
    shared = []
    for which_global in range(2):
        global_block = global_ids[which_global]
        block_rows = own_piece(key_value, global_block, blocks)
        shared.append(spread(block_rows, ("blk", "sub"), global_block // blocks))
    global_keys = jnp.concatenate(shared, axis=0)
    remote = []
    current = key_value
    for hop_count in range(3):
        current = from_behind(current, "blk", -quarter)
        remote.append(current)
    remote_blocks = jnp.stack(remote).reshape(3, blocks, BS, 2 * feature_width)
    source_index = jnp.arange(3, dtype=jnp.int32)[None, :]

    def one_group(group_index):
        first_block = group_index * 4
        window_span = lax.dynamic_slice_in_dim(padded, first_block * BS, 6 * BS, 0)
        windows = jnp.stack([window_span[member * BS : (member + 3) * BS] for member in range(4)])
        random_picks = lax.dynamic_slice_in_dim(rand_pick, first_block, 4, 0)
        chosen = remote_blocks[source_index, random_picks].reshape(4, 3 * BS, 2 * feature_width)
        shared_keys = jnp.broadcast_to(global_keys[None], (4, 2 * BS, 2 * feature_width))
        gathered = jnp.concatenate([windows, shared_keys, chosen], axis=1)
        query_rows = lax.dynamic_slice_in_dim(queries, first_block * BS, 4 * BS, 0).reshape(
            4, BS, feature_width
        )
        return attend(query_rows, gathered[..., :feature_width], gathered[..., feature_width:])

    result = lax.map(one_group, jnp.arange(blocks // 4, dtype=jnp.int32))
    return result.reshape(row_count, feature_width)


def solution(mesh):
    return jax.shard_map(
        per_device,
        mesh=mesh,
        in_specs=(
            P(("blk", "sub"), None),
            P(("blk", "sub"), None),
            P(("blk", "sub"), None),
            P(),
            P(("blk", "sub"), None),
        ),
        out_specs=P(("blk", "sub"), None),
        check_vma=False,
    )
```

profile of v0, /device:TPU:2, one launch (start us, length us, event | category | flops | bytes accessed | tf_op | source)
XLA Modules:
  0.0 688.2 jit_solution(11012248107414518001)
XLA Ops:
  13.3 90.1 %collective-permute-done.2 = bf16[2048,1024]{1,0:T(8,128)(2,1)S(1)} collective-permute-done((bf16[2048,1024]{1,0:T(8,128)(2,1)S(1)}, bf16[2048,1024]{1,0:T(8,128)(2,1)S(1)}, u32[]{:S(2)}, u32[]{:S(2)}) %collective-permute-start.2) | collective-permute-done | bytes 4194336 | tf_op jit(solution)/shard_map/ppermute | solution.py:35
  106.1 90.7 %collective-permute-done.3 = bf16[2048,1024]{1,0:T(8,128)(2,1)} collective-permute-done((bf16[2048,1024]{1,0:T(8,128)(2,1)S(1)}, bf16[2048,1024]{1,0:T(8,128)(2,1)}, u32[]{:S(2)}, u32[]{:S(2)}) %collective-permute-start.3) | collective-permute-done | bytes 4194336 | tf_op jit(solution)/shard_map/ppermute | solution.py:35
  206.6 9.1 %collective-permute-start.1 = (bf16[128,1024]{1,0:T(8,128)(2,1)S(1)}, bf16[128,1024]{1,0:T(8,128)(2,1)S(1)}, u32[]{:S(2)}, u32[]{:S(2)}) collective-permute-start(bf16[128,1024]{1,0:T(8,128)(2,1)S(1)} %get-tuple-element.189), channel_id=1, source_target_pairs={{1,0},{2,1},{3,2},{4,3},{5,4},{6,5},{7,6},{8,7},{9,8},{10,9},{11,1... | collective-permute-start | bytes 786440 | tf_op jit(solution)/shard_map/ppermute | solution.py:22
  215.6 252.5 %all-reduce.3.cloned.1.call-done = (bf16[128,1024]{1,0:T(8,128)(2,1)}, bf16[128,1024]{1,0:T(8,128)(2,1)}) async-done(((bf16[128,1024]{1,0:T(8,128)(2,1)}, bf16[128,1024]{1,0:T(8,128)(2,1)}), (bf16[128,1024]{1,0:T(8,128)(2,1)}, bf16[128,1024]{1,0:T(8,128)(2,1)})) %all-reduce.3.cloned.1.call-update) | async-done | bytes 524304 | tf_op jit(solution)/shard_map/psum | solution.py:29
  470.0 4.2 pad_maximum_fusion.2
  474.9 8.3 %pad_maximum_fusion.1 = bf16[3,16,128,1024]{3,2,1,0:T(8,128)(2,1)} fusion(bf16[1,16,128,1024]{3,2,1,0:T(8,128)(2,1)} %bitcast.4, bf16[1,16,128,1024]{3,2,1,0:T(8,128)(2,1)} %bitcast.3, bf16[1,16,128,1024]{3,2,1,0:T(8,128)(2,1)S(1)} %bitcast.61), kind=kLoop, calls=%fused_computation.29 | loop fusion | flops 12582912 | bytes 25165824 | tf_op jit(solution)/shard_map/stack | solution.py:79
  483.2 198.2 %while.13 = (s32[]{:T(128)}, bf16[4,4,128,512]{3,2,1,0:T(8,128)(2,1)}, s32[4]{0:T(128)S(1)}, bf16[2304,1024]{1,0:T(8,128)(2,1)}, bf16[256,1024]{1,0:T(8,128)(2,1...) while((s32[]{:T(128)}, ...), condition=%wide.region_5.6_spmd.clone, body=%wide.region_2.5_spmd.clone.sunk | while | flops 1141370880 | bytes 137930112 | solution.py:95
  488.8 5.3 gather_fusion
  502.6 6.3 copy.45
  518.7 6.4 copy.44
  525.0 6.6 divide_convert_fusion.2
  538.3 5.3 gather_fusion
  548.3 3.8 fusion.37
  552.1 6.3 copy.45
  568.1 6.4 copy.44
  574.5 6.6 divide_convert_fusion.2
  587.8 5.3 gather_fusion
  601.6 6.3 copy.45
  617.7 6.4 copy.44
  624.0 6.6 divide_convert_fusion.2
  637.5 5.3 gather_fusion
  651.3 6.3 copy.45
  667.3 6.4 copy.44
  673.7 6.6 divide_convert_fusion.2
  (99 shorter events, 107.8 us)
Async XLA Ops:
  6.5 2.2 copy-start.4
  6.5 192.3 %copy-start.6 = (s32[2]{0:T(128)S(1)}, s32[2]{0:T(128)}, u32[]{:S(2)}) copy-start(s32[2]{0:T(128)} %param.10) | copy-start | bytes 28
  6.5 461.6 %all-reduce.3.cloned.1.call-start = ((), (), s32[]{:S(2)}) async-start(), calls=%async_computation | async-start | bytes 1048576 | tf_op jit(solution)/shard_map/psum | solution.py:29
  9.1 2.0 copy-start.1
  11.0 92.3 %collective-permute-start.2 = (bf16[2048,1024]{1,0:T(8,128)(2,1)S(1)}, bf16[2048,1024]{1,0:T(8,128)(2,1)S(1)}, u32[]{:S(2)}, u32[]{:S(2)}) collective-permute-start(bf16[2048,1024]{1,0:T(8,128)(2,1)S(1)} %constant_dynamic-update-slice_fusion.1), channel_id=1, source_target_pairs={{0,192},{4,196},{8,200},{12,204},{16,208},{20,212},{24,216},{28,22... | collective-permute-start | bytes 12582920 | tf_op jit(solution)/shard_map/ppermute | solution.py:35
  103.3 2.0 copy-start.2
  105.3 91.6 %collective-permute-start.3 = (bf16[2048,1024]{1,0:T(8,128)(2,1)S(1)}, bf16[2048,1024]{1,0:T(8,128)(2,1)}, u32[]{:S(2)}, u32[]{:S(2)}) collective-permute-start(bf16[2048,1024]{1,0:T(8,128)(2,1)S(1)} %collective-permute-done.2), channel_id=1, source_target_pairs={{0,192},{4,196},{8,200},{12,204},{16,208},{20,212},{24,216},{28,22... | collective-permute-start | bytes 12582920 | tf_op jit(solution)/shard_map/ppermute | solution.py:35
  196.9 277.3 %collective-permute-start.4 = (bf16[2048,1024]{1,0:T(8,128)(2,1)}, bf16[2048,1024]{1,0:T(8,128)(2,1)}, u32[]{:S(2)}, u32[]{:S(2)}) collective-permute-start(bf16[2048,1024]{1,0:T(8,128)(2,1)} %collective-permute-done.3), channel_id=1, source_target_pairs={{0,192},{4,196},{8,200},{12,204},{16,208},{20,212},{24,216},{28,22... | collective-permute-start | bytes 12582920 | tf_op jit(solution)/shard_map/ppermute | solution.py:35
  206.5 263.5 %collective-permute-start = (bf16[128,1024]{1,0:T(8,128)(2,1)S(1)}, bf16[128,1024]{1,0:T(8,128)(2,1)S(1)}, u32[]{:S(2)}, u32[]{:S(2)}) collective-permute-start(bf16[128,1024]{1,0:T(8,128)(2,1)S(1)} %get-tuple-element.190), channel_id=1, source_target_pairs={{0,1},{1,2},{2,3},{3,4},{4,5},{5,6},{6,7},{7,8},{8,9},{9,10},{10,1... | collective-permute-start | bytes 786440 | tf_op jit(solution)/shard_map/ppermute | solution.py:19
  206.6 263.4 %collective-permute-start.1 = (bf16[128,1024]{1,0:T(8,128)(2,1)S(1)}, bf16[128,1024]{1,0:T(8,128)(2,1)S(1)}, u32[]{:S(2)}, u32[]{:S(2)}) collective-permute-start(bf16[128,1024]{1,0:T(8,128)(2,1)S(1)} %get-tuple-element.189), channel_id=1, source_target_pairs={{1,0},{2,1},{3,2},{4,3},{5,4},{6,5},{7,6},{8,7},{9,8},{10,9},{11,1... | collective-permute-start | bytes 786440 | tf_op jit(solution)/shard_map/ppermute | solution.py:22
  470.0 4.9 copy-start.3
  474.9 8.3 %copy-start.5 = (s32[16,3]{0,1:T(4,128)S(1)}, s32[16,3]{0,1:T(4,128)}, u32[]{:S(2)}) copy-start(s32[16,3]{0,1:T(4,128)} %param.11) | copy-start | bytes 580
  513.7 3.2 copy-start
  563.2 3.2 copy-start
  612.7 3.2 copy-start
  662.4 3.2 copy-start
Sparse Core Ops, SparseCore 0:
  206.6 261.4 all-reduce.2
where the time goes:
time: 691 us; the launch traced here: 688 us
  waiting for transfers between devices  433 us (63%)
  local copies, waits for them, and re-layouts  140 us (20%)
  matrix products  40.5 us (6%)
  other arithmetic  37.1 us (5%)
  between operations  18.3 us (3%)
  starting transfers between devices  14.1 us (2%)
    psum x1, waiting for transfers between devices, spread(): return lax.psum(jnp.where(mine, shard, jnp.zeros_like(shard)), axis)  252 us
    ppermute x3, waiting for transfers between devices, from_behind(): return lax.ppermute(value, axis, pairs)  181 us
    slice x8, local copies, waits for them, and re-layouts, one_group(): gathered[..., :feature_width]  40.7 us
    dot_general x4, matrix products, attend(): jnp.einsum('ghqk,gkhd->gqhd', rounded, value_heads, preferred_element_typ...  26.4 us
    slice x4, local copies, waits for them, and re-layouts, one_group(): gathered[..., feature_width:]  25.4 us
    gather x4, local copies, waits for them, and re-layouts, one_group(): remote_blocks[source_index, random_picks]  21.3 us
    another operation x4, local copies, waits for them, and re-layouts, one_group(): jnp.stack([window_span[member * BS:(member + 3) * BS] for member in range...  14.6 us
    dot_general x4, matrix products, attend(): jnp.einsum('gqhd,gkhd->ghqk', query_heads, key_heads, preferred_element_t...  14.1 us
  transfers between devices with their start and end apart: 6, of which 3 were waited for; matrix products, arithmetic and copies ran while one was open for 1% of the time, Pallas kernels for 0%

commit v1 on v0

v1 whole, which is shorter than its diff:
```python
import functools
import math

import jax
import jax.numpy as jnp
from jax import lax
from jax.experimental import pallas as pl
from jax.experimental.pallas import tpu as pltpu
from jax.sharding import PartitionSpec as P


H = 4
DH = 128
BS = 128
QB = 16
GROUP = 4
W = H * DH
SCALE_LOG2 = math.log2(math.e) / math.sqrt(DH)
G_N, A_N, B_N = 2, 6, 8
NEAR_VMEM, SCORE_VMEM, LAST_VMEM = 24 << 20, 24 << 20, 12 << 20
ANY = pl.BlockSpec(memory_space=pl.ANY)
VM = pl.BlockSpec(memory_space=pltpu.VMEM)
SM = pl.BlockSpec(memory_space=pltpu.SMEM)
HB = pl.BlockSpec(memory_space=pltpu.HBM)


def first_two(gids, blocks):
    p0 = blocks - 1 - lax.rem(gids[0], blocks)
    p1 = blocks - 1 - lax.rem(gids[1], blocks)
    p1 = jnp.where(p1 == p0, lax.rem(p0 + 1, blocks), p1)
    return p0, p1, jnp.minimum(p0, p1), jnp.maximum(p0, p1)


def block_at(position, places, blocks):
    p0, p1, low, high = places
    if position == 0:
        return blocks - 1 - p0
    if position == 1:
        return blocks - 1 - p1
    k = position - 2
    k = k + (k >= low).astype(jnp.int32)
    return blocks - 1 - (k + (k >= high).astype(jnp.int32))


def position_of(block, places, blocks):
    p0, p1, low, high = places
    label = blocks - 1 - block
    rest = label - (label > low).astype(jnp.int32) - (label > high).astype(jnp.int32) + 2
    return jnp.where(label == p0, 0, jnp.where(label == p1, 1, rest))


def pack_kernel(start, count, joined, ends, gids, keys, values, *refs):
    blocks = keys.shape[0]
    places = first_two(gids, blocks)
    outs, (buf, in_sem, out_sem) = refs[:-3], refs[-3:]
    if joined:
        buf = outs[0]
    wanted = [block_at(start + i, places, blocks) for i in range(count)]
    if ends:
        wanted += [blocks - 1, 0]
    loads, stores = [], []
    for half, ref in enumerate((keys, values)):
        for i, block in enumerate(wanted):
            copy = pltpu.make_async_copy(ref.at[block], buf.at[half, i], in_sem.at[half, i])
            copy.start()
            loads.append((half, i, copy))
    for half, i, load in loads:
        load.wait()
        if joined:
            continue
        target = outs[half].at[i] if i < count else outs[2 + i - count].at[half]
        copy = pltpu.make_async_copy(buf.at[half, i], target, out_sem.at[half, i])
        copy.start()
        stores.append(copy)
    for copy in stores:
        copy.wait()


def pack(gids, keys, values, start, count, joined=False, ends=False):
    shapes = [jax.ShapeDtypeStruct((count, BS, W), keys.dtype)] * 2
    if joined:
        shapes = [jax.ShapeDtypeStruct((2, count, BS, W), keys.dtype)]
    if ends:
        shapes += [jax.ShapeDtypeStruct((2, BS, W), keys.dtype)] * 2
    places = count + 2 * ends
    return pl.pallas_call(
        functools.partial(pack_kernel, start, count, joined, ends),
        out_shape=shapes,
        in_specs=[SM, HB, HB],
        out_specs=[VM if joined else ANY] * len(shapes),
        scratch_shapes=[
            pltpu.VMEM((2, 1 if joined else places, BS, W), keys.dtype),
            pltpu.SemaphoreType.DMA((2, places)),
            pltpu.SemaphoreType.DMA((2, places)),
        ],
        compiler_params=pltpu.CompilerParams(vmem_limit_bytes=56 << 20),
        cost_estimate=pl.CostEstimate(
            flops=0, transcendentals=0, bytes_accessed=places * 4 * BS * W * 2
        ),
        name="pack",
    )(gids, keys, values)


def dot_t(a, b):
    return lax.dot_general(a, b, (((1,), (1,)), ((), ())), preferred_element_type=jnp.float32)


def dot(a, b):
    return lax.dot_general(a, b, (((1,), (0,)), ((), ())), preferred_element_type=jnp.float32)


def head(h):
    return slice(h * DH, (h + 1) * DH)


def wide(column):
    return jnp.broadcast_to(column, (BS, DH))


def ones(rows):
    return jnp.ones((rows, DH), jnp.bfloat16)


def top_of(scores, old=None):
    tops = [jnp.max(s, axis=1, keepdims=True) for s in scores]
    top = wide(functools.reduce(jnp.maximum, tops))
    return top if old is None else jnp.maximum(top, old)


def weigh(s, top):
    parts = [
        jnp.exp2((s[:, n : n + DH] - top) * SCALE_LOG2) for n in range(0, s.shape[1], DH)
    ]
    return jnp.concatenate(parts, axis=1).astype(jnp.bfloat16)


def mix(w, v):
    return dot(w, jnp.concatenate([v, ones(v.shape[0])], axis=1))


def state_of(blocks):
    return [jax.ShapeDtypeStruct((blocks, H, BS, DH), jnp.float32)] * 3


def fetch_pick(position, parts, dst, sem):
    at = 0
    for part in parts:
        count = part.shape[0]

        @pl.when((position >= at) & (position < at + count))
        def _(part=part, at=at, count=count):
            pltpu.make_async_copy(part.at[jnp.clip(position - at, 0, count - 1)], dst, sem).start()

        at += count


def near_kernel(blocks, gids, picks, place, q_ref, keys, values, low, high, first, last, *refs):
    side, refs = refs[:5], refs[5:]
    pieces, refs = refs[:4], refs[4:]
    top_ref, total_ref, acc_ref, kbuf, vbuf, shared, buf, sem, shared_sem, pick_sem = refs
    places = first_two(gids, blocks)
    copies = []
    for half, (ref, dst) in enumerate(((keys, kbuf), (values, vbuf))):
        copies.append(pltpu.make_async_copy(ref, dst.at[pl.ds(BS, blocks * BS)], sem.at[half, 0]))
    for n, piece in enumerate(pieces):
        quarter = jnp.bitwise_and(jnp.bitwise_xor(place[0], n), 3)
        rows = piece.shape[1]
        start = jnp.bitwise_and(quarter, 1) * (2 * rows) + jnp.right_shift(quarter, 1) * rows
        at = pl.ds(pl.multiple_of(start, rows), rows)
        copies.append(pltpu.make_async_copy(piece, shared.at[:, at], shared_sem.at[n]))
    for copy in copies:
        copy.start()

    halos = (
        (1, place[3] == 0, first, low, 0),
        (2, place[3] == 1, last, high, (blocks + 1) * BS),
    )
    for n, wraps, there, here, at in halos:
        for half, dst in enumerate((kbuf, vbuf)):

            @pl.when(wraps)
            def _(there=there, half=half, dst=dst, at=at, n=n):
                pltpu.make_async_copy(there.at[half], dst.at[pl.ds(at, BS)], sem.at[half, n]).start()

            @pl.when(jnp.logical_not(wraps))
            def _(here=here, half=half, dst=dst, at=at, n=n):
                pltpu.make_async_copy(here.at[half], dst.at[pl.ds(at, BS)], sem.at[half, n]).start()

    g, a_k, b_k, a_v, b_v = side

    def fetch(j, carry):
        position = position_of(picks[j, 0], places, blocks)
        fetch_pick(position, (g.at[0], a_k, b_k), buf.at[j, 0], pick_sem.at[j, 0])
        fetch_pick(position, (g.at[1], a_v, b_v), buf.at[j, 1], pick_sem.at[j, 1])
        return carry

    lax.fori_loop(0, blocks, fetch, 0)
    for copy in copies:
        copy.wait()
    for n, _, _, here, at in halos:
        for half, dst in enumerate((kbuf, vbuf)):
            pltpu.make_async_copy(here.at[half], dst.at[pl.ds(at, BS)], sem.at[half, n]).wait()

    def step(j, carry):
        rows = pl.ds(pl.multiple_of(j * BS, BS), BS)
        span = pl.ds(pl.multiple_of(j * BS, BS), 3 * BS)
        for half in range(2):
            pltpu.make_async_copy(b_k.at[0], buf.at[j, half], pick_sem.at[j, half]).wait()
        for first in range(0, H, GROUP):
            heads = range(first, first + GROUP)
            keys_of, values_of = [
                [
                    jnp.concatenate(
                        [
                            own[span, head(h)],
                            buf[j, half, :, head(h)],
                            shared[0, half * BS : (half + 1) * BS, head(h)],
                            shared[1, half * BS : (half + 1) * BS, head(h)],
                        ],
                        axis=0,
                    )
                    for h in heads
                ]
                for half, own in enumerate((kbuf, vbuf))
            ]
            scores = [dot_t(q_ref[rows, head(h)], k) for h, k in zip(heads, keys_of)]
            tops = [top_of([s]) for s in scores]
            weights = [weigh(s, top) for s, top in zip(scores, tops)]
            mixed = [mix(w, v) for w, v in zip(weights, values_of)]
            for n, h in enumerate(heads):
                top_ref[j, h] = tops[n]
                total_ref[j, h] = mixed[n][:, DH:]
                acc_ref[j, h] = mixed[n][:, :DH]
        return carry

    lax.fori_loop(0, blocks, step, 0)


def near(gids, picks, place, queries, keys, values, halos, from_right, pieces):
    rows = queries.shape[0]
    blocks = rows // BS
    return pl.pallas_call(
        functools.partial(near_kernel, blocks),
        out_shape=state_of(blocks),
        in_specs=[SM, SM, SM, VM] + [ANY] * 15,
        out_specs=[VM] * 3,
        scratch_shapes=[
            pltpu.VMEM(((blocks + 2) * BS, W), keys.dtype),
            pltpu.VMEM(((blocks + 2) * BS, W), keys.dtype),
            pltpu.VMEM((2, 2 * BS, W), keys.dtype),
            pltpu.VMEM((blocks, 2, BS, W), keys.dtype),
            pltpu.SemaphoreType.DMA((2, 3)),
            pltpu.SemaphoreType.DMA((4,)),
            pltpu.SemaphoreType.DMA((blocks, 2)),
        ],
        compiler_params=pltpu.CompilerParams(vmem_limit_bytes=NEAR_VMEM),
        cost_estimate=pl.CostEstimate(
            flops=rows * 6 * BS * W * 4, transcendentals=rows * 6 * BS * H, bytes_accessed=24 << 20
        ),
        name="near",
    )(gids, picks, place, queries, keys, values, *halos, *from_right, *pieces)


def score_kernel(blocks, gids, picks, q_ref, *refs):
    left, (g_o, ak_o, bk_o), refs = refs[:5], refs[5:8], refs[8:]
    top_in, total_in, acc_in, weight_ref, share_ref, acc_ref, buf, sem = refs
    g_l, ak_l, bk_l, av_l, bv_l = left
    places = first_two(gids, blocks)

    def fetch(j, carry):
        near_at = position_of(picks[j, 2], places, blocks)
        far_at = position_of(picks[j, 1], places, blocks)
        fetch_pick(near_at, (g_l.at[0], ak_l, bk_l), buf.at[j, 0], sem.at[j, 0])
        fetch_pick(far_at, (g_o.at[0], ak_o, bk_o), buf.at[j, 1], sem.at[j, 1])
        fetch_pick(near_at, (g_l.at[1], av_l, bv_l), buf.at[j, 2], sem.at[j, 2])
        return carry

    lax.fori_loop(0, blocks, fetch, 0)

    def step(j, carry):
        rows = pl.ds(pl.multiple_of(j * BS, BS), BS)
        for n in range(3):
            pltpu.make_async_copy(bk_o.at[0], buf.at[j, n], sem.at[j, n]).wait()
        q = [q_ref[rows, head(h)] for h in range(H)]
        k = [jnp.concatenate([buf[j, 0, :, head(h)], buf[j, 1, :, head(h)]], axis=0) for h in range(H)]
        v = [buf[j, 2, :, head(h)] for h in range(H)]
        old_top = [top_in[j, h] for h in range(H)]
        old_total = [total_in[j, h] for h in range(H)]
        old_acc = [acc_in[j, h] for h in range(H)]
        scores = [dot_t(q[h], k[h]) for h in range(H)]
        tops = [top_of([scores[h]], old_top[h]) for h in range(H)]
        weights = [weigh(scores[h], tops[h]) for h in range(H)]
        mixed = [dot(weights[h][:, :BS], v[h]) for h in range(H)]
        sums = [dot(weights[h], ones(2 * BS)) for h in range(H)]
        fades = [jnp.exp2((old_top[h] - tops[h]) * SCALE_LOG2) for h in range(H)]
        shares = [1.0 / (sums[h] + fades[h] * old_total[h]) for h in range(H)]
        for h in range(H):
            weight_ref[j, h] = weights[h][:, BS:]
            share_ref[j, h] = shares[h]
            acc_ref[j, h] = mixed[h] + old_acc[h] * fades[h]
        return carry

    lax.fori_loop(0, blocks, step, 0)


def score(gids, picks, queries, from_left, opposite, state):
    rows = queries.shape[0]
    blocks = rows // BS
    floats = jax.ShapeDtypeStruct((blocks, H, BS, DH), jnp.float32)
    return pl.pallas_call(
        functools.partial(score_kernel, blocks),
        out_shape=[jax.ShapeDtypeStruct((blocks, H, BS, BS), queries.dtype), floats, floats],
        in_specs=[SM, SM, VM] + [ANY] * 8 + [VM] * 3,
        out_specs=[VM] * 3,
        input_output_aliases={12: 1, 13: 2},
        scratch_shapes=[
            pltpu.VMEM((blocks, 3, BS, W), queries.dtype),
            pltpu.SemaphoreType.DMA((blocks, 3)),
        ],
        compiler_params=pltpu.CompilerParams(vmem_limit_bytes=SCORE_VMEM),
        cost_estimate=pl.CostEstimate(
            flops=rows * BS * W * 6, transcendentals=rows * 2 * BS * H, bytes_accessed=30 << 20
        ),
        name="score",
    )(gids, picks, queries, *from_left, *opposite, *state)


def last_kernel(blocks, gids, picks, g, a_v, b_v, weights, share, acc, out, buf, obuf, sem, out_sem):
    places = first_two(gids, blocks)

    def fetch(j, carry):
        fetch_pick(position_of(picks[j, 1], places, blocks), (g.at[1], a_v, b_v), buf.at[j], sem.at[j])
        return carry

    lax.fori_loop(0, blocks, fetch, 0)

    def store(j):
        rows = pl.ds(pl.multiple_of(j * BS, BS), BS)
        return pltpu.make_async_copy(obuf.at[j], out.at[rows], out_sem.at[j])

    def step(j, carry):
        pltpu.make_async_copy(b_v.at[0], buf.at[j], sem.at[j]).wait()
        mixed = [(dot(weights[j, h], buf[j, :, head(h)]) + acc[j, h]) * share[j, h] for h in range(H)]
        for h in range(H):
            obuf[j, :, head(h)] = mixed[h].astype(obuf.dtype)
        store(j).start()
        return carry

    lax.fori_loop(0, blocks, step, 0)

    def drain(j, carry):
        store(j).wait()
        return carry

    lax.fori_loop(0, blocks, drain, 0)


def last(gids, picks, parts, weights, share, acc, like):
    rows = like.shape[0]
    blocks = rows // BS
    return pl.pallas_call(
        functools.partial(last_kernel, blocks),
        out_shape=jax.ShapeDtypeStruct(like.shape, like.dtype),
        in_specs=[SM, SM] + [ANY] * 3 + [VM] * 3,
        out_specs=ANY,
        scratch_shapes=[
            pltpu.VMEM((blocks, BS, W), like.dtype),
            pltpu.VMEM((blocks, BS, W), like.dtype),
            pltpu.SemaphoreType.DMA((blocks,)),
            pltpu.SemaphoreType.DMA((blocks,)),
        ],
        compiler_params=pltpu.CompilerParams(vmem_limit_bytes=LAST_VMEM),
        cost_estimate=pl.CostEstimate(
            flops=rows * BS * W * 2, transcendentals=0, bytes_accessed=10 << 20
        ),
        name="last",
    )(gids, picks, *parts, weights, share, acc)


ALL = ("blk", "sub")


def choose_kernel(gids, place, g, g_r, g_o, g_l, keep, give_1, give_2, give_3, sem):
    blocks = QB
    rows = keep.shape[1]
    p0, p1 = lax.rem(gids[0], blocks), lax.rem(gids[1], blocks)
    slots = (0, jnp.where(p0 == p1, 0, 1))
    outs = (keep, give_1, give_2, give_3)
    for i in range(2):
        distance = lax.rem(place[i + 1] + 4, 4)
        for d, source in enumerate((g, g_r, g_o, g_l)):

            @pl.when(distance == d)
            def _(i=i, source=source):
                for n, out in enumerate(outs):
                    quarter = jnp.bitwise_xor(place[0], n)
                    half = jnp.bitwise_and(quarter, 1)
                    at = pl.ds(pl.multiple_of(jnp.right_shift(quarter, 1) * rows, rows), rows)
                    pltpu.make_async_copy(source.at[half, slots[i], at], out.at[i], sem.at[i, n]).start()

    for i in range(2):
        for n, out in enumerate(outs):
            pltpu.make_async_copy(g.at[0, 0, pl.ds(0, rows)], out.at[i], sem.at[i, n]).wait()


def choose(gids, place, g, g_r, g_o, g_l):
    piece = jax.ShapeDtypeStruct((2, BS // 2, W), g.dtype)
    return pl.pallas_call(
        choose_kernel,
        out_shape=[piece] * 4,
        in_specs=[SM, SM] + [ANY] * 4,
        out_specs=[VM] * 4,
        scratch_shapes=[pltpu.SemaphoreType.DMA((2, 4))],
        compiler_params=pltpu.CompilerParams(vmem_limit_bytes=2 << 20),
        cost_estimate=pl.CostEstimate(flops=0, transcendentals=0, bytes_accessed=1 << 20),
        name="choose",
    )(gids, place, g, g_r, g_o, g_l)


def ends_kernel(gids, g_l, ak_l, av_l, g_r, bk_r, bv_r, tail, lead, sem):
    p0, p1, _, _ = first_two(gids, QB)
    cases = (
        (0, tail, g_l, (ak_l.at[0], av_l.at[0])),
        (QB - 1, lead, g_r, (bk_r.at[B_N - 1], bv_r.at[B_N - 1])),
    )
    for n, (label, out, g, rest) in enumerate(cases):
        for half in range(2):
            done = sem.at[n, half]

            @pl.when(p0 == label)
            def _(g=g, half=half, out=out, done=done):
                pltpu.make_async_copy(g.at[half, 0], out.at[half], done).start()

            @pl.when(p1 == label)
            def _(g=g, half=half, out=out, done=done):
                pltpu.make_async_copy(g.at[half, 1], out.at[half], done).start()

            @pl.when((p0 != label) & (p1 != label))
            def _(rest=rest, half=half, out=out, done=done):
                pltpu.make_async_copy(rest[half], out.at[half], done).start()

    for n, (_, out, _, rest) in enumerate(cases):
        for half in range(2):
            pltpu.make_async_copy(rest[half], out.at[half], sem.at[n, half]).wait()


def ends(gids, g_l, ak_l, av_l, g_r, bk_r, bv_r):
    block = jax.ShapeDtypeStruct((2, BS, W), g_l.dtype)
    return pl.pallas_call(
        ends_kernel,
        out_shape=[block] * 2,
        in_specs=[SM] + [ANY] * 6,
        out_specs=[VM] * 2,
        scratch_shapes=[pltpu.SemaphoreType.DMA((2, 2))],
        compiler_params=pltpu.CompilerParams(vmem_limit_bytes=2 << 20),
        cost_estimate=pl.CostEstimate(flops=0, transcendentals=0, bytes_accessed=1 << 20),
        name="ends",
    )(gids, g_l, ak_l, av_l, g_r, bk_r, bv_r)


def swap(value, bits):
    count = lax.axis_size(ALL)
    return lax.ppermute(value, ALL, [(i, i ^ bits) for i in range(count)])


def pick_slots(mask, a, b):
    return jnp.where(mask[:, None, None], a, b)


def spread(quarters, me, owners):
    value = quarters[0]
    differ = (me ^ owners) & 3
    given = [swap(quarters[n], n) for n in (1, 2, 3)]
    for n in (1, 2, 3):
        value = pick_slots(differ == n, given[n - 1], value)
    for bit in (2, 3, 4, 5):
        same = ((me >> bit) & 1) == ((owners >> bit) & 1)
        value = pick_slots(same, value, swap(value, 1 << bit))
    return [value] + [swap(value, n) for n in (1, 2, 3)]


def whole(queries, keys, values, global_ids, rand_pick):
    rows, width = queries.shape
    blocks = rows // BS
    count = lax.axis_size("blk")
    quarter = count // 4
    right = [(i, (i + quarter) % count) for i in range(count)]
    left = [(i, (i - quarter) % count) for i in range(count)]
    everyone = lax.axis_size(ALL)

    def to_right(v):
        return lax.ppermute(v, "blk", right)

    def to_left(v):
        return lax.ppermute(v, "blk", left)

    plane = everyone // 4

    def along(v, pairs):
        return lax.ppermute(
            v, ALL, [(p * plane + i, p * plane + j) for p in range(4) for i, j in pairs]
        )

    key_blocks = keys.reshape(blocks, BS, width)
    value_blocks = values.reshape(blocks, BS, width)
    (g,) = pack(global_ids, key_blocks, value_blocks, 0, G_N, joined=True)
    g_l, g_r = to_right(g), to_left(g)
    ak, av, tail, lead = pack(global_ids, key_blocks, value_blocks, G_N, A_N, ends=True)
    bk, bv = pack(global_ids, key_blocks, value_blocks, G_N + A_N, B_N)
    ak_l, av_l = to_right(ak), to_right(av)
    bk_r, bv_r = to_left(bk), to_left(bv)
    low = along(tail, [(i, i + 1) for i in range(plane - 1)])
    high = along(lead, [(i + 1, i) for i in range(plane - 1)])
    g_o = to_right(g_l)
    bk_l, bv_l = to_right(bk), to_right(bv)
    ak_r, av_r = to_left(ak), to_left(av)
    ak_o, bk_o = to_right(ak_l), to_left(bk_r)
    av_o, bv_o = to_right(av_l), to_left(bv_r)

    me = lax.axis_index(ALL)
    owners = global_ids // blocks
    distance = owners // plane - me // plane
    spot = me % plane
    edge = jnp.where(spot == 0, 0, jnp.where(spot == plane - 1, 1, 2))
    place = jnp.stack([me & 3, distance[0], distance[1], edge])
    far_tail, far_lead = ends(global_ids, g_l, ak_l, av_l, g_r, bk_r, bv_r)
    first = along(far_tail, [(plane - 1, 0)])
    final = along(far_lead, [(0, plane - 1)])
    quarters = choose(global_ids, place, g, g_r, g_o, g_l)
    pieces = spread(quarters, me, owners)

    state = near(
        global_ids,
        rand_pick,
        place,
        queries,
        keys,
        values,
        (low, high, first, final),
        (g_r, ak_r, bk_r, av_r, bv_r),
        pieces,
    )
    weights, share, acc = score(
        global_ids,
        rand_pick,
        queries,
        (g_l, ak_l, bk_l, av_l, bv_l),
        (g_o, ak_o, bk_o),
        state,
    )
    return last(global_ids, rand_pick, (g_o, av_o, bv_o), weights, share, acc, queries)


def solution(mesh):
    return jax.shard_map(
        whole,
        mesh=mesh,
        in_specs=(
            P(("blk", "sub"), None),
            P(("blk", "sub"), None),
            P(("blk", "sub"), None),
            P(),
            P(("blk", "sub"), None),
        ),
        out_specs=P(("blk", "sub"), None),
        check_vma=False,
    )
```

time: 691 us -> 226 us (0.33)
  waiting for transfers between devices: 433 us -> 101 us
  local copies, waits for them, and re-layouts: 140 us -> 19.4 us
  Pallas kernels: 0 us -> 47.6 us
  matrix products: 40.5 us -> 0 us
  starting transfers between devices: 14.1 us -> 54.4 us
  other arithmetic: 37.1 us -> 0.53 us
  between operations: 18.3 us -> 0.49 us
    psum x1 -> x0, waiting for transfers between devices: 252 us -> none  [spread(): return lax.psum(jnp.where(mine, shard, jnp.zeros_like(shard)), axis)]
    ppermute x5 -> x29, waiting for transfers between devices: 181 us -> 101 us  [the longest x8 49.2 us: to_right(): return lax.ppermute(v, 'blk', right)]
    slice x13 -> x0, local copies, waits for them, and re-layouts: 66.7 us -> none  [the longest x8 40.7 us: one_group(): gathered[..., :feature_width]]
    pallas_call x0 -> x8, Pallas kernels: none -> 47.6 us  [the longest x1 17 us: near(): pl.pallas_call(functools.partial(near_kernel, blocks), out_shape=state_of...]
    dot_general x8 -> x0, matrix products: 40.5 us -> none  [the longest x4 26.4 us: attend(): jnp.einsum('ghqk,gkhd->gqhd', rounded, value_heads, preferred_element_typ...]
    ppermute x5 -> x29, starting transfers between devices: 14.1 us -> 54.4 us  [the longest x10 22.3 us: swap(): return lax.ppermute(value, ALL, [(i, i ^ bits) for i in range(count)])]
    gather x4 -> x0, local copies, waits for them, and re-layouts: 21.3 us -> none  [one_group(): remote_blocks[source_index, random_picks]]
    concatenate x14 -> x0, other arithmetic: 19.6 us -> none  [the longest x4 13.4 us: one_group(): gathered = jnp.concatenate([windows, shared_keys, chosen], axis=1)]
  transfers between devices with their start and end apart: 6 -> 29, of which waited for: 3 -> 13; matrix products, arithmetic and copies ran while one was open for 1% -> 1% of each run, Pallas kernels for 0% -> 18%
where the time goes in v1:
time: 226 us; the launch traced here: 223 us
  waiting for transfers between devices  101 us (45%)
  starting transfers between devices  54.4 us (24%)
  Pallas kernels  47.6 us (21%)
  local copies, waits for them, and re-layouts  19.4 us (9%)
    ppermute x8, waiting for transfers between devices, to_right(): return lax.ppermute(v, 'blk', right)  49.2 us
    ppermute x7, waiting for transfers between devices, to_left(): return lax.ppermute(v, 'blk', left)  36.8 us
    ppermute x10, starting transfers between devices, swap(): return lax.ppermute(value, ALL, [(i, i ^ bits) for i in range(count)])  22.3 us
    unnamed x61, local copies, waits for them, and re-layouts  19.4 us
    pallas_call x1, Pallas kernels, near(): pl.pallas_call(functools.partial(near_kernel, blocks), out_shape=state_of...  17 us
    ppermute x10, waiting for transfers between devices, swap(): return lax.ppermute(value, ALL, [(i, i ^ bits) for i in range(count)])  14.5 us
    pallas_call x1, Pallas kernels, score(): pl.pallas_call(functools.partial(score_kernel, blocks), out_shape=[jax.Sh...  12.6 us
    ppermute x4, starting transfers between devices, along(): lax.ppermute(v, ALL, [(p * plane + i, p * plane + j) for p in range(4) fo...  12.4 us
  transfers between devices with their start and end apart: 29, of which 13 were waited for; matrix products, arithmetic and copies ran while one was open for 1% of the time, Pallas kernels for 18%

profile of v1, /device:TPU:2, one launch (start us, length us, event | category | flops | bytes accessed | tf_op | source)
XLA Modules:
  0.0 223.0 jit_solution(12971480100215805102)
XLA Ops:
  0.0 2.8 %pack.3.g = bf16[2,2,128,512]{3,2,1,0:T(8,128)(2,1)} custom-call(s32[2]{0:T(128)} %gids.15, bf16[16,128,512]{2,1,0:T(8,128)(2,1)} %bitcast.4, bf16[16,128,512]{2,1,0:T(8,128)(2,1)} %bitcast.7), custom_call_target="tpu_custom_call" | custom-call | bytes 1048576 | tf_op jit(solution)/shard_map/pack/pallas_call | solution.py:86
  5.2 3.3 %pack.4 = (bf16[6,128,512]{2,1,0:T(8,128)(2,1)}, bf16[6,128,512]{2,1,0:T(8,128)(2,1)}, bf16[2,128,512]{2,1,0:T(8,128)(2,1)}, bf16[2,128,512]{2,1,0:T(8,128)(2,1)}) custom-call(s32[2]{0:T(128)} %gids.15, bf16[16,128,512]{2,1,0:T(8,128)(2,1)} %bitcast.5, bf16[16,128,512]{2,1,0:T(8,128)(2,1)} %bitcast.8), custom_call_target="tpu_custom_call" | custom-call | bytes 4194304 | tf_op jit(solution)/shard_map/pack/pallas_call | solution.py:86
  11.1 7.0 %collective-permute-done.g_l.refs_0_ = bf16[2,2,128,512]{3,2,1,0:T(8,128)(2,1)S(1)} collective-permute-done((bf16[2,2,128,512]{3,2,1,0:T(8,128)(2,1)}, bf16[2,2,128,512]{3,2,1,0:T(8,128)(2,1)S(1)}, u32[]{:S(2)}, u32[]{:S(2)}) %collective-permute-start) | collective-permute-done | bytes 524320 | tf_op jit(solution)/shard_map/ppermute | solution.py:492
  19.5 42.2 %collective-permute-done.1.g_o.refs_5_.g = bf16[2,2,128,512]{3,2,1,0:T(8,128)(2,1)S(1)} collective-permute-done((bf16[2,2,128,512]{3,2,1,0:T(8,128)(2,1)S(1)}, bf16[2,2,128,512]{3,2,1,0:T(8,128)(2,1)S(1)}, u32[]{:S(2)}, u32[]{:S(2)}) %collective-permute-start.1) | collective-permute-done | bytes 524320 | tf_op jit(solution)/shard_map/ppermute | solution.py:492
  65.8 3.3 %pack.5 = (bf16[8,128,512]{2,1,0:T(8,128)(2,1)}, bf16[8,128,512]{2,1,0:T(8,128)(2,1)}) custom-call(s32[2]{0:T(128)} %gids.15, bf16[16,128,512]{2,1,0:T(8,128)(2,1)} %bitcast.6, bf16[16,128,512]{2,1,0:T(8,128)(2,1)} %bitcast.9), custom_call_target="tpu_custom_call" | custom-call | bytes 4194304 | tf_op jit(solution)/shard_map/pack/pallas_call | solution.py:86
  72.6 2.0 collective-permute-start.22
  76.2 2.0 collective-permute-done.22
  80.1 6.4 %collective-permute-start.23 = (bf16[2,64,512]{2,1,0:T(8,128)(2,1)S(1)}, bf16[2,64,512]{2,1,0:T(8,128)(2,1)S(1)}, u32[]{:S(2)}, u32[]{:S(2)}) collective-permute-start(bf16[2,64,512]{2,1,0:T(8,128)(2,1)S(1)} %broadcast_select_fusion), channel_id=1, source_target_pairs={{0,8},{1,9},{2,10},{3,11},{4,12},{5,13},{6,14},{7,15},{8,0},{9,1},... | collective-permute-start | bytes 393224 | tf_op jit(solution)/shard_map/ppermute | solution.py:463
  88.5 1.9 collective-permute-done.23
  92.2 3.7 %collective-permute-done.10.bk_r.refs_2_ = bf16[8,128,512]{2,1,0:T(8,128)(2,1)} collective-permute-done((bf16[8,128,512]{2,1,0:T(8,128)(2,1)}, bf16[8,128,512]{2,1,0:T(8,128)(2,1)}, u32[]{:S(2)}, u32[]{:S(2)}) %collective-permute-start.10) | collective-permute-done | bytes 1048608 | tf_op jit(solution)/shard_map/ppermute | solution.py:495
  95.9 7.2 %collective-permute-start.24 = (bf16[2,64,512]{2,1,0:T(8,128)(2,1)S(1)}, bf16[2,64,512]{2,1,0:T(8,128)(2,1)S(1)}, u32[]{:S(2)}, u32[]{:S(2)}) collective-permute-start(bf16[2,64,512]{2,1,0:T(8,128)(2,1)S(1)} %broadcast_select_fusion.1), channel_id=1, source_target_pairs={{0,16},{1,17},{2,18},{3,19},{4,20},{5,21},{6,22},{7,23},{8,24},{9,... | collective-permute-start | bytes 393224 | tf_op jit(solution)/shard_map/ppermute | solution.py:463
  103.1 3.7 %collective-permute-done.24 = bf16[2,64,512]{2,1,0:T(8,128)(2,1)S(1)} collective-permute-done((bf16[2,64,512]{2,1,0:T(8,128)(2,1)S(1)}, bf16[2,64,512]{2,1,0:T(8,128)(2,1)S(1)}, u32[]{:S(2)}, u32[]{:S(2)}) %collective-permute-start.24) | collective-permute-done | bytes 131104 | tf_op jit(solution)/shard_map/ppermute | solution.py:463
  108.4 10.0 %collective-permute-done.4.bv_r.refs_4_ = bf16[8,128,512]{2,1,0:T(8,128)(2,1)} collective-permute-done((bf16[8,128,512]{2,1,0:T(8,128)(2,1)}, bf16[8,128,512]{2,1,0:T(8,128)(2,1)}, u32[]{:S(2)}, u32[]{:S(2)}) %collective-permute-start.4) | collective-permute-done | bytes 1048608 | tf_op jit(solution)/shard_map/ppermute | solution.py:495
  118.4 3.3 %collective-permute-start.25 = (bf16[2,64,512]{2,1,0:T(8,128)(2,1)S(1)}, bf16[2,64,512]{2,1,0:T(8,128)(2,1)S(1)}, u32[]{:S(2)}, u32[]{:S(2)}) collective-permute-start(bf16[2,64,512]{2,1,0:T(8,128)(2,1)S(1)} %broadcast_select_fusion.2), channel_id=1, source_target_pairs={{0,32},{1,33},{2,34},{3,35},{4,36},{5,37},{6,38},{7,39},{8,40},{9,... | collective-permute-start | bytes 393224 | tf_op jit(solution)/shard_map/ppermute | solution.py:463
  121.7 1.9 ends.1
  125.6 9.5 %collective-permute-done.17.refs_1_ = bf16[6,128,512]{2,1,0:T(8,128)(2,1)S(1)} collective-permute-done((bf16[6,128,512]{2,1,0:T(8,128)(2,1)}, bf16[6,128,512]{2,1,0:T(8,128)(2,1)S(1)}, u32[]{:S(2)}, u32[]{:S(2)}) %collective-permute-start.17) | collective-permute-done | bytes 786464 | tf_op jit(solution)/shard_map/ppermute | solution.py:495
  137.5 13.6 %collective-permute-done.18.refs_3_ = bf16[6,128,512]{2,1,0:T(8,128)(2,1)S(1)} collective-permute-done((bf16[6,128,512]{2,1,0:T(8,128)(2,1)}, bf16[6,128,512]{2,1,0:T(8,128)(2,1)S(1)}, u32[]{:S(2)}, u32[]{:S(2)}) %collective-permute-start.18) | collective-permute-done | bytes 786464 | tf_op jit(solution)/shard_map/ppermute | solution.py:495
  152.0 8.0 %collective-permute-start.16 = (bf16[2,128,512]{2,1,0:T(8,128)(2,1)S(1)}, bf16[2,128,512]{2,1,0:T(8,128)(2,1)S(1)}, u32[]{:S(2)}, u32[]{:S(2)}) collective-permute-start(bf16[2,128,512]{2,1,0:T(8,128)(2,1)S(1)} %get-tuple-element.30), channel_id=1, source_target_pairs={{0,63},{64,127},{128,191},{192,255}} | collective-permute-start | bytes 786440 | tf_op jit(solution)/shard_map/ppermute | solution.py:500
  160.0 1.8 collective-permute-start.11
  163.6 2.7 %collective-permute-start.5 = (bf16[8,128,512]{2,1,0:T(8,128)(2,1)}, bf16[8,128,512]{2,1,0:T(8,128)(2,1)}, u32[]{:S(2)}, u32[]{:S(2)}) collective-permute-start(bf16[8,128,512]{2,1,0:T(8,128)(2,1)} %collective-permute-done.4.bv_r.refs_4_), channel_id=1, source_target_pairs={{0,192},{4,196},{8,200},{12,204},{16,208},{20,212},{24,216},{28,22... | collective-permute-start | bytes 3145736 | tf_op jit(solution)/shard_map/ppermute | solution.py:495
  169.3 4.1 %collective-permute-done.27.refs_7_ = bf16[2,64,512]{2,1,0:T(8,128)(2,1)S(1)} collective-permute-done((bf16[2,64,512]{2,1,0:T(8,128)(2,1)S(1)}, bf16[2,64,512]{2,1,0:T(8,128)(2,1)S(1)}, u32[]{:S(2)}, u32[]{:S(2)}) %collective-permute-start.27) | collective-permute-done | bytes 131104 | tf_op jit(solution)/shard_map/ppermute | solution.py:463
  187.7 17.0 %near.1 = (f32[16,4,128,128]{3,2,1,0:T(8,128)S(1)}, f32[16,4,128,128]{3,2,1,0:T(8,128)S(1)}, f32[16,4,128,128]{3,2,1,0:T(8,128)S(1)}) custom-call(s32[2]{0:T(128)S(1)} %copy-done.26, s32[16,3]{1,0:T(8,128)S(1)} %copy.10.picks, s32[4]{0:T(128)S(1)} %copy-done.28, bf16[2048,512]{1,0:T(8,128)(2,1)S(1)} %copy-done.2, bf16[2048,512]{1,0:T(8,128)(2,1)S(1)} %copy-done, ...), custom_call_target="tpu_custom_call" | custom-call | flops 3221225472 | bytes 25165824 | tf_op jit(solution)/shard_map/near/pallas_call | solution.py:242
  204.8 12.6 %score.1 = (bf16[16,4,128,128]{3,2,1,0:T(8,128)(2,1)S(1)}, f32[16,4,128,128]{3,2,1,0:T(8,128)S(1)}, f32[16,4,128,128]{3,2,1,0:T(8,128)S(1)}) custom-call(s32[2]{0:T(128)S(1)} %copy-done.26, s32[16,3]{1,0:T(8,128)S(1)} %copy.10.picks, bf16[2048,512]{1,0:T(8,128)(2,1)S(1)} %copy-done.3, ...), custom_call_target="tpu_custom_call", output_to_operand_aliasing={{1}: (12, {}), {2}: (13, {})} | custom-call | flops 805306368 | bytes 31457280 | tf_op jit(solution)/shard_map/score/pallas_call | solution.py:310
  217.5 5.4 %last.1 = bf16[2048,512]{1,0:T(8,128)(2,1)} custom-call(s32[2]{0:T(128)S(1)} %copy-done.26, s32[16,3]{1,0:T(8,128)S(1)} %copy.10.picks, bf16[2,2,128,512]{3,2,1,0:T(8,128)(2,1)S(1)} %copy-done.5, bf16[6,128,512]{2,1,0:T(8,128)(2,1)} %collective-permute-done.3.a_v, bf16[8,128,512]{2,1,0:T(8,128)(2,1)} %collective-permute-done.5.b_v, ...), custom_call_target="tpu_custom_call" | custom-call | flops 268435456 | bytes 10485760 | tf_op jit(solution)/shard_map/last/pallas_call | solution.py:361
  (112 shorter events, 47.2 us)
Async XLA Ops:
  2.8 15.3 %collective-permute-start = (bf16[2,2,128,512]{3,2,1,0:T(8,128)(2,1)}, bf16[2,2,128,512]{3,2,1,0:T(8,128)(2,1)S(1)}, u32[]{:S(2)}, u32[]{:S(2)}) collective-permute-start(bf16[2,2,128,512]{3,2,1,0:T(8,128)(2,1)} %pack.3.g), channel_id=1, source_target_pairs={{0,64},{4,68},{8,72},{12,76},{16,80},{20,84},{24,88},{28,92},{32,9... | collective-permute-start | bytes 1572872 | tf_op jit(solution)/shard_map/ppermute | solution.py:492
  4.3 15.1 %collective-permute-start.14 = (bf16[2,2,128,512]{3,2,1,0:T(8,128)(2,1)}, bf16[2,2,128,512]{3,2,1,0:T(8,128)(2,1)S(1)}, u32[]{:S(2)}, u32[]{:S(2)}) collective-permute-start(bf16[2,2,128,512]{3,2,1,0:T(8,128)(2,1)} %pack.3.g), channel_id=1, source_target_pairs={{0,192},{4,196},{8,200},{12,204},{16,208},{20,212},{24,216},{28,22... | collective-permute-start | bytes 1572872 | tf_op jit(solution)/shard_map/ppermute | solution.py:495
  8.5 78.0 %collective-permute-start.2 = (bf16[6,128,512]{2,1,0:T(8,128)(2,1)}, bf16[6,128,512]{2,1,0:T(8,128)(2,1)}, u32[]{:S(2)}, u32[]{:S(2)}) collective-permute-start(bf16[6,128,512]{2,1,0:T(8,128)(2,1)} %get-tuple-element.23), channel_id=1, source_target_pairs={{0,64},{4,68},{8,72},{12,76},{16,80},{20,84},{24,88},{28,92},{32,9... | collective-permute-start | bytes 2359304 | tf_op jit(solution)/shard_map/ppermute | solution.py:492
  9.8 78.2 %collective-permute-start.6 = (bf16[6,128,512]{2,1,0:T(8,128)(2,1)}, bf16[6,128,512]{2,1,0:T(8,128)(2,1)}, u32[]{:S(2)}, u32[]{:S(2)}) collective-permute-start(bf16[6,128,512]{2,1,0:T(8,128)(2,1)} %get-tuple-element.25), channel_id=1, source_target_pairs={{0,64},{4,68},{8,72},{12,76},{16,80},{20,84},{24,88},{28,92},{32,9... | collective-permute-start | bytes 2359304 | tf_op jit(solution)/shard_map/ppermute | solution.py:492
  18.1 43.6 %collective-permute-start.1 = (bf16[2,2,128,512]{3,2,1,0:T(8,128)(2,1)S(1)}, bf16[2,2,128,512]{3,2,1,0:T(8,128)(2,1)S(1)}, u32[]{:S(2)}, u32[]{:S(2)}) collective-permute-start(bf16[2,2,128,512]{3,2,1,0:T(8,128)(2,1)S(1)} %collective-permute-done.g_l.refs_0_), channel_id=1, source_target_pairs={{0,64},{4,68},{8,72},{12,76},{16,80},{20,84},{24,88},{28,92},{32,9... | collective-permute-start | bytes 1572872 | tf_op jit(solution)/shard_map/ppermute | solution.py:492
  64.0 8.4 %collective-permute-start.20 = (bf16[2,64,512]{2,1,0:T(8,128)(2,1)S(1)}, bf16[2,64,512]{2,1,0:T(8,128)(2,1)S(1)}, u32[]{:S(2)}, u32[]{:S(2)}) collective-permute-start(bf16[2,64,512]{2,1,0:T(8,128)(2,1)S(1)} %get-tuple-element.32), channel_id=1, source_target_pairs={{0,2},{1,3},{2,0},{3,1},{4,6},{5,7},{6,4},{7,5},{8,10},{9,11},{10,... | collective-permute-start | bytes 393224 | tf_op jit(solution)/shard_map/ppermute | solution.py:463
  65.5 7.0 %collective-permute-start.21 = (bf16[2,64,512]{2,1,0:T(8,128)(2,1)S(1)}, bf16[2,64,512]{2,1,0:T(8,128)(2,1)S(1)}, u32[]{:S(2)}, u32[]{:S(2)}) collective-permute-start(bf16[2,64,512]{2,1,0:T(8,128)(2,1)S(1)} %get-tuple-element.33), channel_id=1, source_target_pairs={{0,1},{1,0},{2,3},{3,2},{4,5},{5,4},{6,7},{7,6},{8,9},{9,8},{10,11... | collective-permute-start | bytes 393224 | tf_op jit(solution)/shard_map/ppermute | solution.py:463
  69.6 26.3 %collective-permute-start.10 = (bf16[8,128,512]{2,1,0:T(8,128)(2,1)}, bf16[8,128,512]{2,1,0:T(8,128)(2,1)}, u32[]{:S(2)}, u32[]{:S(2)}) collective-permute-start(bf16[8,128,512]{2,1,0:T(8,128)(2,1)} %get-tuple-element.26), channel_id=1, source_target_pairs={{0,192},{4,196},{8,200},{12,204},{16,208},{20,212},{24,216},{28,22... | collective-permute-start | bytes 3145736 | tf_op jit(solution)/shard_map/ppermute | solution.py:495
  78.2 40.1 %collective-permute-start.4 = (bf16[8,128,512]{2,1,0:T(8,128)(2,1)}, bf16[8,128,512]{2,1,0:T(8,128)(2,1)}, u32[]{:S(2)}, u32[]{:S(2)}) collective-permute-start(bf16[8,128,512]{2,1,0:T(8,128)(2,1)} %get-tuple-element.24), channel_id=1, source_target_pairs={{0,192},{4,196},{8,200},{12,204},{16,208},{20,212},{24,216},{28,22... | collective-permute-start | bytes 3145736 | tf_op jit(solution)/shard_map/ppermute | solution.py:495
  80.1 10.3 %collective-permute-start.23 = (bf16[2,64,512]{2,1,0:T(8,128)(2,1)S(1)}, bf16[2,64,512]{2,1,0:T(8,128)(2,1)S(1)}, u32[]{:S(2)}, u32[]{:S(2)}) collective-permute-start(bf16[2,64,512]{2,1,0:T(8,128)(2,1)S(1)} %broadcast_select_fusion), channel_id=1, source_target_pairs={{0,8},{1,9},{2,10},{3,11},{4,12},{5,13},{6,14},{7,15},{8,0},{9,1},... | collective-permute-start | bytes 393224 | tf_op jit(solution)/shard_map/ppermute | solution.py:463
  86.5 75.5 %collective-permute-start.7 = (bf16[8,128,512]{2,1,0:T(8,128)(2,1)}, bf16[8,128,512]{2,1,0:T(8,128)(2,1)S(1)}, u32[]{:S(2)}, u32[]{:S(2)}) collective-permute-start(bf16[8,128,512]{2,1,0:T(8,128)(2,1)} %get-tuple-element.26), channel_id=1, source_target_pairs={{0,64},{4,68},{8,72},{12,76},{16,80},{20,84},{24,88},{28,92},{32,9... | collective-permute-start | bytes 3145736 | tf_op jit(solution)/shard_map/ppermute | solution.py:492
  87.9 47.2 %collective-permute-start.17 = (bf16[6,128,512]{2,1,0:T(8,128)(2,1)}, bf16[6,128,512]{2,1,0:T(8,128)(2,1)S(1)}, u32[]{:S(2)}, u32[]{:S(2)}) collective-permute-start(bf16[6,128,512]{2,1,0:T(8,128)(2,1)} %get-tuple-element.25), channel_id=1, source_target_pairs={{0,192},{4,196},{8,200},{12,204},{16,208},{20,212},{24,216},{28,22... | collective-permute-start | bytes 2359304 | tf_op jit(solution)/shard_map/ppermute | solution.py:495
  90.3 60.8 %collective-permute-start.18 = (bf16[6,128,512]{2,1,0:T(8,128)(2,1)}, bf16[6,128,512]{2,1,0:T(8,128)(2,1)S(1)}, u32[]{:S(2)}, u32[]{:S(2)}) collective-permute-start(bf16[6,128,512]{2,1,0:T(8,128)(2,1)} %get-tuple-element.23), channel_id=1, source_target_pairs={{0,192},{4,196},{8,200},{12,204},{16,208},{20,212},{24,216},{28,22... | collective-permute-start | bytes 2359304 | tf_op jit(solution)/shard_map/ppermute | solution.py:495
  95.9 10.9 %collective-permute-start.24 = (bf16[2,64,512]{2,1,0:T(8,128)(2,1)S(1)}, bf16[2,64,512]{2,1,0:T(8,128)(2,1)S(1)}, u32[]{:S(2)}, u32[]{:S(2)}) collective-permute-start(bf16[2,64,512]{2,1,0:T(8,128)(2,1)S(1)} %broadcast_select_fusion.1), channel_id=1, source_target_pairs={{0,16},{1,17},{2,18},{3,19},{4,20},{5,21},{6,22},{7,23},{8,24},{9,... | collective-permute-start | bytes 393224 | tf_op jit(solution)/shard_map/ppermute | solution.py:463
  106.8 16.8 %collective-permute-start.13 = (bf16[2,128,512]{2,1,0:T(8,128)(2,1)}, bf16[2,128,512]{2,1,0:T(8,128)(2,1)S(1)}, u32[]{:S(2)}, u32[]{:S(2)}) collective-permute-start(bf16[2,128,512]{2,1,0:T(8,128)(2,1)} %get-tuple-element.28), channel_id=1, source_target_pairs={{1,0},{2,1},{3,2},{4,3},{5,4},{6,5},{7,6},{8,7},{9,8},{10,9},{11,1... | collective-permute-start | bytes 786440 | tf_op jit(solution)/shard_map/ppermute | solution.py:500
  118.4 41.7 %collective-permute-start.25 = (bf16[2,64,512]{2,1,0:T(8,128)(2,1)S(1)}, bf16[2,64,512]{2,1,0:T(8,128)(2,1)S(1)}, u32[]{:S(2)}, u32[]{:S(2)}) collective-permute-start(bf16[2,64,512]{2,1,0:T(8,128)(2,1)S(1)} %broadcast_select_fusion.2), channel_id=1, source_target_pairs={{0,32},{1,33},{2,34},{3,35},{4,36},{5,37},{6,38},{7,39},{8,40},{9,... | collective-permute-start | bytes 393224 | tf_op jit(solution)/shard_map/ppermute | solution.py:463
  124.3 38.6 %collective-permute-start.15 = (bf16[2,128,512]{2,1,0:T(8,128)(2,1)S(1)}, bf16[2,128,512]{2,1,0:T(8,128)(2,1)S(1)}, u32[]{:S(2)}, u32[]{:S(2)}) collective-permute-start(bf16[2,128,512]{2,1,0:T(8,128)(2,1)S(1)} %get-tuple-element.29), channel_id=1, source_target_pairs={{63,0},{127,64},{191,128},{255,192}} | collective-permute-start | bytes 786440 | tf_op jit(solution)/shard_map/ppermute | solution.py:500
  136.0 68.7 %collective-permute-start.8 = (bf16[8,128,512]{2,1,0:T(8,128)(2,1)}, bf16[8,128,512]{2,1,0:T(8,128)(2,1)}, u32[]{:S(2)}, u32[]{:S(2)}) collective-permute-start(bf16[8,128,512]{2,1,0:T(8,128)(2,1)} %get-tuple-element.24), channel_id=1, source_target_pairs={{0,64},{4,68},{8,72},{12,76},{16,80},{20,84},{24,88},{28,92},{32,9... | collective-permute-start | bytes 3145736 | tf_op jit(solution)/shard_map/ppermute | solution.py:492
  152.0 14.3 %collective-permute-start.16 = (bf16[2,128,512]{2,1,0:T(8,128)(2,1)S(1)}, bf16[2,128,512]{2,1,0:T(8,128)(2,1)S(1)}, u32[]{:S(2)}, u32[]{:S(2)}) collective-permute-start(bf16[2,128,512]{2,1,0:T(8,128)(2,1)S(1)} %get-tuple-element.30), channel_id=1, source_target_pairs={{0,63},{64,127},{128,191},{192,255}} | collective-permute-start | bytes 786440 | tf_op jit(solution)/shard_map/ppermute | solution.py:500
  160.0 44.7 %collective-permute-start.11 = (bf16[8,128,512]{2,1,0:T(8,128)(2,1)}, bf16[8,128,512]{2,1,0:T(8,128)(2,1)}, u32[]{:S(2)}, u32[]{:S(2)}) collective-permute-start(bf16[8,128,512]{2,1,0:T(8,128)(2,1)} %collective-permute-done.10.bk_r.refs_2_), channel_id=1, source_target_pairs={{0,192},{4,196},{8,200},{12,204},{16,208},{20,212},{24,216},{28,22... | collective-permute-start | bytes 3145736 | tf_op jit(solution)/shard_map/ppermute | solution.py:495
  163.6 53.8 %collective-permute-start.5 = (bf16[8,128,512]{2,1,0:T(8,128)(2,1)}, bf16[8,128,512]{2,1,0:T(8,128)(2,1)}, u32[]{:S(2)}, u32[]{:S(2)}) collective-permute-start(bf16[8,128,512]{2,1,0:T(8,128)(2,1)} %collective-permute-done.4.bv_r.refs_4_), channel_id=1, source_target_pairs={{0,192},{4,196},{8,200},{12,204},{16,208},{20,212},{24,216},{28,22... | collective-permute-start | bytes 3145736 | tf_op jit(solution)/shard_map/ppermute | solution.py:495
  167.7 7.0 %collective-permute-start.28 = (bf16[2,64,512]{2,1,0:T(8,128)(2,1)S(1)}, bf16[2,64,512]{2,1,0:T(8,128)(2,1)S(1)}, u32[]{:S(2)}, u32[]{:S(2)}) collective-permute-start(bf16[2,64,512]{2,1,0:T(8,128)(2,1)S(1)} %broadcast_select_fusion.3.refs_5_), channel_id=1, source_target_pairs={{0,3},{1,2},{2,1},{3,0},{4,7},{5,6},{6,5},{7,4},{8,11},{9,10},{10,... | collective-permute-start | bytes 393224 | tf_op jit(solution)/shard_map/ppermute | solution.py:463
  174.0 30.7 %collective-permute-start.9 = (bf16[6,128,512]{2,1,0:T(8,128)(2,1)}, bf16[6,128,512]{2,1,0:T(8,128)(2,1)}, u32[]{:S(2)}, u32[]{:S(2)}) collective-permute-start(bf16[6,128,512]{2,1,0:T(8,128)(2,1)} %collective-permute-done.6.ak_l.refs_1_), channel_id=1, source_target_pairs={{0,64},{4,68},{8,72},{12,76},{16,80},{20,84},{24,88},{28,92},{32,9... | collective-permute-start | bytes 2359304 | tf_op jit(solution)/shard_map/ppermute | solution.py:492
  175.4 42.1 %collective-permute-start.3 = (bf16[6,128,512]{2,1,0:T(8,128)(2,1)}, bf16[6,128,512]{2,1,0:T(8,128)(2,1)}, u32[]{:S(2)}, u32[]{:S(2)}) collective-permute-start(bf16[6,128,512]{2,1,0:T(8,128)(2,1)} %collective-permute-done.2.av_l.refs_3_), channel_id=1, source_target_pairs={{0,64},{4,68},{8,72},{12,76},{16,80},{20,84},{24,88},{28,92},{32,9... | collective-permute-start | bytes 2359304 | tf_op jit(solution)/shard_map/ppermute | solution.py:492
  (35 other events, 613.7 us)

commit v2 on v1

--- a/solution.py
+++ b/solution.py
@@ -13,7 +13,6 @@
 DH = 128
 BS = 128
 QB = 16
-GROUP = 4
 W = H * DH
 SCALE_LOG2 = math.log2(math.e) / math.sqrt(DH)
 G_N, A_N, B_N = 2, 6, 8
@@ -155,13 +154,103 @@
 
 
 def near_kernel(blocks, gids, picks, place, q_ref, keys, values, low, high, first, last, *refs):
-    side, refs = refs[:5], refs[5:]
-    pieces, refs = refs[:4], refs[4:]
-    top_ref, total_ref, acc_ref, kbuf, vbuf, shared, buf, sem, shared_sem, pick_sem = refs
+    sides, refs = (refs[:5], refs[5:10]), refs[10:]
+    top_ref, total_ref, acc_ref, kbuf, vbuf, buf, sem, pick_sem = refs
     places = first_two(gids, blocks)
     copies = []
     for half, (ref, dst) in enumerate(((keys, kbuf), (values, vbuf))):
         copies.append(pltpu.make_async_copy(ref, dst.at[pl.ds(BS, blocks * BS)], sem.at[half, 0]))
+    for copy in copies:
+        copy.start()
+    halos = (
+        (1, place[3] == 0, first, low, 0),
+        (2, place[3] == 1, last, high, (blocks + 1) * BS),
+    )
+    for n, wraps, there, here, at in halos:
+        for half, dst in enumerate((kbuf, vbuf)):
+
+            @pl.when(wraps)
+            def _(there=there, half=half, dst=dst, at=at, n=n):
+                pltpu.make_async_copy(there.at[half], dst.at[pl.ds(at, BS)], sem.at[half, n]).start()
+
+            @pl.when(jnp.logical_not(wraps))
+            def _(here=here, half=half, dst=dst, at=at, n=n):
+                pltpu.make_async_copy(here.at[half], dst.at[pl.ds(at, BS)], sem.at[half, n]).start()
+
+    def fetch(j, carry):
+        for side, column in ((0, 0), (1, 2)):
+            g, a_k, b_k, a_v, b_v = sides[side]
+            position = position_of(picks[j, column], places, blocks)
+            fetch_pick(position, (g.at[0], a_k, b_k), buf.at[j, 0, side], pick_sem.at[j, 0, side])
+            fetch_pick(position, (g.at[1], a_v, b_v), buf.at[j, 1, side], pick_sem.at[j, 1, side])
+        return carry
+
+    lax.fori_loop(0, blocks, fetch, 0)
+    for copy in copies:
+        copy.wait()
+    for n, _, _, here, at in halos:
+        for half, dst in enumerate((kbuf, vbuf)):
+            pltpu.make_async_copy(here.at[half], dst.at[pl.ds(at, BS)], sem.at[half, n]).wait()
+
+    def step(j, carry):
+        rows = pl.ds(pl.multiple_of(j * BS, BS), BS)
+        span = pl.ds(pl.multiple_of(j * BS, BS), 3 * BS)
+        for half in range(2):
+            for side in range(2):
+                pltpu.make_async_copy(
+                    sides[side][2].at[0], buf.at[j, half, side], pick_sem.at[j, half, side]
+                ).wait()
+        keys_of, values_of = [
+            [
+                jnp.concatenate(
+                    [own[span, head(h)], buf[j, half, 0, :, head(h)], buf[j, half, 1, :, head(h)]],
+                    axis=0,
+                )
+                for h in range(H)
+            ]
+            for half, own in enumerate((kbuf, vbuf))
+        ]
+        scores = [dot_t(q_ref[rows, head(h)], keys_of[h]) for h in range(H)]
+        tops = [top_of([s]) for s in scores]
+        weights = [weigh(s, top) for s, top in zip(scores, tops)]
+        mixed = [mix(w, v) for w, v in zip(weights, values_of)]
+        for h in range(H):
+            top_ref[j, h] = tops[h]
+            total_ref[j, h] = mixed[h][:, DH:]
+            acc_ref[j, h] = mixed[h][:, :DH]
+        return carry
+
+    lax.fori_loop(0, blocks, step, 0)
+
+
+def near(gids, picks, place, queries, keys, values, halos, from_right, from_left):
+    rows = queries.shape[0]
+    blocks = rows // BS
+    return pl.pallas_call(
+        functools.partial(near_kernel, blocks),
+        out_shape=state_of(blocks),
+        in_specs=[SM, SM, SM, VM] + [ANY] * 16,
+        out_specs=[VM] * 3,
+        scratch_shapes=[
+            pltpu.VMEM(((blocks + 2) * BS, W), keys.dtype),
+            pltpu.VMEM(((blocks + 2) * BS, W), keys.dtype),
+            pltpu.VMEM((blocks, 2, 2, BS, W), keys.dtype),
+            pltpu.SemaphoreType.DMA((2, 3)),
+            pltpu.SemaphoreType.DMA((blocks, 2, 2)),
+        ],
+        compiler_params=pltpu.CompilerParams(vmem_limit_bytes=NEAR_VMEM),
+        cost_estimate=pl.CostEstimate(
+            flops=rows * 5 * BS * W * 4, transcendentals=rows * 5 * BS * H, bytes_accessed=26 << 20
+        ),
+        name="near",
+    )(gids, picks, place, queries, keys, values, *halos, *from_right, *from_left)
+
+
+def score_kernel(blocks, gids, picks, place, q_ref, *refs):
+    pieces, (g_o, ak_o, bk_o), refs = refs[:4], refs[4:7], refs[7:]
+    top_in, total_in, acc_in, weight_ref, share_ref, acc_ref, shared, buf, shared_sem, sem = refs
+    places = first_two(gids, blocks)
+    copies = []
     for n, piece in enumerate(pieces):
         quarter = jnp.bitwise_and(jnp.bitwise_xor(place[0], n), 3)
         rows = piece.shape[1]
@@ -171,158 +260,67 @@
     for copy in copies:
         copy.start()
 
-    halos = (
-        (1, place[3] == 0, first, low, 0),
-        (2, place[3] == 1, last, high, (blocks + 1) * BS),
-    )
-    for n, wraps, there, here, at in halos:
-        for half, dst in enumerate((kbuf, vbuf)):
-
-            @pl.when(wraps)
-            def _(there=there, half=half, dst=dst, at=at, n=n):
-                pltpu.make_async_copy(there.at[half], dst.at[pl.ds(at, BS)], sem.at[half, n]).start()
-
-            @pl.when(jnp.logical_not(wraps))
-            def _(here=here, half=half, dst=dst, at=at, n=n):
-                pltpu.make_async_copy(here.at[half], dst.at[pl.ds(at, BS)], sem.at[half, n]).start()
-
-    g, a_k, b_k, a_v, b_v = side
-
     def fetch(j, carry):
-        position = position_of(picks[j, 0], places, blocks)
-        fetch_pick(position, (g.at[0], a_k, b_k), buf.at[j, 0], pick_sem.at[j, 0])
-        fetch_pick(position, (g.at[1], a_v, b_v), buf.at[j, 1], pick_sem.at[j, 1])
+        position = position_of(picks[j, 1], places, blocks)
+        fetch_pick(position, (g_o.at[0], ak_o, bk_o), buf.at[j], sem.at[j])
         return carry
 
     lax.fori_loop(0, blocks, fetch, 0)
     for copy in copies:
         copy.wait()
-    for n, _, _, here, at in halos:
-        for half, dst in enumerate((kbuf, vbuf)):
-            pltpu.make_async_copy(here.at[half], dst.at[pl.ds(at, BS)], sem.at[half, n]).wait()
 
     def step(j, carry):
         rows = pl.ds(pl.multiple_of(j * BS, BS), BS)
-        span = pl.ds(pl.multiple_of(j * BS, BS), 3 * BS)
-        for half in range(2):
-            pltpu.make_async_copy(b_k.at[0], buf.at[j, half], pick_sem.at[j, half]).wait()
-        for first in range(0, H, GROUP):
-            heads = range(first, first + GROUP)
-            keys_of, values_of = [
-                [
-                    jnp.concatenate(
-                        [
-                            own[span, head(h)],
-                            buf[j, half, :, head(h)],
-                            shared[0, half * BS : (half + 1) * BS, head(h)],
-                            shared[1, half * BS : (half + 1) * BS, head(h)],
-                        ],
-                        axis=0,
-                    )
-                    for h in heads
-                ]
-                for half, own in enumerate((kbuf, vbuf))
-            ]
-            scores = [dot_t(q_ref[rows, head(h)], k) for h, k in zip(heads, keys_of)]
-            tops = [top_of([s]) for s in scores]
-            weights = [weigh(s, top) for s, top in zip(scores, tops)]
-            mixed = [mix(w, v) for w, v in zip(weights, values_of)]
-            for n, h in enumerate(heads):
-                top_ref[j, h] = tops[n]
-                total_ref[j, h] = mixed[n][:, DH:]
-                acc_ref[j, h] = mixed[n][:, :DH]
-        return carry
-
-    lax.fori_loop(0, blocks, step, 0)
-
-
-def near(gids, picks, place, queries, keys, values, halos, from_right, pieces):
-    rows = queries.shape[0]
-    blocks = rows // BS
-    return pl.pallas_call(
-        functools.partial(near_kernel, blocks),
-        out_shape=state_of(blocks),
-        in_specs=[SM, SM, SM, VM] + [ANY] * 15,
-        out_specs=[VM] * 3,
-        scratch_shapes=[
-            pltpu.VMEM(((blocks + 2) * BS, W), keys.dtype),
-            pltpu.VMEM(((blocks + 2) * BS, W), keys.dtype),
-            pltpu.VMEM((2, 2 * BS, W), keys.dtype),
-            pltpu.VMEM((blocks, 2, BS, W), keys.dtype),
-            pltpu.SemaphoreType.DMA((2, 3)),
-            pltpu.SemaphoreType.DMA((4,)),
-            pltpu.SemaphoreType.DMA((blocks, 2)),
-        ],
-        compiler_params=pltpu.CompilerParams(vmem_limit_bytes=NEAR_VMEM),
-        cost_estimate=pl.CostEstimate(
-            flops=rows * 6 * BS * W * 4, transcendentals=rows * 6 * BS * H, bytes_accessed=24 << 20
-        ),
-        name="near",
-    )(gids, picks, place, queries, keys, values, *halos, *from_right, *pieces)
-
-
-def score_kernel(blocks, gids, picks, q_ref, *refs):
-    left, (g_o, ak_o, bk_o), refs = refs[:5], refs[5:8], refs[8:]
-    top_in, total_in, acc_in, weight_ref, share_ref, acc_ref, buf, sem = refs
-    g_l, ak_l, bk_l, av_l, bv_l = left
-    places = first_two(gids, blocks)
-
-    def fetch(j, carry):
-        near_at = position_of(picks[j, 2], places, blocks)
-        far_at = position_of(picks[j, 1], places, blocks)
-        fetch_pick(near_at, (g_l.at[0], ak_l, bk_l), buf.at[j, 0], sem.at[j, 0])
-        fetch_pick(far_at, (g_o.at[0], ak_o, bk_o), buf.at[j, 1], sem.at[j, 1])
-        fetch_pick(near_at, (g_l.at[1], av_l, bv_l), buf.at[j, 2], sem.at[j, 2])
-        return carry
-
-    lax.fori_loop(0, blocks, fetch, 0)
-
-    def step(j, carry):
-        rows = pl.ds(pl.multiple_of(j * BS, BS), BS)
-        for n in range(3):
-            pltpu.make_async_copy(bk_o.at[0], buf.at[j, n], sem.at[j, n]).wait()
+        pltpu.make_async_copy(bk_o.at[0], buf.at[j], sem.at[j]).wait()
         q = [q_ref[rows, head(h)] for h in range(H)]
-        k = [jnp.concatenate([buf[j, 0, :, head(h)], buf[j, 1, :, head(h)]], axis=0) for h in range(H)]
-        v = [buf[j, 2, :, head(h)] for h in range(H)]
+        k = [
+            jnp.concatenate(
+                [shared[0, :BS, head(h)], shared[1, :BS, head(h)], buf[j, :, head(h)]], axis=0
+            )
+            for h in range(H)
+        ]
+        v = [jnp.concatenate([shared[n, BS:, head(h)] for n in range(2)], axis=0) for h in range(H)]
         old_top = [top_in[j, h] for h in range(H)]
         old_total = [total_in[j, h] for h in range(H)]
         old_acc = [acc_in[j, h] for h in range(H)]
         scores = [dot_t(q[h], k[h]) for h in range(H)]
         tops = [top_of([scores[h]], old_top[h]) for h in range(H)]
         weights = [weigh(scores[h], tops[h]) for h in range(H)]
-        mixed = [dot(weights[h][:, :BS], v[h]) for h in range(H)]
-        sums = [dot(weights[h], ones(2 * BS)) for h in range(H)]
+        mixed = [mix(weights[h][:, : 2 * BS], v[h]) for h in range(H)]
+        sums = [mixed[h][:, DH:] + dot(weights[h][:, 2 * BS :], ones(BS)) for h in range(H)]
         fades = [jnp.exp2((old_top[h] - tops[h]) * SCALE_LOG2) for h in range(H)]
         shares = [1.0 / (sums[h] + fades[h] * old_total[h]) for h in range(H)]
         for h in range(H):
-            weight_ref[j, h] = weights[h][:, BS:]
+            weight_ref[j, h] = weights[h][:, 2 * BS :]
             share_ref[j, h] = shares[h]
-            acc_ref[j, h] = mixed[h] + old_acc[h] * fades[h]
+            acc_ref[j, h] = mixed[h][:, :DH] + old_acc[h] * fades[h]
         return carry
 
     lax.fori_loop(0, blocks, step, 0)
 
 
-def score(gids, picks, queries, from_left, opposite, state):
+def score(gids, picks, place, queries, pieces, opposite, state):
     rows = queries.shape[0]
     blocks = rows // BS
     floats = jax.ShapeDtypeStruct((blocks, H, BS, DH), jnp.float32)
     return pl.pallas_call(
         functools.partial(score_kernel, blocks),
         out_shape=[jax.ShapeDtypeStruct((blocks, H, BS, BS), queries.dtype), floats, floats],
-        in_specs=[SM, SM, VM] + [ANY] * 8 + [VM] * 3,
+        in_specs=[SM, SM, SM, VM] + [ANY] * 7 + [VM] * 3,
         out_specs=[VM] * 3,
         input_output_aliases={12: 1, 13: 2},
         scratch_shapes=[
-            pltpu.VMEM((blocks, 3, BS, W), queries.dtype),
-            pltpu.SemaphoreType.DMA((blocks, 3)),
+            pltpu.VMEM((2, 2 * BS, W), queries.dtype),
+            pltpu.VMEM((blocks, BS, W), queries.dtype),
+            pltpu.SemaphoreType.DMA((4,)),
+            pltpu.SemaphoreType.DMA((blocks,)),
         ],
         compiler_params=pltpu.CompilerParams(vmem_limit_bytes=SCORE_VMEM),
         cost_estimate=pl.CostEstimate(
-            flops=rows * BS * W * 6, transcendentals=rows * 2 * BS * H, bytes_accessed=30 << 20
+            flops=rows * BS * W * 10, transcendentals=rows * 3 * BS * H, bytes_accessed=28 << 20
         ),
         name="score",
-    )(gids, picks, queries, *from_left, *opposite, *state)
+    )(gids, picks, place, queries, *pieces, *opposite, *state)
 
 
 def last_kernel(blocks, gids, picks, g, a_v, b_v, weights, share, acc, out, buf, obuf, sem, out_sem):
@@ -538,15 +536,10 @@
         values,
         (low, high, first, final),
         (g_r, ak_r, bk_r, av_r, bv_r),
-        pieces,
+        (g_l, ak_l, bk_l, av_l, bv_l),
     )
     weights, share, acc = score(
-        global_ids,
-        rand_pick,
-        queries,
-        (g_l, ak_l, bk_l, av_l, bv_l),
-        (g_o, ak_o, bk_o),
-        state,
+        global_ids, rand_pick, place, queries, pieces, (g_o, ak_o, bk_o), state
     )
     return last(global_ids, rand_pick, (g_o, av_o, bv_o), weights, share, acc, queries)
 

time: 226 us -> 195 us (0.86)
  the two profiles are of different devices: /device:TPU:2 before, /device:TPU:1 now
where the time goes in v2:
time: 195 us; the launch traced here: 194 us
  waiting for transfers between devices  67.7 us (35%)
  starting transfers between devices  61.2 us (31%)
  Pallas kernels  50.1 us (26%)
  local copies, waits for them, and re-layouts  13.9 us (7%)
    ppermute x8, waiting for transfers between devices, to_right(): return lax.ppermute(v, 'blk', right)  55 us
    ppermute x10, starting transfers between devices, swap(): return lax.ppermute(value, ALL, [(i, i ^ bits) for i in range(count)])  36 us
    pallas_call x1, Pallas kernels, near(): pl.pallas_call(functools.partial(near_kernel, blocks), out_shape=state_of...  20.4 us
    unnamed x49, local copies, waits for them, and re-layouts  13.9 us
    ppermute x7, starting transfers between devices, to_left(): return lax.ppermute(v, 'blk', left)  13.2 us
    ppermute x10, waiting for transfers between devices, swap(): return lax.ppermute(value, ALL, [(i, i ^ bits) for i in range(count)])  12.6 us
    pallas_call x1, Pallas kernels, score(): pl.pallas_call(functools.partial(score_kernel, blocks), out_shape=[jax.Sh...  11.6 us
    pallas_call x3, Pallas kernels, pack(): pl.pallas_call(functools.partial(pack_kernel, start, count, joined, ends)...  9.35 us
  transfers between devices with their start and end apart: 29, of which 10 were waited for; matrix products, arithmetic and copies ran while one was open for 1% of the time, Pallas kernels for 22%

profile of v2, /device:TPU:1, one launch (start us, length us, event | category | flops | bytes accessed | tf_op | source)
XLA Modules:
  0.0 194.1 jit_solution(16491138572948195675)
XLA Ops:
  0.0 2.8 %pack.3.g = bf16[2,2,128,512]{3,2,1,0:T(8,128)(2,1)} custom-call(s32[2]{0:T(128)} %gids.15, bf16[16,128,512]{2,1,0:T(8,128)(2,1)} %bitcast.4, bf16[16,128,512]{2,1,0:T(8,128)(2,1)} %bitcast.7), custom_call_target="tpu_custom_call" | custom-call | bytes 1048576 | tf_op jit(solution)/shard_map/pack/pallas_call | solution.py:85
  6.2 3.3 %pack.4 = (bf16[6,128,512]{2,1,0:T(8,128)(2,1)}, bf16[6,128,512]{2,1,0:T(8,128)(2,1)}, bf16[2,128,512]{2,1,0:T(8,128)(2,1)}, bf16[2,128,512]{2,1,0:T(8,128)(2,1)}) custom-call(s32[2]{0:T(128)} %gids.15, bf16[16,128,512]{2,1,0:T(8,128)(2,1)} %bitcast.5, bf16[16,128,512]{2,1,0:T(8,128)(2,1)} %bitcast.8), custom_call_target="tpu_custom_call" | custom-call | bytes 4194304 | tf_op jit(solution)/shard_map/pack/pallas_call | solution.py:85
  11.0 4.8 %collective-permute-done.g_l.refs_5_ = bf16[2,2,128,512]{3,2,1,0:T(8,128)(2,1)S(1)} collective-permute-done((bf16[2,2,128,512]{3,2,1,0:T(8,128)(2,1)}, bf16[2,2,128,512]{3,2,1,0:T(8,128)(2,1)S(1)}, u32[]{:S(2)}, u32[]{:S(2)}) %collective-permute-start) | collective-permute-done | bytes 524320 | tf_op jit(solution)/shard_map/ppermute | solution.py:490
  17.8 10.7 %collective-permute-done.1.g_o.refs_4_.g = bf16[2,2,128,512]{3,2,1,0:T(8,128)(2,1)S(1)} collective-permute-done((bf16[2,2,128,512]{3,2,1,0:T(8,128)(2,1)S(1)}, bf16[2,2,128,512]{3,2,1,0:T(8,128)(2,1)S(1)}, u32[]{:S(2)}, u32[]{:S(2)}) %collective-permute-start.1) | collective-permute-done | bytes 524320 | tf_op jit(solution)/shard_map/ppermute | solution.py:490
  30.7 6.2 %collective-permute-start.7 = (bf16[2,64,512]{2,1,0:T(8,128)(2,1)S(1)}, bf16[2,64,512]{2,1,0:T(8,128)(2,1)S(1)}, u32[]{:S(2)}, u32[]{:S(2)}) collective-permute-start(bf16[2,64,512]{2,1,0:T(8,128)(2,1)S(1)} %get-tuple-element.25), channel_id=1, source_target_pairs={{0,3},{1,2},{2,1},{3,0},{4,7},{5,6},{6,5},{7,4},{8,11},{9,10},{10,... | collective-permute-start | bytes 393224 | tf_op jit(solution)/shard_map/ppermute | solution.py:461
  44.0 2.3 %collective-permute-start.22 = (bf16[2,128,512]{2,1,0:T(8,128)(2,1)}, bf16[2,128,512]{2,1,0:T(8,128)(2,1)S(1)}, u32[]{:S(2)}, u32[]{:S(2)}) collective-permute-start(bf16[2,128,512]{2,1,0:T(8,128)(2,1)} %get-tuple-element.32), channel_id=1, source_target_pairs={{1,0},{2,1},{3,2},{4,3},{5,4},{6,5},{7,6},{8,7},{9,8},{10,9},{11,1... | collective-permute-start | bytes 786440 | tf_op jit(solution)/shard_map/ppermute | solution.py:498
  46.4 5.8 %collective-permute-start.10 = (bf16[2,64,512]{2,1,0:T(8,128)(2,1)S(1)}, bf16[2,64,512]{2,1,0:T(8,128)(2,1)S(1)}, u32[]{:S(2)}, u32[]{:S(2)}) collective-permute-start(bf16[2,64,512]{2,1,0:T(8,128)(2,1)S(1)} %select_select_fusion), channel_id=1, source_target_pairs={{0,4},{1,5},{2,6},{3,7},{4,0},{5,1},{6,2},{7,3},{8,12},{9,13},{10,... | collective-permute-start | bytes 393224 | tf_op jit(solution)/shard_map/ppermute | solution.py:461
  52.2 3.3 %pack.5 = (bf16[8,128,512]{2,1,0:T(8,128)(2,1)}, bf16[8,128,512]{2,1,0:T(8,128)(2,1)}) custom-call(s32[2]{0:T(128)} %gids.15, bf16[16,128,512]{2,1,0:T(8,128)(2,1)} %bitcast.6, bf16[16,128,512]{2,1,0:T(8,128)(2,1)} %bitcast.9), custom_call_target="tpu_custom_call" | custom-call | bytes 4194304 | tf_op jit(solution)/shard_map/pack/pallas_call | solution.py:85
  55.6 2.7 %collective-permute-start.4 = (bf16[8,128,512]{2,1,0:T(8,128)(2,1)}, bf16[8,128,512]{2,1,0:T(8,128)(2,1)}, u32[]{:S(2)}, u32[]{:S(2)}) collective-permute-start(bf16[8,128,512]{2,1,0:T(8,128)(2,1)} %get-tuple-element.24), channel_id=1, source_target_pairs={{0,192},{4,196},{8,200},{12,204},{16,208},{20,212},{24,216},{28,22... | collective-permute-start | bytes 3145736 | tf_op jit(solution)/shard_map/ppermute | solution.py:493
  58.4 3.9 %collective-permute-start.11 = (bf16[2,64,512]{2,1,0:T(8,128)(2,1)S(1)}, bf16[2,64,512]{2,1,0:T(8,128)(2,1)S(1)}, u32[]{:S(2)}, u32[]{:S(2)}) collective-permute-start(bf16[2,64,512]{2,1,0:T(8,128)(2,1)S(1)} %broadcast_select_fusion), channel_id=1, source_target_pairs={{0,8},{1,9},{2,10},{3,11},{4,12},{5,13},{6,14},{7,15},{8,0},{9,1},... | collective-permute-start | bytes 393224 | tf_op jit(solution)/shard_map/ppermute | solution.py:461
  63.8 4.9 %collective-permute-done.11 = bf16[2,64,512]{2,1,0:T(8,128)(2,1)S(1)} collective-permute-done((bf16[2,64,512]{2,1,0:T(8,128)(2,1)S(1)}, bf16[2,64,512]{2,1,0:T(8,128)(2,1)S(1)}, u32[]{:S(2)}, u32[]{:S(2)}) %collective-permute-start.11) | collective-permute-done | bytes 131104 | tf_op jit(solution)/shard_map/ppermute | solution.py:461
  69.8 28.6 %collective-permute-done.17.ak_l.refs_6_ = bf16[6,128,512]{2,1,0:T(8,128)(2,1)} collective-permute-done((bf16[6,128,512]{2,1,0:T(8,128)(2,1)S(1)}, bf16[6,128,512]{2,1,0:T(8,128)(2,1)}, u32[]{:S(2)}, u32[]{:S(2)}) %collective-permute-start.17) | collective-permute-done | bytes 786464 | tf_op jit(solution)/shard_map/ppermute | solution.py:490
  98.4 6.0 %collective-permute-start.12 = (bf16[2,64,512]{2,1,0:T(8,128)(2,1)S(1)}, bf16[2,64,512]{2,1,0:T(8,128)(2,1)S(1)}, u32[]{:S(2)}, u32[]{:S(2)}) collective-permute-start(bf16[2,64,512]{2,1,0:T(8,128)(2,1)S(1)} %broadcast_select_fusion.1), channel_id=1, source_target_pairs={{0,16},{1,17},{2,18},{3,19},{4,20},{5,21},{6,22},{7,23},{8,24},{9,... | collective-permute-start | bytes 393224 | tf_op jit(solution)/shard_map/ppermute | solution.py:461
  104.4 2.8 %collective-permute-start.20 = (bf16[8,128,512]{2,1,0:T(8,128)(2,1)}, bf16[8,128,512]{2,1,0:T(8,128)(2,1)}, u32[]{:S(2)}, u32[]{:S(2)}) collective-permute-start(bf16[8,128,512]{2,1,0:T(8,128)(2,1)} %collective-permute-done.19.bk_r.refs_2_), channel_id=1, source_target_pairs={{0,192},{4,196},{8,200},{12,204},{16,208},{20,212},{24,216},{28,22... | collective-permute-start | bytes 3145736 | tf_op jit(solution)/shard_map/ppermute | solution.py:493
  110.9 2.7 %collective-permute-start.5 = (bf16[8,128,512]{2,1,0:T(8,128)(2,1)}, bf16[8,128,512]{2,1,0:T(8,128)(2,1)}, u32[]{:S(2)}, u32[]{:S(2)}) collective-permute-start(bf16[8,128,512]{2,1,0:T(8,128)(2,1)} %collective-permute-done.4.bv_r.refs_4_), channel_id=1, source_target_pairs={{0,192},{4,196},{8,200},{12,204},{16,208},{20,212},{24,216},{28,22... | collective-permute-start | bytes 3145736 | tf_op jit(solution)/shard_map/ppermute | solution.py:493
  113.7 7.0 %collective-permute-done.27.refs_7_ = bf16[8,128,512]{2,1,0:T(8,128)(2,1)S(1)} collective-permute-done((bf16[8,128,512]{2,1,0:T(8,128)(2,1)}, bf16[8,128,512]{2,1,0:T(8,128)(2,1)S(1)}, u32[]{:S(2)}, u32[]{:S(2)}) %collective-permute-start.27) | collective-permute-done | bytes 1048608 | tf_op jit(solution)/shard_map/ppermute | solution.py:490
  121.9 5.1 %collective-permute-done.13 = bf16[2,64,512]{2,1,0:T(8,128)(2,1)S(1)} collective-permute-done((bf16[2,64,512]{2,1,0:T(8,128)(2,1)S(1)}, bf16[2,64,512]{2,1,0:T(8,128)(2,1)S(1)}, u32[]{:S(2)}, u32[]{:S(2)}) %collective-permute-start.13) | collective-permute-done | bytes 131104 | tf_op jit(solution)/shard_map/ppermute | solution.py:461
  128.5 4.4 %collective-permute-start.16 = (bf16[2,64,512]{2,1,0:T(8,128)(2,1)S(1)}, bf16[2,64,512]{2,1,0:T(8,128)(2,1)}, u32[]{:S(2)}, u32[]{:S(2)}) collective-permute-start(bf16[2,64,512]{2,1,0:T(8,128)(2,1)S(1)} %broadcast_select_fusion.3.refs_0_), channel_id=1, source_target_pairs={{0,3},{1,2},{2,1},{3,0},{4,7},{5,6},{6,5},{7,4},{8,11},{9,10},{10,... | collective-permute-start | bytes 393224 | tf_op jit(solution)/shard_map/ppermute | solution.py:461
  133.7 4.0 %collective-permute-done.18.refs_5_ = bf16[6,128,512]{2,1,0:T(8,128)(2,1)} collective-permute-done((bf16[6,128,512]{2,1,0:T(8,128)(2,1)}, bf16[6,128,512]{2,1,0:T(8,128)(2,1)}, u32[]{:S(2)}, u32[]{:S(2)}) %collective-permute-start.18) | collective-permute-done | bytes 786464 | tf_op jit(solution)/shard_map/ppermute | solution.py:490
  137.7 6.6 %collective-permute-start.15 = (bf16[2,64,512]{2,1,0:T(8,128)(2,1)S(1)}, bf16[2,64,512]{2,1,0:T(8,128)(2,1)S(1)}, u32[]{:S(2)}, u32[]{:S(2)}) collective-permute-start(bf16[2,64,512]{2,1,0:T(8,128)(2,1)S(1)} %broadcast_select_fusion.3.refs_0_), channel_id=1, source_target_pairs={{0,2},{1,3},{2,0},{3,1},{4,6},{5,7},{6,4},{7,5},{8,10},{9,11},{10,... | collective-permute-start | bytes 393224 | tf_op jit(solution)/shard_map/ppermute | solution.py:461
  144.3 2.4 %collective-permute-start.14 = (bf16[2,64,512]{2,1,0:T(8,128)(2,1)S(1)}, bf16[2,64,512]{2,1,0:T(8,128)(2,1)S(1)}, u32[]{:S(2)}, u32[]{:S(2)}) collective-permute-start(bf16[2,64,512]{2,1,0:T(8,128)(2,1)S(1)} %broadcast_select_fusion.3.refs_0_), channel_id=1, source_target_pairs={{0,1},{1,0},{2,3},{3,2},{4,5},{5,4},{6,7},{7,6},{8,9},{9,8},{10,11... | collective-permute-start | bytes 393224 | tf_op jit(solution)/shard_map/ppermute | solution.py:461
  156.3 20.4 %near.1 = (f32[16,4,128,128]{3,2,1,0:T(8,128)S(1)}, f32[16,4,128,128]{3,2,1,0:T(8,128)S(1)}, f32[16,4,128,128]{3,2,1,0:T(8,128)S(1)}) custom-call(s32[2]{0:T(128)S(1)} %copy-done.20, s32[16,3]{1,0:T(8,128)S(1)} %copy.10.picks, s32[4]{0:T(128)S(1)} %copy-done.22, bf16[2048,512]{1,0:T(8,128)(2,1)S(1)} %copy-done.2, bf16[2048,512]{1,0:T(8,128)(2,1)S(1)} %copy-done, ...), custom_call_target="tpu_custom_call" | custom-call | flops 2684354560 | bytes 27262976 | tf_op jit(solution)/shard_map/near/pallas_call | solution.py:229
  176.8 11.6 %score.1 = (bf16[16,4,128,128]{3,2,1,0:T(8,128)(2,1)S(1)}, f32[16,4,128,128]{3,2,1,0:T(8,128)S(1)}, f32[16,4,128,128]{3,2,1,0:T(8,128)S(1)}) custom-call(s32[2]{0:T(128)S(1)} %copy-done.20, s32[16,3]{1,0:T(8,128)S(1)} %copy.10.picks, s32[4]{0:T(128)S(1)} %copy-done.22, ...), custom_call_target="tpu_custom_call", output_to_operand_aliasing={{1}: (12, {}), {2}: (13, {})} | custom-call | flops 1342177280 | bytes 29360128 | tf_op jit(solution)/shard_map/score/pallas_call | solution.py:306
  188.5 5.4 %last.1 = bf16[2048,512]{1,0:T(8,128)(2,1)} custom-call(s32[2]{0:T(128)S(1)} %copy-done.20, s32[16,3]{1,0:T(8,128)S(1)} %copy.10.picks, bf16[2,2,128,512]{3,2,1,0:T(8,128)(2,1)S(1)} %copy-done.5, bf16[6,128,512]{2,1,0:T(8,128)(2,1)} %collective-permute-done.3.a_v, bf16[8,128,512]{2,1,0:T(8,128)(2,1)} %collective-permute-done.5.b_v, ...), custom_call_target="tpu_custom_call" | custom-call | flops 268435456 | bytes 10485760 | tf_op jit(solution)/shard_map/last/pallas_call | solution.py:359
  (100 shorter events, 35.9 us)
Async XLA Ops:
  2.8 13.0 %collective-permute-start = (bf16[2,2,128,512]{3,2,1,0:T(8,128)(2,1)}, bf16[2,2,128,512]{3,2,1,0:T(8,128)(2,1)S(1)}, u32[]{:S(2)}, u32[]{:S(2)}) collective-permute-start(bf16[2,2,128,512]{3,2,1,0:T(8,128)(2,1)} %pack.3.g), channel_id=1, source_target_pairs={{0,64},{4,68},{8,72},{12,76},{16,80},{20,84},{24,88},{28,92},{32,9... | collective-permute-start | bytes 1572872 | tf_op jit(solution)/shard_map/ppermute | solution.py:490
  4.9 12.9 %collective-permute-start.6 = (bf16[2,2,128,512]{3,2,1,0:T(8,128)(2,1)}, bf16[2,2,128,512]{3,2,1,0:T(8,128)(2,1)S(1)}, u32[]{:S(2)}, u32[]{:S(2)}) collective-permute-start(bf16[2,2,128,512]{3,2,1,0:T(8,128)(2,1)} %pack.3.g), channel_id=1, source_target_pairs={{0,192},{4,196},{8,200},{12,204},{16,208},{20,212},{24,216},{28,22... | collective-permute-start | bytes 1572872 | tf_op jit(solution)/shard_map/ppermute | solution.py:493
  9.6 46.0 %collective-permute-start.26 = (bf16[6,128,512]{2,1,0:T(8,128)(2,1)}, bf16[6,128,512]{2,1,0:T(8,128)(2,1)}, u32[]{:S(2)}, u32[]{:S(2)}) collective-permute-start(bf16[6,128,512]{2,1,0:T(8,128)(2,1)} %get-tuple-element.23), channel_id=1, source_target_pairs={{0,192},{4,196},{8,200},{12,204},{16,208},{20,212},{24,216},{28,22... | collective-permute-start | bytes 2359304 | tf_op jit(solution)/shard_map/ppermute | solution.py:493
  15.8 12.6 %collective-permute-start.1 = (bf16[2,2,128,512]{3,2,1,0:T(8,128)(2,1)S(1)}, bf16[2,2,128,512]{3,2,1,0:T(8,128)(2,1)S(1)}, u32[]{:S(2)}, u32[]{:S(2)}) collective-permute-start(bf16[2,2,128,512]{3,2,1,0:T(8,128)(2,1)S(1)} %collective-permute-done.g_l.refs_5_), channel_id=1, source_target_pairs={{0,64},{4,68},{8,72},{12,76},{16,80},{20,84},{24,88},{28,92},{32,9... | collective-permute-start | bytes 1572872 | tf_op jit(solution)/shard_map/ppermute | solution.py:490
  36.9 21.6 %collective-permute-start.2 = (bf16[6,128,512]{2,1,0:T(8,128)(2,1)}, bf16[6,128,512]{2,1,0:T(8,128)(2,1)}, u32[]{:S(2)}, u32[]{:S(2)}) collective-permute-start(bf16[6,128,512]{2,1,0:T(8,128)(2,1)} %get-tuple-element.23), channel_id=1, source_target_pairs={{0,64},{4,68},{8,72},{12,76},{16,80},{20,84},{24,88},{28,92},{32,9... | collective-permute-start | bytes 2359304 | tf_op jit(solution)/shard_map/ppermute | solution.py:490
  36.9 9.5 %collective-permute-start.21 = (bf16[2,128,512]{2,1,0:T(8,128)(2,1)}, bf16[2,128,512]{2,1,0:T(8,128)(2,1)S(1)}, u32[]{:S(2)}, u32[]{:S(2)}) collective-permute-start(bf16[2,128,512]{2,1,0:T(8,128)(2,1)} %get-tuple-element.31), channel_id=1, source_target_pairs={{0,1},{1,2},{2,3},{3,4},{4,5},{5,6},{6,7},{7,8},{8,9},{9,10},{10,1... | collective-permute-start | bytes 786440 | tf_op jit(solution)/shard_map/ppermute | solution.py:498
  39.7 22.6 %collective-permute-start.25 = (bf16[6,128,512]{2,1,0:T(8,128)(2,1)}, bf16[6,128,512]{2,1,0:T(8,128)(2,1)S(1)}, u32[]{:S(2)}, u32[]{:S(2)}) collective-permute-start(bf16[6,128,512]{2,1,0:T(8,128)(2,1)} %get-tuple-element.29), channel_id=1, source_target_pairs={{0,192},{4,196},{8,200},{12,204},{16,208},{20,212},{24,216},{28,22... | collective-permute-start | bytes 2359304 | tf_op jit(solution)/shard_map/ppermute | solution.py:493
  44.0 11.5 %collective-permute-start.22 = (bf16[2,128,512]{2,1,0:T(8,128)(2,1)}, bf16[2,128,512]{2,1,0:T(8,128)(2,1)S(1)}, u32[]{:S(2)}, u32[]{:S(2)}) collective-permute-start(bf16[2,128,512]{2,1,0:T(8,128)(2,1)} %get-tuple-element.32), channel_id=1, source_target_pairs={{1,0},{2,1},{3,2},{4,3},{5,4},{6,5},{7,6},{8,7},{9,8},{10,9},{11,1... | collective-permute-start | bytes 786440 | tf_op jit(solution)/shard_map/ppermute | solution.py:498
  46.4 11.9 %collective-permute-start.10 = (bf16[2,64,512]{2,1,0:T(8,128)(2,1)S(1)}, bf16[2,64,512]{2,1,0:T(8,128)(2,1)S(1)}, u32[]{:S(2)}, u32[]{:S(2)}) collective-permute-start(bf16[2,64,512]{2,1,0:T(8,128)(2,1)S(1)} %select_select_fusion), channel_id=1, source_target_pairs={{0,4},{1,5},{2,6},{3,7},{4,0},{5,1},{6,2},{7,3},{8,12},{9,13},{10,... | collective-permute-start | bytes 393224 | tf_op jit(solution)/shard_map/ppermute | solution.py:461
  55.5 53.7 %collective-permute-start.28 = (bf16[8,128,512]{2,1,0:T(8,128)(2,1)}, bf16[8,128,512]{2,1,0:T(8,128)(2,1)S(1)}, u32[]{:S(2)}, u32[]{:S(2)}) collective-permute-start(bf16[8,128,512]{2,1,0:T(8,128)(2,1)} %get-tuple-element.24), channel_id=1, source_target_pairs={{0,64},{4,68},{8,72},{12,76},{16,80},{20,84},{24,88},{28,92},{32,9... | collective-permute-start | bytes 3145736 | tf_op jit(solution)/shard_map/ppermute | solution.py:490
  55.6 51.6 %collective-permute-start.4 = (bf16[8,128,512]{2,1,0:T(8,128)(2,1)}, bf16[8,128,512]{2,1,0:T(8,128)(2,1)}, u32[]{:S(2)}, u32[]{:S(2)}) collective-permute-start(bf16[8,128,512]{2,1,0:T(8,128)(2,1)} %get-tuple-element.24), channel_id=1, source_target_pairs={{0,192},{4,196},{8,200},{12,204},{16,208},{20,212},{24,216},{28,22... | collective-permute-start | bytes 3145736 | tf_op jit(solution)/shard_map/ppermute | solution.py:493
  58.3 46.2 %collective-permute-start.19 = (bf16[8,128,512]{2,1,0:T(8,128)(2,1)}, bf16[8,128,512]{2,1,0:T(8,128)(2,1)}, u32[]{:S(2)}, u32[]{:S(2)}) collective-permute-start(bf16[8,128,512]{2,1,0:T(8,128)(2,1)} %get-tuple-element.30), channel_id=1, source_target_pairs={{0,192},{4,196},{8,200},{12,204},{16,208},{20,212},{24,216},{28,22... | collective-permute-start | bytes 3145736 | tf_op jit(solution)/shard_map/ppermute | solution.py:493
  58.4 10.2 %collective-permute-start.11 = (bf16[2,64,512]{2,1,0:T(8,128)(2,1)S(1)}, bf16[2,64,512]{2,1,0:T(8,128)(2,1)S(1)}, u32[]{:S(2)}, u32[]{:S(2)}) collective-permute-start(bf16[2,64,512]{2,1,0:T(8,128)(2,1)S(1)} %broadcast_select_fusion), channel_id=1, source_target_pairs={{0,8},{1,9},{2,10},{3,11},{4,12},{5,13},{6,14},{7,15},{8,0},{9,1},... | collective-permute-start | bytes 393224 | tf_op jit(solution)/shard_map/ppermute | solution.py:461
  62.3 36.1 %collective-permute-start.17 = (bf16[6,128,512]{2,1,0:T(8,128)(2,1)S(1)}, bf16[6,128,512]{2,1,0:T(8,128)(2,1)}, u32[]{:S(2)}, u32[]{:S(2)}) collective-permute-start(bf16[6,128,512]{2,1,0:T(8,128)(2,1)S(1)} %copy-done.23), channel_id=1, source_target_pairs={{0,64},{4,68},{8,72},{12,76},{16,80},{20,84},{24,88},{28,92},{32,9... | collective-permute-start | bytes 2359304 | tf_op jit(solution)/shard_map/ppermute | solution.py:490
  68.7 52.1 %collective-permute-start.27 = (bf16[8,128,512]{2,1,0:T(8,128)(2,1)}, bf16[8,128,512]{2,1,0:T(8,128)(2,1)S(1)}, u32[]{:S(2)}, u32[]{:S(2)}) collective-permute-start(bf16[8,128,512]{2,1,0:T(8,128)(2,1)} %get-tuple-element.30), channel_id=1, source_target_pairs={{0,64},{4,68},{8,72},{12,76},{16,80},{20,84},{24,88},{28,92},{32,9... | collective-permute-start | bytes 3145736 | tf_op jit(solution)/shard_map/ppermute | solution.py:490
  98.4 12.5 %collective-permute-start.12 = (bf16[2,64,512]{2,1,0:T(8,128)(2,1)S(1)}, bf16[2,64,512]{2,1,0:T(8,128)(2,1)S(1)}, u32[]{:S(2)}, u32[]{:S(2)}) collective-permute-start(bf16[2,64,512]{2,1,0:T(8,128)(2,1)S(1)} %broadcast_select_fusion.1), channel_id=1, source_target_pairs={{0,16},{1,17},{2,18},{3,19},{4,20},{5,21},{6,22},{7,23},{8,24},{9,... | collective-permute-start | bytes 393224 | tf_op jit(solution)/shard_map/ppermute | solution.py:461
  104.4 72.4 %collective-permute-start.20 = (bf16[8,128,512]{2,1,0:T(8,128)(2,1)}, bf16[8,128,512]{2,1,0:T(8,128)(2,1)}, u32[]{:S(2)}, u32[]{:S(2)}) collective-permute-start(bf16[8,128,512]{2,1,0:T(8,128)(2,1)} %collective-permute-done.19.bk_r.refs_2_), channel_id=1, source_target_pairs={{0,192},{4,196},{8,200},{12,204},{16,208},{20,212},{24,216},{28,22... | collective-permute-start | bytes 3145736 | tf_op jit(solution)/shard_map/ppermute | solution.py:493
  107.2 30.5 %collective-permute-start.18 = (bf16[6,128,512]{2,1,0:T(8,128)(2,1)}, bf16[6,128,512]{2,1,0:T(8,128)(2,1)}, u32[]{:S(2)}, u32[]{:S(2)}) collective-permute-start(bf16[6,128,512]{2,1,0:T(8,128)(2,1)} %collective-permute-done.17.ak_l.refs_6_), channel_id=1, source_target_pairs={{0,64},{4,68},{8,72},{12,76},{16,80},{20,84},{24,88},{28,92},{32,9... | collective-permute-start | bytes 2359304 | tf_op jit(solution)/shard_map/ppermute | solution.py:490
  110.2 11.7 %collective-permute-start.23 = (bf16[2,128,512]{2,1,0:T(8,128)(2,1)S(1)}, bf16[2,128,512]{2,1,0:T(8,128)(2,1)S(1)}, u32[]{:S(2)}, u32[]{:S(2)}) collective-permute-start(bf16[2,128,512]{2,1,0:T(8,128)(2,1)S(1)} %get-tuple-element.33), channel_id=1, source_target_pairs={{63,0},{127,64},{191,128},{255,192}} | collective-permute-start | bytes 786440 | tf_op jit(solution)/shard_map/ppermute | solution.py:498
  110.9 77.6 %collective-permute-start.5 = (bf16[8,128,512]{2,1,0:T(8,128)(2,1)}, bf16[8,128,512]{2,1,0:T(8,128)(2,1)}, u32[]{:S(2)}, u32[]{:S(2)}) collective-permute-start(bf16[8,128,512]{2,1,0:T(8,128)(2,1)} %collective-permute-done.4.bv_r.refs_4_), channel_id=1, source_target_pairs={{0,192},{4,196},{8,200},{12,204},{16,208},{20,212},{24,216},{28,22... | collective-permute-start | bytes 3145736 | tf_op jit(solution)/shard_map/ppermute | solution.py:493
  121.9 66.6 %collective-permute-start.3 = (bf16[6,128,512]{2,1,0:T(8,128)(2,1)}, bf16[6,128,512]{2,1,0:T(8,128)(2,1)}, u32[]{:S(2)}, u32[]{:S(2)}) collective-permute-start(bf16[6,128,512]{2,1,0:T(8,128)(2,1)} %collective-permute-done.2.av_l.refs_8_), channel_id=1, source_target_pairs={{0,64},{4,68},{8,72},{12,76},{16,80},{20,84},{24,88},{28,92},{32,9... | collective-permute-start | bytes 2359304 | tf_op jit(solution)/shard_map/ppermute | solution.py:490
  128.5 15.7 %collective-permute-start.16 = (bf16[2,64,512]{2,1,0:T(8,128)(2,1)S(1)}, bf16[2,64,512]{2,1,0:T(8,128)(2,1)}, u32[]{:S(2)}, u32[]{:S(2)}) collective-permute-start(bf16[2,64,512]{2,1,0:T(8,128)(2,1)S(1)} %broadcast_select_fusion.3.refs_0_), channel_id=1, source_target_pairs={{0,3},{1,2},{2,1},{3,0},{4,7},{5,6},{6,5},{7,4},{8,11},{9,10},{10,... | collective-permute-start | bytes 393224 | tf_op jit(solution)/shard_map/ppermute | solution.py:461
  137.7 39.1 %collective-permute-start.15 = (bf16[2,64,512]{2,1,0:T(8,128)(2,1)S(1)}, bf16[2,64,512]{2,1,0:T(8,128)(2,1)S(1)}, u32[]{:S(2)}, u32[]{:S(2)}) collective-permute-start(bf16[2,64,512]{2,1,0:T(8,128)(2,1)S(1)} %broadcast_select_fusion.3.refs_0_), channel_id=1, source_target_pairs={{0,2},{1,3},{2,0},{3,1},{4,6},{5,7},{6,4},{7,5},{8,10},{9,11},{10,... | collective-permute-start | bytes 393224 | tf_op jit(solution)/shard_map/ppermute | solution.py:461
  144.3 32.5 %collective-permute-start.14 = (bf16[2,64,512]{2,1,0:T(8,128)(2,1)S(1)}, bf16[2,64,512]{2,1,0:T(8,128)(2,1)S(1)}, u32[]{:S(2)}, u32[]{:S(2)}) collective-permute-start(bf16[2,64,512]{2,1,0:T(8,128)(2,1)S(1)} %broadcast_select_fusion.3.refs_0_), channel_id=1, source_target_pairs={{0,1},{1,0},{2,3},{3,2},{4,5},{5,4},{6,7},{7,6},{8,9},{9,8},{10,11... | collective-permute-start | bytes 393224 | tf_op jit(solution)/shard_map/ppermute | solution.py:461
  (29 other events, 594.5 us)

commit v3 on v2

--- a/solution.py
+++ b/solution.py
@@ -16,7 +16,7 @@
 W = H * DH
 SCALE_LOG2 = math.log2(math.e) / math.sqrt(DH)
 G_N, A_N, B_N = 2, 6, 8
-NEAR_VMEM, SCORE_VMEM, LAST_VMEM = 24 << 20, 24 << 20, 12 << 20
+NEAR_VMEM, SCORE_VMEM, LAST_VMEM = 41 << 20, 24 << 20, 12 << 20
 ANY = pl.BlockSpec(memory_space=pl.ANY)
 VM = pl.BlockSpec(memory_space=pltpu.VMEM)
 SM = pl.BlockSpec(memory_space=pltpu.SMEM)
@@ -138,7 +138,7 @@
 
 
 def state_of(blocks):
-    return [jax.ShapeDtypeStruct((blocks, H, BS, DH), jnp.float32)] * 3
+    return [pltpu.VMEM((blocks, H, BS, DH), jnp.float32)] * 3
 
 
 def fetch_pick(position, parts, dst, sem):
@@ -155,9 +155,9 @@
 
 def near_kernel(blocks, gids, picks, place, q_ref, keys, values, low, high, first, last, *refs):
     sides, refs = (refs[:5], refs[5:10]), refs[10:]
-    top_ref, total_ref, acc_ref, kbuf, vbuf, buf, sem, pick_sem = refs
+    top_ref, total_ref, acc_ref, qbuf, kbuf, vbuf, buf, sem, pick_sem = refs
     places = first_two(gids, blocks)
-    copies = []
+    copies = [pltpu.make_async_copy(q_ref, qbuf, sem.at[0, 3])]
     for half, (ref, dst) in enumerate(((keys, kbuf), (values, vbuf))):
         copies.append(pltpu.make_async_copy(ref, dst.at[pl.ds(BS, blocks * BS)], sem.at[half, 0]))
     for copy in copies:
@@ -200,20 +200,25 @@
                 pltpu.make_async_copy(
                     sides[side][2].at[0], buf.at[j, half, side], pick_sem.at[j, half, side]
                 ).wait()
-        keys_of, values_of = [
+        q = [qbuf[rows, head(h)] for h in range(H)]
+        own_keys = [kbuf[span, head(h)] for h in range(H)]
+        own_values = [vbuf[span, head(h)] for h in range(H)]
+        side_keys, side_values = [
             [
-                jnp.concatenate(
-                    [own[span, head(h)], buf[j, half, 0, :, head(h)], buf[j, half, 1, :, head(h)]],
-                    axis=0,
-                )
+                jnp.concatenate([buf[j, half, side, :, head(h)] for side in range(2)], axis=0)
                 for h in range(H)
             ]
-            for half, own in enumerate((kbuf, vbuf))
+            for half in range(2)
         ]
-        scores = [dot_t(q_ref[rows, head(h)], keys_of[h]) for h in range(H)]
-        tops = [top_of([s]) for s in scores]
-        weights = [weigh(s, top) for s, top in zip(scores, tops)]
-        mixed = [mix(w, v) for w, v in zip(weights, values_of)]
+        own_scores = [dot_t(q[h], own_keys[h]) for h in range(H)]
+        side_scores = [dot_t(q[h], side_keys[h]) for h in range(H)]
+        tops = [top_of([own_scores[h], side_scores[h]]) for h in range(H)]
+        own_weights = [weigh(own_scores[h], tops[h]) for h in range(H)]
+        side_weights = [weigh(side_scores[h], tops[h]) for h in range(H)]
+        mixed = [
+            mix(own_weights[h], own_values[h]) + mix(side_weights[h], side_values[h])
+            for h in range(H)
+        ]
         for h in range(H):
             top_ref[j, h] = tops[h]
             total_ref[j, h] = mixed[h][:, DH:]
@@ -229,13 +234,14 @@
     return pl.pallas_call(
         functools.partial(near_kernel, blocks),
         out_shape=state_of(blocks),
-        in_specs=[SM, SM, SM, VM] + [ANY] * 16,
+        in_specs=[SM, SM, SM] + [ANY] * 17,
         out_specs=[VM] * 3,
         scratch_shapes=[
+            pltpu.VMEM((rows, W), keys.dtype),
             pltpu.VMEM(((blocks + 2) * BS, W), keys.dtype),
             pltpu.VMEM(((blocks + 2) * BS, W), keys.dtype),
             pltpu.VMEM((blocks, 2, 2, BS, W), keys.dtype),
-            pltpu.SemaphoreType.DMA((2, 3)),
+            pltpu.SemaphoreType.DMA((2, 4)),
             pltpu.SemaphoreType.DMA((blocks, 2, 2)),
         ],
         compiler_params=pltpu.CompilerParams(vmem_limit_bytes=NEAR_VMEM),
@@ -323,24 +329,33 @@
     )(gids, picks, place, queries, *pieces, *opposite, *state)
 
 
-def last_kernel(blocks, gids, picks, g, a_v, b_v, weights, share, acc, out, buf, obuf, sem, out_sem):
+def last_kernel(blocks, gids, picks, g, a_v, b_v, weights, share, acc, out, obuf, out_sem):
     places = first_two(gids, blocks)
-
-    def fetch(j, carry):
-        fetch_pick(position_of(picks[j, 1], places, blocks), (g.at[1], a_v, b_v), buf.at[j], sem.at[j])
-        return carry
-
-    lax.fori_loop(0, blocks, fetch, 0)
 
     def store(j):
         rows = pl.ds(pl.multiple_of(j * BS, BS), BS)
         return pltpu.make_async_copy(obuf.at[j], out.at[rows], out_sem.at[j])
 
     def step(j, carry):
-        pltpu.make_async_copy(b_v.at[0], buf.at[j], sem.at[j]).wait()
-        mixed = [(dot(weights[j, h], buf[j, :, head(h)]) + acc[j, h]) * share[j, h] for h in range(H)]
-        for h in range(H):
-            obuf[j, :, head(h)] = mixed[h].astype(obuf.dtype)
+        position = position_of(picks[j, 1], places, blocks)
+
+        def finish(v):
+            mixed = [(dot(weights[j, h], v[:, head(h)]) + acc[j, h]) * share[j, h] for h in range(H)]
+            for h in range(H):
+                obuf[j, :, head(h)] = mixed[h].astype(obuf.dtype)
+
+        @pl.when(position < G_N)
+        def _():
+            finish(g.at[1, jnp.minimum(position, G_N - 1)])
+
+        @pl.when((position >= G_N) & (position < G_N + A_N))
+        def _():
+            finish(a_v.at[jnp.clip(position - G_N, 0, A_N - 1)])
+
+        @pl.when(position >= G_N + A_N)
+        def _():
+            finish(b_v.at[jnp.clip(position - G_N - A_N, 0, B_N - 1)])
+
         store(j).start()
         return carry
 
@@ -359,12 +374,10 @@
     return pl.pallas_call(
         functools.partial(last_kernel, blocks),
         out_shape=jax.ShapeDtypeStruct(like.shape, like.dtype),
-        in_specs=[SM, SM] + [ANY] * 3 + [VM] * 3,
+        in_specs=[SM, SM] + [VM] * 6,
         out_specs=ANY,
         scratch_shapes=[
             pltpu.VMEM((blocks, BS, W), like.dtype),
-            pltpu.VMEM((blocks, BS, W), like.dtype),
-            pltpu.SemaphoreType.DMA((blocks,)),
             pltpu.SemaphoreType.DMA((blocks,)),
         ],
         compiler_params=pltpu.CompilerParams(vmem_limit_bytes=LAST_VMEM),
@@ -409,7 +422,7 @@
         in_specs=[SM, SM] + [ANY] * 4,
         out_specs=[VM] * 4,
         scratch_shapes=[pltpu.SemaphoreType.DMA((2, 4))],
-        compiler_params=pltpu.CompilerParams(vmem_limit_bytes=2 << 20),
+        compiler_params=pltpu.CompilerParams(vmem_limit_bytes=56 << 20),
         cost_estimate=pl.CostEstimate(flops=0, transcendentals=0, bytes_accessed=1 << 20),
         name="choose",
     )(gids, place, g, g_r, g_o, g_l)
@@ -450,7 +463,7 @@
         in_specs=[SM] + [ANY] * 6,
         out_specs=[VM] * 2,
         scratch_shapes=[pltpu.SemaphoreType.DMA((2, 2))],
-        compiler_params=pltpu.CompilerParams(vmem_limit_bytes=2 << 20),
+        compiler_params=pltpu.CompilerParams(vmem_limit_bytes=8 << 20),
         cost_estimate=pl.CostEstimate(flops=0, transcendentals=0, bytes_accessed=1 << 20),
         name="ends",
     )(gids, g_l, ak_l, av_l, g_r, bk_r, bv_r)
@@ -541,6 +554,8 @@
     weights, share, acc = score(
         global_ids, rand_pick, place, queries, pieces, (g_o, ak_o, bk_o), state
     )
+    av_o = pltpu.with_memory_space_constraint(av_o, pltpu.VMEM)
+    bv_o = pltpu.with_memory_space_constraint(bv_o, pltpu.VMEM)
     return last(global_ids, rand_pick, (g_o, av_o, bv_o), weights, share, acc, queries)
 
 

time: 195 us -> 185 us (0.949)
  local copies, waits for them, and re-layouts: 13.9 us -> 4.88 us
  starting transfers between devices: 61.2 us -> 58.1 us
  waiting for transfers between devices: 67.7 us -> 70.4 us
    unnamed x49 -> x43, local copies, waits for them, and re-layouts: 13.9 us -> 4.88 us
    ppermute x8, waiting for transfers between devices: 55 us -> 58.5 us  [to_right(): return lax.ppermute(v, 'blk', right)]
    ppermute x10, starting transfers between devices: 36 us -> 33.6 us  [swap(): return lax.ppermute(value, ALL, [(i, i ^ bits) for i in range(count)])]
    pallas_call x1, Pallas kernels: 20.4 us -> 18.2 us  [near(): pl.pallas_call(functools.partial(near_kernel, blocks), out_shape=state_of...]
where the time goes in v3:
time: 185 us
  waiting for transfers between devices  70.4 us (38%)
  starting transfers between devices  58.1 us (31%)
  Pallas kernels  48.6 us (26%)
  local copies, waits for them, and re-layouts  4.88 us (3%)
  other arithmetic  1.95 us (1%)
    ppermute x8, waiting for transfers between devices, to_right(): return lax.ppermute(v, 'blk', right)  58.5 us
    ppermute x10, starting transfers between devices, swap(): return lax.ppermute(value, ALL, [(i, i ^ bits) for i in range(count)])  33.6 us
    pallas_call x1, Pallas kernels, near(): pl.pallas_call(functools.partial(near_kernel, blocks), out_shape=state_of...  18.2 us
    ppermute x7, starting transfers between devices, to_left(): return lax.ppermute(v, 'blk', left)  12.2 us
    pallas_call x1, Pallas kernels, score(): pl.pallas_call(functools.partial(score_kernel, blocks), out_shape=[jax.Sh...  12 us
    ppermute x10, waiting for transfers between devices, swap(): return lax.ppermute(value, ALL, [(i, i ^ bits) for i in range(count)])  11.9 us
    pallas_call x3, Pallas kernels, pack(): pl.pallas_call(functools.partial(pack_kernel, start, count, joined, ends)...  9.29 us
    ppermute x8, starting transfers between devices, to_right(): return lax.ppermute(v, 'blk', right)  6.55 us
  transfers between devices with their start and end apart: 29, of which 10 were waited for; matrix products, arithmetic and copies ran while one was open for 1% of the time, Pallas kernels for 22%

profile of v3, /device:TPU:1, one launch (start us, length us, event | category | flops | bytes accessed | tf_op | source)
XLA Modules:
  0.0 184.5 jit_solution(15554788561473527362)
XLA Ops:
  0.0 2.8 %pack.3.g = bf16[2,2,128,512]{3,2,1,0:T(8,128)(2,1)} custom-call(s32[2]{0:T(128)} %gids.15, bf16[16,128,512]{2,1,0:T(8,128)(2,1)} %bitcast.4, bf16[16,128,512]{2,1,0:T(8,128)(2,1)} %bitcast.7), custom_call_target="tpu_custom_call" | custom-call | bytes 1048576 | tf_op jit(solution)/shard_map/pack/pallas_call | solution.py:85
  6.2 3.3 %pack.4 = (bf16[6,128,512]{2,1,0:T(8,128)(2,1)}, bf16[6,128,512]{2,1,0:T(8,128)(2,1)}, bf16[2,128,512]{2,1,0:T(8,128)(2,1)}, bf16[2,128,512]{2,1,0:T(8,128)(2,1)}) custom-call(s32[2]{0:T(128)} %gids.15, bf16[16,128,512]{2,1,0:T(8,128)(2,1)} %bitcast.5, bf16[16,128,512]{2,1,0:T(8,128)(2,1)} %bitcast.8), custom_call_target="tpu_custom_call" | custom-call | bytes 4194304 | tf_op jit(solution)/shard_map/pack/pallas_call | solution.py:85
  11.0 4.8 %collective-permute-done.g_l.refs_5_ = bf16[2,2,128,512]{3,2,1,0:T(8,128)(2,1)S(1)} collective-permute-done((bf16[2,2,128,512]{3,2,1,0:T(8,128)(2,1)}, bf16[2,2,128,512]{3,2,1,0:T(8,128)(2,1)S(1)}, u32[]{:S(2)}, u32[]{:S(2)}) %collective-permute-start) | collective-permute-done | bytes 524320 | tf_op jit(solution)/shard_map/ppermute | solution.py:503
  18.3 10.1 %collective-permute-done.1.g_o.refs_4_.g = bf16[2,2,128,512]{3,2,1,0:T(8,128)(2,1)S(1)} collective-permute-done((bf16[2,2,128,512]{3,2,1,0:T(8,128)(2,1)S(1)}, bf16[2,2,128,512]{3,2,1,0:T(8,128)(2,1)S(1)}, u32[]{:S(2)}, u32[]{:S(2)}) %collective-permute-start.1) | collective-permute-done | bytes 524320 | tf_op jit(solution)/shard_map/ppermute | solution.py:503
  29.2 2.6 %choose.1 = (bf16[2,64,512]{2,1,0:T(8,128)(2,1)}, bf16[2,64,512]{2,1,0:T(8,128)(2,1)}, bf16[2,64,512]{2,1,0:T(8,128)(2,1)}, bf16[2,64,512]{2,1,0:T(8,128)(2,1)}) custom-call(s32[2]{0:T(128)} %gids.15, s32[4]{0:T(128)} %pad_add_fusion.place, bf16[2,2,128,512]{3,2,1,0:T(8,128)(2,1)} %pack.3.g, bf16[2,2,128,512]{3,2,1,0:T(8,128)(2,1)} %copy-done.3, ...), custom_call_target="tpu_custom_call" | custom-call | bytes 1048576 | tf_op jit(solution)/shard_map/choose/pallas_call | solution.py:419
  31.9 6.3 %collective-permute-start.7 = (bf16[2,64,512]{2,1,0:T(8,128)(2,1)}, bf16[2,64,512]{2,1,0:T(8,128)(2,1)S(1)}, u32[]{:S(2)}, u32[]{:S(2)}) collective-permute-start(bf16[2,64,512]{2,1,0:T(8,128)(2,1)} %get-tuple-element.25), channel_id=1, source_target_pairs={{0,3},{1,2},{2,1},{3,0},{4,7},{5,6},{6,5},{7,4},{8,11},{9,10},{10,... | collective-permute-start | bytes 393224 | tf_op jit(solution)/shard_map/ppermute | solution.py:474
  45.7 2.3 %collective-permute-start.22 = (bf16[2,128,512]{2,1,0:T(8,128)(2,1)}, bf16[2,128,512]{2,1,0:T(8,128)(2,1)S(1)}, u32[]{:S(2)}, u32[]{:S(2)}) collective-permute-start(bf16[2,128,512]{2,1,0:T(8,128)(2,1)} %get-tuple-element.32), channel_id=1, source_target_pairs={{1,0},{2,1},{3,2},{4,3},{5,4},{6,5},{7,6},{8,7},{9,8},{10,9},{11,1... | collective-permute-start | bytes 786440 | tf_op jit(solution)/shard_map/ppermute | solution.py:511
  49.0 5.8 %collective-permute-start.10 = (bf16[2,64,512]{2,1,0:T(8,128)(2,1)S(1)}, bf16[2,64,512]{2,1,0:T(8,128)(2,1)S(1)}, u32[]{:S(2)}, u32[]{:S(2)}) collective-permute-start(bf16[2,64,512]{2,1,0:T(8,128)(2,1)S(1)} %select_select_fusion), channel_id=1, source_target_pairs={{0,4},{1,5},{2,6},{3,7},{4,0},{5,1},{6,2},{7,3},{8,12},{9,13},{10,... | collective-permute-start | bytes 393224 | tf_op jit(solution)/shard_map/ppermute | solution.py:474
  54.8 3.2 %pack.5 = (bf16[8,128,512]{2,1,0:T(8,128)(2,1)}, bf16[8,128,512]{2,1,0:T(8,128)(2,1)}) custom-call(s32[2]{0:T(128)} %gids.15, bf16[16,128,512]{2,1,0:T(8,128)(2,1)} %bitcast.6, bf16[16,128,512]{2,1,0:T(8,128)(2,1)} %bitcast.9), custom_call_target="tpu_custom_call" | custom-call | bytes 4194304 | tf_op jit(solution)/shard_map/pack/pallas_call | solution.py:85
  58.8 2.7 %collective-permute-start.4 = (bf16[8,128,512]{2,1,0:T(8,128)(2,1)}, bf16[8,128,512]{2,1,0:T(8,128)(2,1)S(1)}, u32[]{:S(2)}, u32[]{:S(2)}) collective-permute-start(bf16[8,128,512]{2,1,0:T(8,128)(2,1)} %get-tuple-element.24), channel_id=1, source_target_pairs={{0,192},{4,196},{8,200},{12,204},{16,208},{20,212},{24,216},{28,22... | collective-permute-start | bytes 3145736 | tf_op jit(solution)/shard_map/ppermute | solution.py:506
  61.6 3.1 %collective-permute-start.11 = (bf16[2,64,512]{2,1,0:T(8,128)(2,1)S(1)}, bf16[2,64,512]{2,1,0:T(8,128)(2,1)S(1)}, u32[]{:S(2)}, u32[]{:S(2)}) collective-permute-start(bf16[2,64,512]{2,1,0:T(8,128)(2,1)S(1)} %broadcast_select_fusion), channel_id=1, source_target_pairs={{0,8},{1,9},{2,10},{3,11},{4,12},{5,13},{6,14},{7,15},{8,0},{9,1},... | collective-permute-start | bytes 393224 | tf_op jit(solution)/shard_map/ppermute | solution.py:474
  66.2 4.4 %collective-permute-done.11 = bf16[2,64,512]{2,1,0:T(8,128)(2,1)S(1)} collective-permute-done((bf16[2,64,512]{2,1,0:T(8,128)(2,1)S(1)}, bf16[2,64,512]{2,1,0:T(8,128)(2,1)S(1)}, u32[]{:S(2)}, u32[]{:S(2)}) %collective-permute-start.11) | collective-permute-done | bytes 131104 | tf_op jit(solution)/shard_map/ppermute | solution.py:474
  71.7 29.8 %collective-permute-done.17.ak_l.refs_6_ = bf16[6,128,512]{2,1,0:T(8,128)(2,1)} collective-permute-done((bf16[6,128,512]{2,1,0:T(8,128)(2,1)S(1)}, bf16[6,128,512]{2,1,0:T(8,128)(2,1)}, u32[]{:S(2)}, u32[]{:S(2)}) %collective-permute-start.17) | collective-permute-done | bytes 786464 | tf_op jit(solution)/shard_map/ppermute | solution.py:503
  101.6 6.0 %collective-permute-start.12 = (bf16[2,64,512]{2,1,0:T(8,128)(2,1)S(1)}, bf16[2,64,512]{2,1,0:T(8,128)(2,1)S(1)}, u32[]{:S(2)}, u32[]{:S(2)}) collective-permute-start(bf16[2,64,512]{2,1,0:T(8,128)(2,1)S(1)} %broadcast_select_fusion.1), channel_id=1, source_target_pairs={{0,16},{1,17},{2,18},{3,19},{4,20},{5,21},{6,22},{7,23},{8,24},{9,... | collective-permute-start | bytes 393224 | tf_op jit(solution)/shard_map/ppermute | solution.py:474
  111.6 2.7 %collective-permute-start.5 = (bf16[8,128,512]{2,1,0:T(8,128)(2,1)S(1)}, bf16[8,128,512]{2,1,0:T(8,128)(2,1)S(1)}, u32[]{:S(2)}, u32[]{:S(2)}) collective-permute-start(bf16[8,128,512]{2,1,0:T(8,128)(2,1)S(1)} %collective-permute-done.4.bv_r.refs_4_), channel_id=1, source_target_pairs={{0,192},{4,196},{8,200},{12,204},{16,208},{20,212},{24,216},{28,22... | collective-permute-start | bytes 3145736 | tf_op jit(solution)/shard_map/ppermute | solution.py:506
  114.4 9.6 %collective-permute-done.27.refs_7_ = bf16[8,128,512]{2,1,0:T(8,128)(2,1)S(1)} collective-permute-done((bf16[8,128,512]{2,1,0:T(8,128)(2,1)}, bf16[8,128,512]{2,1,0:T(8,128)(2,1)S(1)}, u32[]{:S(2)}, u32[]{:S(2)}) %collective-permute-start.27) | collective-permute-done | bytes 1048608 | tf_op jit(solution)/shard_map/ppermute | solution.py:503
  124.6 4.7 %collective-permute-done.13 = bf16[2,64,512]{2,1,0:T(8,128)(2,1)S(1)} collective-permute-done((bf16[2,64,512]{2,1,0:T(8,128)(2,1)S(1)}, bf16[2,64,512]{2,1,0:T(8,128)(2,1)S(1)}, u32[]{:S(2)}, u32[]{:S(2)}) %collective-permute-start.13) | collective-permute-done | bytes 131104 | tf_op jit(solution)/shard_map/ppermute | solution.py:474
  130.8 5.2 %collective-permute-start.16 = (bf16[2,64,512]{2,1,0:T(8,128)(2,1)S(1)}, bf16[2,64,512]{2,1,0:T(8,128)(2,1)}, u32[]{:S(2)}, u32[]{:S(2)}) collective-permute-start(bf16[2,64,512]{2,1,0:T(8,128)(2,1)S(1)} %broadcast_select_fusion.3.refs_0_), channel_id=1, source_target_pairs={{0,3},{1,2},{2,1},{3,0},{4,7},{5,6},{6,5},{7,4},{8,11},{9,10},{10,... | collective-permute-start | bytes 393224 | tf_op jit(solution)/shard_map/ppermute | solution.py:474
  136.7 4.2 %collective-permute-done.18.refs_5_ = bf16[6,128,512]{2,1,0:T(8,128)(2,1)} collective-permute-done((bf16[6,128,512]{2,1,0:T(8,128)(2,1)}, bf16[6,128,512]{2,1,0:T(8,128)(2,1)}, u32[]{:S(2)}, u32[]{:S(2)}) %collective-permute-start.18) | collective-permute-done | bytes 786464 | tf_op jit(solution)/shard_map/ppermute | solution.py:503
  140.9 3.7 %collective-permute-start.15 = (bf16[2,64,512]{2,1,0:T(8,128)(2,1)S(1)}, bf16[2,64,512]{2,1,0:T(8,128)(2,1)S(1)}, u32[]{:S(2)}, u32[]{:S(2)}) collective-permute-start(bf16[2,64,512]{2,1,0:T(8,128)(2,1)S(1)} %broadcast_select_fusion.3.refs_0_), channel_id=1, source_target_pairs={{0,2},{1,3},{2,0},{3,1},{4,6},{5,7},{6,4},{7,5},{8,10},{9,11},{10,... | collective-permute-start | bytes 393224 | tf_op jit(solution)/shard_map/ppermute | solution.py:474
  144.7 2.3 %collective-permute-start.14 = (bf16[2,64,512]{2,1,0:T(8,128)(2,1)S(1)}, bf16[2,64,512]{2,1,0:T(8,128)(2,1)S(1)}, u32[]{:S(2)}, u32[]{:S(2)}) collective-permute-start(bf16[2,64,512]{2,1,0:T(8,128)(2,1)S(1)} %broadcast_select_fusion.3.refs_0_), channel_id=1, source_target_pairs={{0,1},{1,0},{2,3},{3,2},{4,5},{5,4},{6,7},{7,6},{8,9},{9,8},{10,11... | collective-permute-start | bytes 393224 | tf_op jit(solution)/shard_map/ppermute | solution.py:474
  148.9 18.2 %near.1 = (f32[16,4,128,128]{3,2,1,0:T(8,128)S(1)}, f32[16,4,128,128]{3,2,1,0:T(8,128)S(1)}, f32[16,4,128,128]{3,2,1,0:T(8,128)S(1)}) custom-call(s32[2]{0:T(128)S(1)} %copy-done.14, s32[16,3]{1,0:T(8,128)S(1)} %copy.10.picks, s32[4]{0:T(128)S(1)} %copy-done.15, bf16[2048,512]{1,0:T(8,128)(2,1)} %q_ref.3, bf16[2048,512]{1,0:T(8,128)(2,1)} %keys.1, ...), custom_call_target="tpu_custom_call" | custom-call | flops 2684354560 | bytes 27262976 | tf_op jit(solution)/shard_map/near/pallas_call | solution.py:234
  167.1 12.0 %score.1 = (bf16[16,4,128,128]{3,2,1,0:T(8,128)(2,1)S(1)}, f32[16,4,128,128]{3,2,1,0:T(8,128)S(1)}, f32[16,4,128,128]{3,2,1,0:T(8,128)S(1)}) custom-call(s32[2]{0:T(128)S(1)} %copy-done.14, s32[16,3]{1,0:T(8,128)S(1)} %copy.10.picks, s32[4]{0:T(128)S(1)} %copy-done.15, ...), custom_call_target="tpu_custom_call", output_to_operand_aliasing={{1}: (12, {}), {2}: (13, {})} | custom-call | flops 1342177280 | bytes 29360128 | tf_op jit(solution)/shard_map/score/pallas_call | solution.py:312
  179.1 5.3 %last.1 = bf16[2048,512]{1,0:T(8,128)(2,1)} custom-call(s32[2]{0:T(128)S(1)} %copy-done.14, s32[16,3]{1,0:T(8,128)S(1)} %copy.10.picks, bf16[2,2,128,512]{3,2,1,0:T(8,128)(2,1)S(1)} %copy-done.6, bf16[6,128,512]{2,1,0:T(8,128)(2,1)} %collective-permute-done.3.a_v, bf16[8,128,512]{2,1,0:T(8,128)(2,1)S(1)} %collective-permute-done.5.b_v, ...), custom_call_target="tpu_custom_call" | custom-call | flops 268435456 | bytes 10485760 | tf_op jit(solution)/shard_map/last/pallas_call | solution.py:374
  (94 shorter events, 29.0 us)
Async XLA Ops:
  2.8 13.0 %collective-permute-start = (bf16[2,2,128,512]{3,2,1,0:T(8,128)(2,1)}, bf16[2,2,128,512]{3,2,1,0:T(8,128)(2,1)S(1)}, u32[]{:S(2)}, u32[]{:S(2)}) collective-permute-start(bf16[2,2,128,512]{3,2,1,0:T(8,128)(2,1)} %pack.3.g), channel_id=1, source_target_pairs={{0,64},{4,68},{8,72},{12,76},{16,80},{20,84},{24,88},{28,92},{32,9... | collective-permute-start | bytes 1572872 | tf_op jit(solution)/shard_map/ppermute | solution.py:503
  4.9 13.4 %collective-permute-start.6 = (bf16[2,2,128,512]{3,2,1,0:T(8,128)(2,1)}, bf16[2,2,128,512]{3,2,1,0:T(8,128)(2,1)S(1)}, u32[]{:S(2)}, u32[]{:S(2)}) collective-permute-start(bf16[2,2,128,512]{3,2,1,0:T(8,128)(2,1)} %pack.3.g), channel_id=1, source_target_pairs={{0,192},{4,196},{8,200},{12,204},{16,208},{20,212},{24,216},{28,22... | collective-permute-start | bytes 1572872 | tf_op jit(solution)/shard_map/ppermute | solution.py:506
  9.5 49.2 %collective-permute-start.26 = (bf16[6,128,512]{2,1,0:T(8,128)(2,1)}, bf16[6,128,512]{2,1,0:T(8,128)(2,1)}, u32[]{:S(2)}, u32[]{:S(2)}) collective-permute-start(bf16[6,128,512]{2,1,0:T(8,128)(2,1)} %get-tuple-element.23), channel_id=1, source_target_pairs={{0,192},{4,196},{8,200},{12,204},{16,208},{20,212},{24,216},{28,22... | collective-permute-start | bytes 2359304 | tf_op jit(solution)/shard_map/ppermute | solution.py:506
  15.8 12.6 %collective-permute-start.1 = (bf16[2,2,128,512]{3,2,1,0:T(8,128)(2,1)S(1)}, bf16[2,2,128,512]{3,2,1,0:T(8,128)(2,1)S(1)}, u32[]{:S(2)}, u32[]{:S(2)}) collective-permute-start(bf16[2,2,128,512]{3,2,1,0:T(8,128)(2,1)S(1)} %collective-permute-done.g_l.refs_5_), channel_id=1, source_target_pairs={{0,64},{4,68},{8,72},{12,76},{16,80},{20,84},{24,88},{28,92},{32,9... | collective-permute-start | bytes 1572872 | tf_op jit(solution)/shard_map/ppermute | solution.py:503
  31.9 9.4 %collective-permute-start.7 = (bf16[2,64,512]{2,1,0:T(8,128)(2,1)}, bf16[2,64,512]{2,1,0:T(8,128)(2,1)S(1)}, u32[]{:S(2)}, u32[]{:S(2)}) collective-permute-start(bf16[2,64,512]{2,1,0:T(8,128)(2,1)} %get-tuple-element.25), channel_id=1, source_target_pairs={{0,3},{1,2},{2,1},{3,0},{4,7},{5,6},{6,5},{7,4},{8,11},{9,10},{10,... | collective-permute-start | bytes 393224 | tf_op jit(solution)/shard_map/ppermute | solution.py:474
  38.2 23.5 %collective-permute-start.2 = (bf16[6,128,512]{2,1,0:T(8,128)(2,1)}, bf16[6,128,512]{2,1,0:T(8,128)(2,1)}, u32[]{:S(2)}, u32[]{:S(2)}) collective-permute-start(bf16[6,128,512]{2,1,0:T(8,128)(2,1)} %get-tuple-element.23), channel_id=1, source_target_pairs={{0,64},{4,68},{8,72},{12,76},{16,80},{20,84},{24,88},{28,92},{32,9... | collective-permute-start | bytes 2359304 | tf_op jit(solution)/shard_map/ppermute | solution.py:503
  38.2 10.8 %collective-permute-start.21 = (bf16[2,128,512]{2,1,0:T(8,128)(2,1)}, bf16[2,128,512]{2,1,0:T(8,128)(2,1)S(1)}, u32[]{:S(2)}, u32[]{:S(2)}) collective-permute-start(bf16[2,128,512]{2,1,0:T(8,128)(2,1)} %get-tuple-element.31), channel_id=1, source_target_pairs={{0,1},{1,2},{2,3},{3,4},{4,5},{5,6},{6,7},{7,8},{8,9},{9,10},{10,1... | collective-permute-start | bytes 786440 | tf_op jit(solution)/shard_map/ppermute | solution.py:511
  41.3 23.5 %collective-permute-start.25 = (bf16[6,128,512]{2,1,0:T(8,128)(2,1)}, bf16[6,128,512]{2,1,0:T(8,128)(2,1)S(1)}, u32[]{:S(2)}, u32[]{:S(2)}) collective-permute-start(bf16[6,128,512]{2,1,0:T(8,128)(2,1)} %get-tuple-element.29), channel_id=1, source_target_pairs={{0,192},{4,196},{8,200},{12,204},{16,208},{20,212},{24,216},{28,22... | collective-permute-start | bytes 2359304 | tf_op jit(solution)/shard_map/ppermute | solution.py:506
  45.7 12.4 %collective-permute-start.22 = (bf16[2,128,512]{2,1,0:T(8,128)(2,1)}, bf16[2,128,512]{2,1,0:T(8,128)(2,1)S(1)}, u32[]{:S(2)}, u32[]{:S(2)}) collective-permute-start(bf16[2,128,512]{2,1,0:T(8,128)(2,1)} %get-tuple-element.32), channel_id=1, source_target_pairs={{1,0},{2,1},{3,2},{4,3},{5,4},{6,5},{7,6},{8,7},{9,8},{10,9},{11,1... | collective-permute-start | bytes 786440 | tf_op jit(solution)/shard_map/ppermute | solution.py:511
  49.0 12.5 %collective-permute-start.10 = (bf16[2,64,512]{2,1,0:T(8,128)(2,1)S(1)}, bf16[2,64,512]{2,1,0:T(8,128)(2,1)S(1)}, u32[]{:S(2)}, u32[]{:S(2)}) collective-permute-start(bf16[2,64,512]{2,1,0:T(8,128)(2,1)S(1)} %select_select_fusion), channel_id=1, source_target_pairs={{0,4},{1,5},{2,6},{3,7},{4,0},{5,1},{6,2},{7,3},{8,12},{9,13},{10,... | collective-permute-start | bytes 393224 | tf_op jit(solution)/shard_map/ppermute | solution.py:474
  58.8 52.1 %collective-permute-start.28 = (bf16[8,128,512]{2,1,0:T(8,128)(2,1)}, bf16[8,128,512]{2,1,0:T(8,128)(2,1)S(1)}, u32[]{:S(2)}, u32[]{:S(2)}) collective-permute-start(bf16[8,128,512]{2,1,0:T(8,128)(2,1)} %get-tuple-element.24), channel_id=1, source_target_pairs={{0,64},{4,68},{8,72},{12,76},{16,80},{20,84},{24,88},{28,92},{32,9... | collective-permute-start | bytes 3145736 | tf_op jit(solution)/shard_map/ppermute | solution.py:503
  58.8 50.7 %collective-permute-start.4 = (bf16[8,128,512]{2,1,0:T(8,128)(2,1)}, bf16[8,128,512]{2,1,0:T(8,128)(2,1)S(1)}, u32[]{:S(2)}, u32[]{:S(2)}) collective-permute-start(bf16[8,128,512]{2,1,0:T(8,128)(2,1)} %get-tuple-element.24), channel_id=1, source_target_pairs={{0,192},{4,196},{8,200},{12,204},{16,208},{20,212},{24,216},{28,22... | collective-permute-start | bytes 3145736 | tf_op jit(solution)/shard_map/ppermute | solution.py:506
  61.5 46.1 %collective-permute-start.19 = (bf16[8,128,512]{2,1,0:T(8,128)(2,1)}, bf16[8,128,512]{2,1,0:T(8,128)(2,1)S(1)}, u32[]{:S(2)}, u32[]{:S(2)}) collective-permute-start(bf16[8,128,512]{2,1,0:T(8,128)(2,1)} %get-tuple-element.30), channel_id=1, source_target_pairs={{0,192},{4,196},{8,200},{12,204},{16,208},{20,212},{24,216},{28,22... | collective-permute-start | bytes 3145736 | tf_op jit(solution)/shard_map/ppermute | solution.py:506
  64.7 36.9 %collective-permute-start.17 = (bf16[6,128,512]{2,1,0:T(8,128)(2,1)S(1)}, bf16[6,128,512]{2,1,0:T(8,128)(2,1)}, u32[]{:S(2)}, u32[]{:S(2)}) collective-permute-start(bf16[6,128,512]{2,1,0:T(8,128)(2,1)S(1)} %copy-done.20), channel_id=1, source_target_pairs={{0,64},{4,68},{8,72},{12,76},{16,80},{20,84},{24,88},{28,92},{32,9... | collective-permute-start | bytes 2359304 | tf_op jit(solution)/shard_map/ppermute | solution.py:503
  70.6 53.4 %collective-permute-start.27 = (bf16[8,128,512]{2,1,0:T(8,128)(2,1)}, bf16[8,128,512]{2,1,0:T(8,128)(2,1)S(1)}, u32[]{:S(2)}, u32[]{:S(2)}) collective-permute-start(bf16[8,128,512]{2,1,0:T(8,128)(2,1)} %get-tuple-element.30), channel_id=1, source_target_pairs={{0,64},{4,68},{8,72},{12,76},{16,80},{20,84},{24,88},{28,92},{32,9... | collective-permute-start | bytes 3145736 | tf_op jit(solution)/shard_map/ppermute | solution.py:503
  101.6 10.0 %collective-permute-start.12 = (bf16[2,64,512]{2,1,0:T(8,128)(2,1)S(1)}, bf16[2,64,512]{2,1,0:T(8,128)(2,1)S(1)}, u32[]{:S(2)}, u32[]{:S(2)}) collective-permute-start(bf16[2,64,512]{2,1,0:T(8,128)(2,1)S(1)} %broadcast_select_fusion.1), channel_id=1, source_target_pairs={{0,16},{1,17},{2,18},{3,19},{4,20},{5,21},{6,22},{7,23},{8,24},{9,... | collective-permute-start | bytes 393224 | tf_op jit(solution)/shard_map/ppermute | solution.py:474
  107.6 59.5 %collective-permute-start.20 = (bf16[8,128,512]{2,1,0:T(8,128)(2,1)S(1)}, bf16[8,128,512]{2,1,0:T(8,128)(2,1)}, u32[]{:S(2)}, u32[]{:S(2)}) collective-permute-start(bf16[8,128,512]{2,1,0:T(8,128)(2,1)S(1)} %collective-permute-done.19.bk_r.refs_2_), channel_id=1, source_target_pairs={{0,192},{4,196},{8,200},{12,204},{16,208},{20,212},{24,216},{28,22... | collective-permute-start | bytes 3145736 | tf_op jit(solution)/shard_map/ppermute | solution.py:506
  109.5 31.4 %collective-permute-start.18 = (bf16[6,128,512]{2,1,0:T(8,128)(2,1)}, bf16[6,128,512]{2,1,0:T(8,128)(2,1)}, u32[]{:S(2)}, u32[]{:S(2)}) collective-permute-start(bf16[6,128,512]{2,1,0:T(8,128)(2,1)} %collective-permute-done.17.ak_l.refs_6_), channel_id=1, source_target_pairs={{0,64},{4,68},{8,72},{12,76},{16,80},{20,84},{24,88},{28,92},{32,9... | collective-permute-start | bytes 2359304 | tf_op jit(solution)/shard_map/ppermute | solution.py:503
  110.9 13.7 %collective-permute-start.23 = (bf16[2,128,512]{2,1,0:T(8,128)(2,1)S(1)}, bf16[2,128,512]{2,1,0:T(8,128)(2,1)S(1)}, u32[]{:S(2)}, u32[]{:S(2)}) collective-permute-start(bf16[2,128,512]{2,1,0:T(8,128)(2,1)S(1)} %get-tuple-element.33), channel_id=1, source_target_pairs={{63,0},{127,64},{191,128},{255,192}} | collective-permute-start | bytes 786440 | tf_op jit(solution)/shard_map/ppermute | solution.py:511
  111.6 67.5 %collective-permute-start.5 = (bf16[8,128,512]{2,1,0:T(8,128)(2,1)S(1)}, bf16[8,128,512]{2,1,0:T(8,128)(2,1)S(1)}, u32[]{:S(2)}, u32[]{:S(2)}) collective-permute-start(bf16[8,128,512]{2,1,0:T(8,128)(2,1)S(1)} %collective-permute-done.4.bv_r.refs_4_), channel_id=1, source_target_pairs={{0,192},{4,196},{8,200},{12,204},{16,208},{20,212},{24,216},{28,22... | collective-permute-start | bytes 3145736 | tf_op jit(solution)/shard_map/ppermute | solution.py:506
  124.6 54.5 %collective-permute-start.3 = (bf16[6,128,512]{2,1,0:T(8,128)(2,1)}, bf16[6,128,512]{2,1,0:T(8,128)(2,1)}, u32[]{:S(2)}, u32[]{:S(2)}) collective-permute-start(bf16[6,128,512]{2,1,0:T(8,128)(2,1)} %collective-permute-done.2.av_l.refs_8_), channel_id=1, source_target_pairs={{0,64},{4,68},{8,72},{12,76},{16,80},{20,84},{24,88},{28,92},{32,9... | collective-permute-start | bytes 2359304 | tf_op jit(solution)/shard_map/ppermute | solution.py:503
  130.8 13.9 %collective-permute-start.16 = (bf16[2,64,512]{2,1,0:T(8,128)(2,1)S(1)}, bf16[2,64,512]{2,1,0:T(8,128)(2,1)}, u32[]{:S(2)}, u32[]{:S(2)}) collective-permute-start(bf16[2,64,512]{2,1,0:T(8,128)(2,1)S(1)} %broadcast_select_fusion.3.refs_0_), channel_id=1, source_target_pairs={{0,3},{1,2},{2,1},{3,0},{4,7},{5,6},{6,5},{7,4},{8,11},{9,10},{10,... | collective-permute-start | bytes 393224 | tf_op jit(solution)/shard_map/ppermute | solution.py:474
  140.9 26.2 %collective-permute-start.15 = (bf16[2,64,512]{2,1,0:T(8,128)(2,1)S(1)}, bf16[2,64,512]{2,1,0:T(8,128)(2,1)S(1)}, u32[]{:S(2)}, u32[]{:S(2)}) collective-permute-start(bf16[2,64,512]{2,1,0:T(8,128)(2,1)S(1)} %broadcast_select_fusion.3.refs_0_), channel_id=1, source_target_pairs={{0,2},{1,3},{2,0},{3,1},{4,6},{5,7},{6,4},{7,5},{8,10},{9,11},{10,... | collective-permute-start | bytes 393224 | tf_op jit(solution)/shard_map/ppermute | solution.py:474
  144.7 22.4 %collective-permute-start.14 = (bf16[2,64,512]{2,1,0:T(8,128)(2,1)S(1)}, bf16[2,64,512]{2,1,0:T(8,128)(2,1)S(1)}, u32[]{:S(2)}, u32[]{:S(2)}) collective-permute-start(bf16[2,64,512]{2,1,0:T(8,128)(2,1)S(1)} %broadcast_select_fusion.3.refs_0_), channel_id=1, source_target_pairs={{0,1},{1,0},{2,3},{3,2},{4,5},{5,4},{6,7},{7,6},{8,9},{9,8},{10,11... | collective-permute-start | bytes 393224 | tf_op jit(solution)/shard_map/ppermute | solution.py:474
  (26 other events, 669.4 us)

commit v4 on v3

--- a/solution.py
+++ b/solution.py
@@ -16,7 +16,10 @@
 W = H * DH
 SCALE_LOG2 = math.log2(math.e) / math.sqrt(DH)
 G_N, A_N, B_N = 2, 6, 8
-NEAR_VMEM, SCORE_VMEM, LAST_VMEM = 41 << 20, 24 << 20, 12 << 20
+NEAR_VMEM, SCORE_VMEM, LAST_VMEM = 24 << 20, 24 << 20, 12 << 20
+WINDOW_VMEM = 41 << 20
+SMALL_VMEM = 8 << 20
+HIDE = -1e30
 ANY = pl.BlockSpec(memory_space=pl.ANY)
 VM = pl.BlockSpec(memory_space=pltpu.VMEM)
 SM = pl.BlockSpec(memory_space=pltpu.SMEM)
@@ -153,29 +156,80 @@
         at += count
 
 
-def near_kernel(blocks, gids, picks, place, q_ref, keys, values, low, high, first, last, *refs):
-    sides, refs = (refs[:5], refs[5:10]), refs[10:]
-    top_ref, total_ref, acc_ref, qbuf, kbuf, vbuf, buf, sem, pick_sem = refs
-    places = first_two(gids, blocks)
-    copies = [pltpu.make_async_copy(q_ref, qbuf, sem.at[0, 3])]
+def window_kernel(blocks, place, picks, queries, keys, values, low, high, top_ref, total_ref, acc_ref, qbuf, kbuf, vbuf, sem):
+    copies = [pltpu.make_async_copy(queries, qbuf, sem.at[0, 3])]
     for half, (ref, dst) in enumerate(((keys, kbuf), (values, vbuf))):
         copies.append(pltpu.make_async_copy(ref, dst.at[pl.ds(BS, blocks * BS)], sem.at[half, 0]))
+        copies.append(pltpu.make_async_copy(low.at[half], dst.at[pl.ds(0, BS)], sem.at[half, 1]))
+        copies.append(
+            pltpu.make_async_copy(high.at[half], dst.at[pl.ds((blocks + 1) * BS, BS)], sem.at[half, 2])
+        )
     for copy in copies:
         copy.start()
-    halos = (
-        (1, place[3] == 0, first, low, 0),
-        (2, place[3] == 1, last, high, (blocks + 1) * BS),
-    )
-    for n, wraps, there, here, at in halos:
-        for half, dst in enumerate((kbuf, vbuf)):
-
-            @pl.when(wraps)
-            def _(there=there, half=half, dst=dst, at=at, n=n):
-                pltpu.make_async_copy(there.at[half], dst.at[pl.ds(at, BS)], sem.at[half, n]).start()
-
-            @pl.when(jnp.logical_not(wraps))
-            def _(here=here, half=half, dst=dst, at=at, n=n):
-                pltpu.make_async_copy(here.at[half], dst.at[pl.ds(at, BS)], sem.at[half, n]).start()
+    for copy in copies:
+        copy.wait()
+
+    def step(j, carry):
+        rows = pl.ds(pl.multiple_of(j * BS, BS), BS)
+        span = pl.ds(pl.multiple_of(j * BS, BS), 3 * BS)
+        no_low = jnp.where((place[3] == 0) & (j == 0), HIDE, 0.0)
+        no_high = jnp.where((place[3] == 1) & (j == blocks - 1), HIDE, 0.0)
+        q = [qbuf[rows, head(h)] for h in range(H)]
+        k = [kbuf[span, head(h)] for h in range(H)]
+        v = [vbuf[span, head(h)] for h in range(H)]
+        scores = []
+        for h in range(H):
+            s = dot_t(q[h], k[h])
+            scores.append(
+                jnp.concatenate(
+                    [s[:, :BS] + no_low, s[:, BS : 2 * BS], s[:, 2 * BS :] + no_high], axis=1
+                )
+            )
+        tops = [top_of([scores[h]]) for h in range(H)]
+        weights = [weigh(scores[h], tops[h]) for h in range(H)]
+        mixed = [mix(weights[h], v[h]) for h in range(H)]
+        for h in range(H):
+            top_ref[j, h] = tops[h]
+            total_ref[j, h] = mixed[h][:, DH:]
+            acc_ref[j, h] = mixed[h][:, :DH]
+        return carry
+
+    lax.fori_loop(0, blocks, step, 0)
+
+
+def window(place, picks, queries, keys, values, low, high):
+    rows = queries.shape[0]
+    blocks = rows // BS
+    return pl.pallas_call(
+        functools.partial(window_kernel, blocks),
+        out_shape=state_of(blocks),
+        in_specs=[SM, SM] + [ANY] * 5,
+        out_specs=[VM] * 3,
+        scratch_shapes=[
+            pltpu.VMEM((rows, W), keys.dtype),
+            pltpu.VMEM(((blocks + 2) * BS, W), keys.dtype),
+            pltpu.VMEM(((blocks + 2) * BS, W), keys.dtype),
+            pltpu.SemaphoreType.DMA((2, 4)),
+        ],
+        compiler_params=pltpu.CompilerParams(vmem_limit_bytes=WINDOW_VMEM),
+        cost_estimate=pl.CostEstimate(
+            flops=rows * 3 * BS * W * 4, transcendentals=rows * 3 * BS * H, bytes_accessed=20 << 20
+        ),
+        name="window",
+    )(place, picks, queries, keys, values, low, high)
+
+
+def near_kernel(blocks, gids, picks, place, queries, first, last, *refs):
+    sides, refs = (refs[:5], refs[5:10]), refs[10:]
+    top_in, total_in, acc_in, top_ref, total_ref, acc_ref, qbuf, wrap, buf, sem, pick_sem = refs
+    places = first_two(gids, blocks)
+    copies = [
+        pltpu.make_async_copy(queries, qbuf, sem.at[0]),
+        pltpu.make_async_copy(first, wrap.at[0], sem.at[1]),
+        pltpu.make_async_copy(last, wrap.at[1], sem.at[2]),
+    ]
+    for copy in copies:
+        copy.start()
 
     def fetch(j, carry):
         for side, column in ((0, 0), (1, 2)):
@@ -188,68 +242,75 @@
     lax.fori_loop(0, blocks, fetch, 0)
     for copy in copies:
         copy.wait()
-    for n, _, _, here, at in halos:
-        for half, dst in enumerate((kbuf, vbuf)):
-            pltpu.make_async_copy(here.at[half], dst.at[pl.ds(at, BS)], sem.at[half, n]).wait()
+
+    def update(j, keys_of, values_of, source):
+        rows = pl.ds(pl.multiple_of(j * BS, BS), BS)
+        tops_in, totals_in, accs_in = source
+        q = [qbuf[rows, head(h)] for h in range(H)]
+        old_top = [tops_in[j, h] for h in range(H)]
+        old_total = [totals_in[j, h] for h in range(H)]
+        old_acc = [accs_in[j, h] for h in range(H)]
+        scores = [dot_t(q[h], keys_of[h]) for h in range(H)]
+        tops = [top_of([scores[h]], old_top[h]) for h in range(H)]
+        weights = [weigh(scores[h], tops[h]) for h in range(H)]
+        mixed = [mix(weights[h], values_of[h]) for h in range(H)]
+        fades = [jnp.exp2((old_top[h] - tops[h]) * SCALE_LOG2) for h in range(H)]
+        for h in range(H):
+            top_ref[j, h] = tops[h]
+            total_ref[j, h] = mixed[h][:, DH:] + fades[h] * old_total[h]
+            acc_ref[j, h] = mixed[h][:, :DH] + fades[h] * old_acc[h]
 
     def step(j, carry):
-        rows = pl.ds(pl.multiple_of(j * BS, BS), BS)
-        span = pl.ds(pl.multiple_of(j * BS, BS), 3 * BS)
         for half in range(2):
             for side in range(2):
                 pltpu.make_async_copy(
                     sides[side][2].at[0], buf.at[j, half, side], pick_sem.at[j, half, side]
                 ).wait()
-        q = [qbuf[rows, head(h)] for h in range(H)]
-        own_keys = [kbuf[span, head(h)] for h in range(H)]
-        own_values = [vbuf[span, head(h)] for h in range(H)]
-        side_keys, side_values = [
+        keys_of, values_of = [
             [
                 jnp.concatenate([buf[j, half, side, :, head(h)] for side in range(2)], axis=0)
                 for h in range(H)
             ]
             for half in range(2)
         ]
-        own_scores = [dot_t(q[h], own_keys[h]) for h in range(H)]
-        side_scores = [dot_t(q[h], side_keys[h]) for h in range(H)]
-        tops = [top_of([own_scores[h], side_scores[h]]) for h in range(H)]
-        own_weights = [weigh(own_scores[h], tops[h]) for h in range(H)]
-        side_weights = [weigh(side_scores[h], tops[h]) for h in range(H)]
-        mixed = [
-            mix(own_weights[h], own_values[h]) + mix(side_weights[h], side_values[h])
-            for h in range(H)
-        ]
-        for h in range(H):
-            top_ref[j, h] = tops[h]
-            total_ref[j, h] = mixed[h][:, DH:]
-            acc_ref[j, h] = mixed[h][:, :DH]
+        update(j, keys_of, values_of, (top_in, total_in, acc_in))
         return carry
 
     lax.fori_loop(0, blocks, step, 0)
 
-
-def near(gids, picks, place, queries, keys, values, halos, from_right, from_left):
+    @pl.when(place[3] < 2)
+    def _():
+        edge = jnp.where(place[3] == 0, 0, 1)
+        update(
+            jnp.where(place[3] == 0, 0, blocks - 1),
+            [wrap[edge, 0, :, head(h)] for h in range(H)],
+            [wrap[edge, 1, :, head(h)] for h in range(H)],
+            (top_ref, total_ref, acc_ref),
+        )
+
+
+def near(gids, picks, place, queries, first, last, from_right, from_left, state):
     rows = queries.shape[0]
     blocks = rows // BS
     return pl.pallas_call(
         functools.partial(near_kernel, blocks),
         out_shape=state_of(blocks),
-        in_specs=[SM, SM, SM] + [ANY] * 17,
+        in_specs=[SM, SM, SM] + [ANY] * 13 + [VM] * 3,
         out_specs=[VM] * 3,
+        input_output_aliases={16: 0, 17: 1, 18: 2},
         scratch_shapes=[
-            pltpu.VMEM((rows, W), keys.dtype),
-            pltpu.VMEM(((blocks + 2) * BS, W), keys.dtype),
-            pltpu.VMEM(((blocks + 2) * BS, W), keys.dtype),
-            pltpu.VMEM((blocks, 2, 2, BS, W), keys.dtype),
-            pltpu.SemaphoreType.DMA((2, 4)),
+            pltpu.VMEM((rows, W), queries.dtype),
+            pltpu.VMEM((2, 2, BS, W), queries.dtype),
+            pltpu.VMEM((blocks, 2, 2, BS, W), queries.dtype),
+            pltpu.SemaphoreType.DMA((3,)),
             pltpu.SemaphoreType.DMA((blocks, 2, 2)),
         ],
         compiler_params=pltpu.CompilerParams(vmem_limit_bytes=NEAR_VMEM),
         cost_estimate=pl.CostEstimate(
-            flops=rows * 5 * BS * W * 4, transcendentals=rows * 5 * BS * H, bytes_accessed=26 << 20
+            flops=rows * 2 * BS * W * 4, transcendentals=rows * 2 * BS * H, bytes_accessed=30 << 20
         ),
         name="near",
-    )(gids, picks, place, queries, keys, values, *halos, *from_right, *from_left)
+    )(gids, picks, place, queries, first, last, *from_right, *from_left, *state)
 
 
 def score_kernel(blocks, gids, picks, place, q_ref, *refs):
@@ -422,7 +483,7 @@
         in_specs=[SM, SM] + [ANY] * 4,
         out_specs=[VM] * 4,
         scratch_shapes=[pltpu.SemaphoreType.DMA((2, 4))],
-        compiler_params=pltpu.CompilerParams(vmem_limit_bytes=56 << 20),
+        compiler_params=pltpu.CompilerParams(vmem_limit_bytes=SMALL_VMEM),
         cost_estimate=pl.CostEstimate(flops=0, transcendentals=0, bytes_accessed=1 << 20),
         name="choose",
     )(gids, place, g, g_r, g_o, g_l)
@@ -463,7 +524,7 @@
         in_specs=[SM] + [ANY] * 6,
         out_specs=[VM] * 2,
         scratch_shapes=[pltpu.SemaphoreType.DMA((2, 2))],
-        compiler_params=pltpu.CompilerParams(vmem_limit_bytes=8 << 20),
+        compiler_params=pltpu.CompilerParams(vmem_limit_bytes=SMALL_VMEM),
         cost_estimate=pl.CostEstimate(flops=0, transcendentals=0, bytes_accessed=1 << 20),
         name="ends",
     )(gids, g_l, ak_l, av_l, g_r, bk_r, bv_r)
@@ -478,15 +539,20 @@
     return jnp.where(mask[:, None, None], a, b)
 
 
-def spread(quarters, me, owners):
+def masks_of(me, owners):
+    differ = (me ^ owners) & 3
+    rows = [differ == n for n in (1, 2, 3)]
+    rows += [((me >> bit) & 1) == ((owners >> bit) & 1) for bit in (2, 3, 4, 5)]
+    return jnp.stack(rows).astype(jnp.int32)
+
+
+def spread(quarters, masks):
     value = quarters[0]
-    differ = (me ^ owners) & 3
     given = [swap(quarters[n], n) for n in (1, 2, 3)]
     for n in (1, 2, 3):
-        value = pick_slots(differ == n, given[n - 1], value)
+        value = pick_slots(masks[n - 1] == 1, given[n - 1], value)
     for bit in (2, 3, 4, 5):
-        same = ((me >> bit) & 1) == ((owners >> bit) & 1)
-        value = pick_slots(same, value, swap(value, 1 << bit))
+        value = pick_slots(masks[bit + 1] == 1, value, swap(value, 1 << bit))
     return [value] + [swap(value, n) for n in (1, 2, 3)]
 
 
@@ -534,22 +600,24 @@
     spot = me % plane
     edge = jnp.where(spot == 0, 0, jnp.where(spot == plane - 1, 1, 2))
     place = jnp.stack([me & 3, distance[0], distance[1], edge])
+    place, masks = lax.optimization_barrier((place, masks_of(me, owners)))
+    state = window(place, rand_pick, queries, keys, values, low, high)
     far_tail, far_lead = ends(global_ids, g_l, ak_l, av_l, g_r, bk_r, bv_r)
     first = along(far_tail, [(plane - 1, 0)])
     final = along(far_lead, [(0, plane - 1)])
     quarters = choose(global_ids, place, g, g_r, g_o, g_l)
-    pieces = spread(quarters, me, owners)
+    pieces = spread(quarters, masks)
 
     state = near(
         global_ids,
         rand_pick,
         place,
         queries,
-        keys,
-        values,
-        (low, high, first, final),
+        first,
+        final,
         (g_r, ak_r, bk_r, av_r, bv_r),
         (g_l, ak_l, bk_l, av_l, bv_l),
+        state,
     )
     weights, share, acc = score(
         global_ids, rand_pick, place, queries, pieces, (g_o, ak_o, bk_o), state

time: 185 us -> 229 us (1.24)
  the two profiles are of different devices: /device:TPU:1 before, /device:TPU:2 now
where the time goes in v4:
time: 229 us; the launch traced here: 225 us
  waiting for transfers between devices  100 us (44%)
  Pallas kernels  59.6 us (26%)
  starting transfers between devices  51.1 us (22%)
  local copies, waits for them, and re-layouts  12.6 us (6%)
    ppermute x7, waiting for transfers between devices, to_left(): return lax.ppermute(v, 'blk', left)  48.1 us
    ppermute x8, waiting for transfers between devices, to_right(): return lax.ppermute(v, 'blk', right)  36.3 us
    ppermute x10, starting transfers between devices, swap(): return lax.ppermute(value, ALL, [(i, i ^ bits) for i in range(count)])  16.8 us
    pallas_call x1, Pallas kernels, near(): pl.pallas_call(functools.partial(near_kernel, blocks), out_shape=state_of...  16.2 us
    ppermute x7, starting transfers between devices, to_left(): return lax.ppermute(v, 'blk', left)  13.2 us
    pallas_call x1, Pallas kernels, window(): pl.pallas_call(functools.partial(window_kernel, blocks), out_shape=state_...  13.1 us
    unnamed x53, local copies, waits for them, and re-layouts  12.6 us
    ppermute x8, starting transfers between devices, to_right(): return lax.ppermute(v, 'blk', right)  12.1 us
  transfers between devices with their start and end apart: 29, of which 11 were waited for; matrix products, arithmetic and copies ran while one was open for 0% of the time, Pallas kernels for 23%

profile of v4, /device:TPU:2, one launch (start us, length us, event | category | flops | bytes accessed | tf_op | source)
XLA Modules:
  0.0 224.7 jit_solution(17392355791875598398)
XLA Ops:
  0.0 2.8 %pack.3.g = bf16[2,2,128,512]{3,2,1,0:T(8,128)(2,1)} custom-call(s32[2]{0:T(128)} %gids.15, bf16[16,128,512]{2,1,0:T(8,128)(2,1)} %bitcast.32, bf16[16,128,512]{2,1,0:T(8,128)(2,1)} %bitcast.35), custom_call_target="tpu_custom_call" | custom-call | bytes 1048576 | tf_op jit(solution)/shard_map/pack/pallas_call | solution.py:88
  5.2 3.3 %pack.4 = (bf16[6,128,512]{2,1,0:T(8,128)(2,1)}, bf16[6,128,512]{2,1,0:T(8,128)(2,1)}, bf16[2,128,512]{2,1,0:T(8,128)(2,1)}, bf16[2,128,512]{2,1,0:T(8,128)(2,1)}) custom-call(s32[2]{0:T(128)} %gids.15, bf16[16,128,512]{2,1,0:T(8,128)(2,1)} %bitcast.33, bf16[16,128,512]{2,1,0:T(8,128)(2,1)} %bitcast.36), custom_call_target="tpu_custom_call" | custom-call | bytes 4194304 | tf_op jit(solution)/shard_map/pack/pallas_call | solution.py:88
  9.8 8.3 %collective-permute-done.g_l.refs_5_ = bf16[2,2,128,512]{3,2,1,0:T(8,128)(2,1)S(1)} collective-permute-done((bf16[2,2,128,512]{3,2,1,0:T(8,128)(2,1)}, bf16[2,2,128,512]{3,2,1,0:T(8,128)(2,1)S(1)}, u32[]{:S(2)}, u32[]{:S(2)}) %collective-permute-start) | collective-permute-done | bytes 524320 | tf_op jit(solution)/shard_map/ppermute | solution.py:569
  19.5 25.3 %collective-permute-done.1.g_o.refs_4_.g = bf16[2,2,128,512]{3,2,1,0:T(8,128)(2,1)S(1)} collective-permute-done((bf16[2,2,128,512]{3,2,1,0:T(8,128)(2,1)S(1)}, bf16[2,2,128,512]{3,2,1,0:T(8,128)(2,1)S(1)}, u32[]{:S(2)}, u32[]{:S(2)}) %collective-permute-start.1) | collective-permute-done | bytes 524320 | tf_op jit(solution)/shard_map/ppermute | solution.py:569
  57.7 2.8 %collective-permute-start.10 = (bf16[2,64,512]{2,1,0:T(8,128)(2,1)S(1)}, bf16[2,64,512]{2,1,0:T(8,128)(2,1)S(1)}, u32[]{:S(2)}, u32[]{:S(2)}) collective-permute-start(bf16[2,64,512]{2,1,0:T(8,128)(2,1)S(1)} %select_select_fusion), channel_id=1, source_target_pairs={{0,4},{1,5},{2,6},{3,7},{4,0},{5,1},{6,2},{7,3},{8,12},{9,13},{10,... | collective-permute-start | bytes 393224 | tf_op jit(solution)/shard_map/ppermute | solution.py:535
  60.5 3.3 %pack.5 = (bf16[8,128,512]{2,1,0:T(8,128)(2,1)}, bf16[8,128,512]{2,1,0:T(8,128)(2,1)}) custom-call(s32[2]{0:T(128)} %gids.15, bf16[16,128,512]{2,1,0:T(8,128)(2,1)} %bitcast.34, bf16[16,128,512]{2,1,0:T(8,128)(2,1)} %bitcast.37), custom_call_target="tpu_custom_call" | custom-call | bytes 4194304 | tf_op jit(solution)/shard_map/pack/pallas_call | solution.py:88
  65.4 2.7 %collective-permute-start.25 = (bf16[8,128,512]{2,1,0:T(8,128)(2,1)}, bf16[8,128,512]{2,1,0:T(8,128)(2,1)S(1)}, u32[]{:S(2)}, u32[]{:S(2)}) collective-permute-start(bf16[8,128,512]{2,1,0:T(8,128)(2,1)} %get-tuple-element.37), channel_id=1, source_target_pairs={{0,64},{4,68},{8,72},{12,76},{16,80},{20,84},{24,88},{28,92},{32,9... | collective-permute-start | bytes 3145736 | tf_op jit(solution)/shard_map/ppermute | solution.py:569
  70.0 2.7 %collective-permute-done.2.av_l.refs_8_ = bf16[6,128,512]{2,1,0:T(8,128)(2,1)} collective-permute-done((bf16[6,128,512]{2,1,0:T(8,128)(2,1)}, bf16[6,128,512]{2,1,0:T(8,128)(2,1)}, u32[]{:S(2)}, u32[]{:S(2)}) %collective-permute-start.2) | collective-permute-done | bytes 786464 | tf_op jit(solution)/shard_map/ppermute | solution.py:569
  72.7 3.1 %collective-permute-start.11 = (bf16[2,64,512]{2,1,0:T(8,128)(2,1)S(1)}, bf16[2,64,512]{2,1,0:T(8,128)(2,1)S(1)}, u32[]{:S(2)}, u32[]{:S(2)}) collective-permute-start(bf16[2,64,512]{2,1,0:T(8,128)(2,1)S(1)} %broadcast_select_fusion), channel_id=1, source_target_pairs={{0,8},{1,9},{2,10},{3,11},{4,12},{5,13},{6,14},{7,15},{8,0},{9,1},... | collective-permute-start | bytes 393224 | tf_op jit(solution)/shard_map/ppermute | solution.py:535
  75.8 3.1 %collective-permute-start.24 = (bf16[6,128,512]{2,1,0:T(8,128)(2,1)S(1)}, bf16[6,128,512]{2,1,0:T(8,128)(2,1)S(1)}, u32[]{:S(2)}, u32[]{:S(2)}) collective-permute-start(bf16[6,128,512]{2,1,0:T(8,128)(2,1)S(1)} %copy-done.25), channel_id=1, source_target_pairs={{0,192},{4,196},{8,200},{12,204},{16,208},{20,212},{24,216},{28,22... | collective-permute-start | bytes 2359304 | tf_op jit(solution)/shard_map/ppermute | solution.py:572
  78.8 2.5 %collective-permute-done.11 = bf16[2,64,512]{2,1,0:T(8,128)(2,1)S(1)} collective-permute-done((bf16[2,64,512]{2,1,0:T(8,128)(2,1)S(1)}, bf16[2,64,512]{2,1,0:T(8,128)(2,1)S(1)}, u32[]{:S(2)}, u32[]{:S(2)}) %collective-permute-start.11) | collective-permute-done | bytes 131104 | tf_op jit(solution)/shard_map/ppermute | solution.py:535
  83.0 48.1 %collective-permute-done.24.refs_3_ = bf16[6,128,512]{2,1,0:T(8,128)(2,1)S(1)} collective-permute-done((bf16[6,128,512]{2,1,0:T(8,128)(2,1)S(1)}, bf16[6,128,512]{2,1,0:T(8,128)(2,1)S(1)}, u32[]{:S(2)}, u32[]{:S(2)}) %collective-permute-start.24) | collective-permute-done | bytes 786464 | tf_op jit(solution)/shard_map/ppermute | solution.py:572
  132.0 6.3 %collective-permute-start.12 = (bf16[2,64,512]{2,1,0:T(8,128)(2,1)S(1)}, bf16[2,64,512]{2,1,0:T(8,128)(2,1)S(1)}, u32[]{:S(2)}, u32[]{:S(2)}) collective-permute-start(bf16[2,64,512]{2,1,0:T(8,128)(2,1)S(1)} %broadcast_select_fusion.1), channel_id=1, source_target_pairs={{0,16},{1,17},{2,18},{3,19},{4,20},{5,21},{6,22},{7,23},{8,24},{9,... | collective-permute-start | bytes 393224 | tf_op jit(solution)/shard_map/ppermute | solution.py:535
  144.7 2.8 %collective-permute-start.5 = (bf16[8,128,512]{2,1,0:T(8,128)(2,1)}, bf16[8,128,512]{2,1,0:T(8,128)(2,1)}, u32[]{:S(2)}, u32[]{:S(2)}) collective-permute-start(bf16[8,128,512]{2,1,0:T(8,128)(2,1)} %collective-permute-done.4.bv_r.refs_4_), channel_id=1, source_target_pairs={{0,192},{4,196},{8,200},{12,204},{16,208},{20,212},{24,216},{28,22... | collective-permute-start | bytes 3145736 | tf_op jit(solution)/shard_map/ppermute | solution.py:572
  148.6 2.3 %collective-permute-start.13 = (bf16[2,64,512]{2,1,0:T(8,128)(2,1)S(1)}, bf16[2,64,512]{2,1,0:T(8,128)(2,1)S(1)}, u32[]{:S(2)}, u32[]{:S(2)}) collective-permute-start(bf16[2,64,512]{2,1,0:T(8,128)(2,1)S(1)} %broadcast_select_fusion.2), channel_id=1, source_target_pairs={{0,32},{1,33},{2,34},{3,35},{4,36},{5,37},{6,38},{7,39},{8,40},{9,... | collective-permute-start | bytes 393224 | tf_op jit(solution)/shard_map/ppermute | solution.py:535
  150.9 4.9 %collective-permute-done.21.first = bf16[2,128,512]{2,1,0:T(8,128)(2,1)S(1)} collective-permute-done((bf16[2,128,512]{2,1,0:T(8,128)(2,1)S(1)}, bf16[2,128,512]{2,1,0:T(8,128)(2,1)S(1)}, u32[]{:S(2)}, u32[]{:S(2)}) %collective-permute-start.21) | collective-permute-done | bytes 262176 | tf_op jit(solution)/shard_map/ppermute | solution.py:577
  157.3 4.6 %collective-permute-start.22 = (bf16[2,128,512]{2,1,0:T(8,128)(2,1)S(1)}, bf16[2,128,512]{2,1,0:T(8,128)(2,1)S(1)}, u32[]{:S(2)}, u32[]{:S(2)}) collective-permute-start(bf16[2,128,512]{2,1,0:T(8,128)(2,1)S(1)} %get-tuple-element.39), channel_id=1, source_target_pairs={{0,63},{64,127},{128,191},{192,255}} | collective-permute-start | bytes 786440 | tf_op jit(solution)/shard_map/ppermute | solution.py:577
  162.0 3.8 %collective-permute-done.22.last = bf16[2,128,512]{2,1,0:T(8,128)(2,1)S(1)} collective-permute-done((bf16[2,128,512]{2,1,0:T(8,128)(2,1)S(1)}, bf16[2,128,512]{2,1,0:T(8,128)(2,1)S(1)}, u32[]{:S(2)}, u32[]{:S(2)}) %collective-permute-start.22) | collective-permute-done | bytes 262176 | tf_op jit(solution)/shard_map/ppermute | solution.py:577
  171.2 13.1 %window.1 = (f32[16,4,128,128]{3,2,1,0:T(8,128)S(1)}, f32[16,4,128,128]{3,2,1,0:T(8,128)S(1)}, f32[16,4,128,128]{3,2,1,0:T(8,128)S(1)}) custom-call(s32[4]{0:T(128)S(1)} %copy-done.23, s32[16,3]{1,0:T(8,128)S(1)} %copy.14.picks, bf16[2048,512]{1,0:T(8,128)(2,1)} %q_ref.1, bf16[2048,512]{1,0:T(8,128)(2,1)} %keys.1, bf16[2048,512]{1,0:T(8,128)(2,1)} %values.1, ...), custom_call_target="tpu_custom_call" | custom-call | flops 1610612736 | bytes 20971520 | tf_op jit(solution)/shard_map/window/pallas_call | solution.py:203
  184.3 2.0 copy-done.1
  186.3 2.2 copy-done.2
  190.6 16.2 %near.1 = (f32[16,4,128,128]{3,2,1,0:T(8,128)S(1)}, f32[16,4,128,128]{3,2,1,0:T(8,128)S(1)}, f32[16,4,128,128]{3,2,1,0:T(8,128)S(1)}) custom-call(s32[2]{0:T(128)S(1)} %copy-done.21, s32[16,3]{1,0:T(8,128)S(1)} %copy.14.picks, s32[4]{0:T(128)S(1)} %copy-done.23, ...), custom_call_target="tpu_custom_call", output_to_operand_aliasing={{0}: (16, {}), {1}: (17, {}), {2}: (18, {})} | custom-call | flops 1073741824 | bytes 31457280 | tf_op jit(solution)/shard_map/near/pallas_call | solution.py:295
  206.8 12.0 %score.1 = (bf16[16,4,128,128]{3,2,1,0:T(8,128)(2,1)S(1)}, f32[16,4,128,128]{3,2,1,0:T(8,128)S(1)}, f32[16,4,128,128]{3,2,1,0:T(8,128)S(1)}) custom-call(s32[2]{0:T(128)S(1)} %copy-done.21, s32[16,3]{1,0:T(8,128)S(1)} %copy.14.picks, s32[4]{0:T(128)S(1)} %copy-done.23, ...), custom_call_target="tpu_custom_call", output_to_operand_aliasing={{1}: (12, {}), {2}: (13, {})} | custom-call | flops 1342177280 | bytes 29360128 | tf_op jit(solution)/shard_map/score/pallas_call | solution.py:373
  218.9 5.6 %last.1 = bf16[2048,512]{1,0:T(8,128)(2,1)} custom-call(s32[2]{0:T(128)S(1)} %copy-done.21, s32[16,3]{1,0:T(8,128)S(1)} %copy.14.picks, bf16[2,2,128,512]{3,2,1,0:T(8,128)(2,1)S(1)} %copy-done.4, bf16[6,128,512]{2,1,0:T(8,128)(2,1)} %collective-permute-done.3.a_v, bf16[8,128,512]{2,1,0:T(8,128)(2,1)} %collective-permute-done.5.b_v, ...), custom_call_target="tpu_custom_call" | custom-call | flops 268435456 | bytes 10485760 | tf_op jit(solution)/shard_map/last/pallas_call | solution.py:435
  (108 shorter events, 40.6 us)
Async XLA Ops:
  2.8 15.3 %collective-permute-start = (bf16[2,2,128,512]{3,2,1,0:T(8,128)(2,1)}, bf16[2,2,128,512]{3,2,1,0:T(8,128)(2,1)S(1)}, u32[]{:S(2)}, u32[]{:S(2)}) collective-permute-start(bf16[2,2,128,512]{3,2,1,0:T(8,128)(2,1)} %pack.3.g), channel_id=1, source_target_pairs={{0,64},{4,68},{8,72},{12,76},{16,80},{20,84},{24,88},{28,92},{32,9... | collective-permute-start | bytes 1572872 | tf_op jit(solution)/shard_map/ppermute | solution.py:569
  4.3 15.2 %collective-permute-start.6 = (bf16[2,2,128,512]{3,2,1,0:T(8,128)(2,1)}, bf16[2,2,128,512]{3,2,1,0:T(8,128)(2,1)S(1)}, u32[]{:S(2)}, u32[]{:S(2)}) collective-permute-start(bf16[2,2,128,512]{3,2,1,0:T(8,128)(2,1)} %pack.3.g), channel_id=1, source_target_pairs={{0,192},{4,196},{8,200},{12,204},{16,208},{20,212},{24,216},{28,22... | collective-permute-start | bytes 1572872 | tf_op jit(solution)/shard_map/ppermute | solution.py:572
  8.5 56.9 %collective-permute-start.17 = (bf16[6,128,512]{2,1,0:T(8,128)(2,1)}, bf16[6,128,512]{2,1,0:T(8,128)(2,1)}, u32[]{:S(2)}, u32[]{:S(2)}) collective-permute-start(bf16[6,128,512]{2,1,0:T(8,128)(2,1)} %get-tuple-element.36), channel_id=1, source_target_pairs={{0,64},{4,68},{8,72},{12,76},{16,80},{20,84},{24,88},{28,92},{32,9... | collective-permute-start | bytes 2359304 | tf_op jit(solution)/shard_map/ppermute | solution.py:569
  18.1 26.7 %collective-permute-start.1 = (bf16[2,2,128,512]{3,2,1,0:T(8,128)(2,1)S(1)}, bf16[2,2,128,512]{3,2,1,0:T(8,128)(2,1)S(1)}, u32[]{:S(2)}, u32[]{:S(2)}) collective-permute-start(bf16[2,2,128,512]{3,2,1,0:T(8,128)(2,1)S(1)} %collective-permute-done.g_l.refs_5_), channel_id=1, source_target_pairs={{0,64},{4,68},{8,72},{12,76},{16,80},{20,84},{24,88},{28,92},{32,9... | collective-permute-start | bytes 1572872 | tf_op jit(solution)/shard_map/ppermute | solution.py:569
  46.5 8.4 %collective-permute-start.8 = (bf16[2,64,512]{2,1,0:T(8,128)(2,1)S(1)}, bf16[2,64,512]{2,1,0:T(8,128)(2,1)S(1)}, u32[]{:S(2)}, u32[]{:S(2)}) collective-permute-start(bf16[2,64,512]{2,1,0:T(8,128)(2,1)S(1)} %get-tuple-element.33), channel_id=1, source_target_pairs={{0,2},{1,3},{2,0},{3,1},{4,6},{5,7},{6,4},{7,5},{8,10},{9,11},{10,... | collective-permute-start | bytes 393224 | tf_op jit(solution)/shard_map/ppermute | solution.py:535
  48.0 27.8 %collective-permute-start.23 = (bf16[6,128,512]{2,1,0:T(8,128)(2,1)}, bf16[6,128,512]{2,1,0:T(8,128)(2,1)S(1)}, u32[]{:S(2)}, u32[]{:S(2)}) collective-permute-start(bf16[6,128,512]{2,1,0:T(8,128)(2,1)} %get-tuple-element.36), channel_id=1, source_target_pairs={{0,192},{4,196},{8,200},{12,204},{16,208},{20,212},{24,216},{28,22... | collective-permute-start | bytes 2359304 | tf_op jit(solution)/shard_map/ppermute | solution.py:572
  52.0 20.7 %collective-permute-start.2 = (bf16[6,128,512]{2,1,0:T(8,128)(2,1)}, bf16[6,128,512]{2,1,0:T(8,128)(2,1)}, u32[]{:S(2)}, u32[]{:S(2)}) collective-permute-start(bf16[6,128,512]{2,1,0:T(8,128)(2,1)} %get-tuple-element.28), channel_id=1, source_target_pairs={{0,64},{4,68},{8,72},{12,76},{16,80},{20,84},{24,88},{28,92},{32,9... | collective-permute-start | bytes 2359304 | tf_op jit(solution)/shard_map/ppermute | solution.py:569
  57.7 10.4 %collective-permute-start.10 = (bf16[2,64,512]{2,1,0:T(8,128)(2,1)S(1)}, bf16[2,64,512]{2,1,0:T(8,128)(2,1)S(1)}, u32[]{:S(2)}, u32[]{:S(2)}) collective-permute-start(bf16[2,64,512]{2,1,0:T(8,128)(2,1)S(1)} %select_select_fusion), channel_id=1, source_target_pairs={{0,4},{1,5},{2,6},{3,7},{4,0},{5,1},{6,2},{7,3},{8,12},{9,13},{10,... | collective-permute-start | bytes 393224 | tf_op jit(solution)/shard_map/ppermute | solution.py:535
  63.7 74.5 %collective-permute-start.19 = (bf16[8,128,512]{2,1,0:T(8,128)(2,1)}, bf16[8,128,512]{2,1,0:T(8,128)(2,1)}, u32[]{:S(2)}, u32[]{:S(2)}) collective-permute-start(bf16[8,128,512]{2,1,0:T(8,128)(2,1)} %get-tuple-element.37), channel_id=1, source_target_pairs={{0,192},{4,196},{8,200},{12,204},{16,208},{20,212},{24,216},{28,22... | collective-permute-start | bytes 3145736 | tf_op jit(solution)/shard_map/ppermute | solution.py:572
  65.4 76.8 %collective-permute-start.25 = (bf16[8,128,512]{2,1,0:T(8,128)(2,1)}, bf16[8,128,512]{2,1,0:T(8,128)(2,1)S(1)}, u32[]{:S(2)}, u32[]{:S(2)}) collective-permute-start(bf16[8,128,512]{2,1,0:T(8,128)(2,1)} %get-tuple-element.37), channel_id=1, source_target_pairs={{0,64},{4,68},{8,72},{12,76},{16,80},{20,84},{24,88},{28,92},{32,9... | collective-permute-start | bytes 3145736 | tf_op jit(solution)/shard_map/ppermute | solution.py:569
  68.1 71.4 %collective-permute-start.4 = (bf16[8,128,512]{2,1,0:T(8,128)(2,1)}, bf16[8,128,512]{2,1,0:T(8,128)(2,1)}, u32[]{:S(2)}, u32[]{:S(2)}) collective-permute-start(bf16[8,128,512]{2,1,0:T(8,128)(2,1)} %get-tuple-element.29), channel_id=1, source_target_pairs={{0,192},{4,196},{8,200},{12,204},{16,208},{20,212},{24,216},{28,22... | collective-permute-start | bytes 3145736 | tf_op jit(solution)/shard_map/ppermute | solution.py:572
  72.7 8.7 %collective-permute-start.11 = (bf16[2,64,512]{2,1,0:T(8,128)(2,1)S(1)}, bf16[2,64,512]{2,1,0:T(8,128)(2,1)S(1)}, u32[]{:S(2)}, u32[]{:S(2)}) collective-permute-start(bf16[2,64,512]{2,1,0:T(8,128)(2,1)S(1)} %broadcast_select_fusion), channel_id=1, source_target_pairs={{0,8},{1,9},{2,10},{3,11},{4,12},{5,13},{6,14},{7,15},{8,0},{9,1},... | collective-permute-start | bytes 393224 | tf_op jit(solution)/shard_map/ppermute | solution.py:535
  75.8 55.3 %collective-permute-start.24 = (bf16[6,128,512]{2,1,0:T(8,128)(2,1)S(1)}, bf16[6,128,512]{2,1,0:T(8,128)(2,1)S(1)}, u32[]{:S(2)}, u32[]{:S(2)}) collective-permute-start(bf16[6,128,512]{2,1,0:T(8,128)(2,1)S(1)} %copy-done.25), channel_id=1, source_target_pairs={{0,192},{4,196},{8,200},{12,204},{16,208},{20,212},{24,216},{28,22... | collective-permute-start | bytes 2359304 | tf_op jit(solution)/shard_map/ppermute | solution.py:572
  81.4 66.2 %collective-permute-start.26 = (bf16[8,128,512]{2,1,0:T(8,128)(2,1)}, bf16[8,128,512]{2,1,0:T(8,128)(2,1)S(1)}, u32[]{:S(2)}, u32[]{:S(2)}) collective-permute-start(bf16[8,128,512]{2,1,0:T(8,128)(2,1)} %get-tuple-element.29), channel_id=1, source_target_pairs={{0,64},{4,68},{8,72},{12,76},{16,80},{20,84},{24,88},{28,92},{32,9... | collective-permute-start | bytes 3145736 | tf_op jit(solution)/shard_map/ppermute | solution.py:569
  132.0 12.7 %collective-permute-start.12 = (bf16[2,64,512]{2,1,0:T(8,128)(2,1)S(1)}, bf16[2,64,512]{2,1,0:T(8,128)(2,1)S(1)}, u32[]{:S(2)}, u32[]{:S(2)}) collective-permute-start(bf16[2,64,512]{2,1,0:T(8,128)(2,1)S(1)} %broadcast_select_fusion.1), channel_id=1, source_target_pairs={{0,16},{1,17},{2,18},{3,19},{4,20},{5,21},{6,22},{7,23},{8,24},{9,... | collective-permute-start | bytes 393224 | tf_op jit(solution)/shard_map/ppermute | solution.py:535
  138.3 68.5 %collective-permute-start.20 = (bf16[8,128,512]{2,1,0:T(8,128)(2,1)}, bf16[8,128,512]{2,1,0:T(8,128)(2,1)}, u32[]{:S(2)}, u32[]{:S(2)}) collective-permute-start(bf16[8,128,512]{2,1,0:T(8,128)(2,1)} %collective-permute-done.19.bk_r.refs_2_), channel_id=1, source_target_pairs={{0,192},{4,196},{8,200},{12,204},{16,208},{20,212},{24,216},{28,22... | collective-permute-start | bytes 3145736 | tf_op jit(solution)/shard_map/ppermute | solution.py:572
  139.5 27.1 %collective-permute-start.18 = (bf16[6,128,512]{2,1,0:T(8,128)(2,1)}, bf16[6,128,512]{2,1,0:T(8,128)(2,1)}, u32[]{:S(2)}, u32[]{:S(2)}) collective-permute-start(bf16[6,128,512]{2,1,0:T(8,128)(2,1)} %collective-permute-done.17.ak_l.refs_6_), channel_id=1, source_target_pairs={{0,64},{4,68},{8,72},{12,76},{16,80},{20,84},{24,88},{28,92},{32,9... | collective-permute-start | bytes 2359304 | tf_op jit(solution)/shard_map/ppermute | solution.py:569
  143.2 12.5 %collective-permute-start.21 = (bf16[2,128,512]{2,1,0:T(8,128)(2,1)S(1)}, bf16[2,128,512]{2,1,0:T(8,128)(2,1)S(1)}, u32[]{:S(2)}, u32[]{:S(2)}) collective-permute-start(bf16[2,128,512]{2,1,0:T(8,128)(2,1)S(1)} %get-tuple-element.38), channel_id=1, source_target_pairs={{63,0},{127,64},{191,128},{255,192}} | collective-permute-start | bytes 786440 | tf_op jit(solution)/shard_map/ppermute | solution.py:577
  144.7 74.2 %collective-permute-start.5 = (bf16[8,128,512]{2,1,0:T(8,128)(2,1)}, bf16[8,128,512]{2,1,0:T(8,128)(2,1)}, u32[]{:S(2)}, u32[]{:S(2)}) collective-permute-start(bf16[8,128,512]{2,1,0:T(8,128)(2,1)} %collective-permute-done.4.bv_r.refs_4_), channel_id=1, source_target_pairs={{0,192},{4,196},{8,200},{12,204},{16,208},{20,212},{24,216},{28,22... | collective-permute-start | bytes 3145736 | tf_op jit(solution)/shard_map/ppermute | solution.py:572
  148.6 8.8 %collective-permute-start.13 = (bf16[2,64,512]{2,1,0:T(8,128)(2,1)S(1)}, bf16[2,64,512]{2,1,0:T(8,128)(2,1)S(1)}, u32[]{:S(2)}, u32[]{:S(2)}) collective-permute-start(bf16[2,64,512]{2,1,0:T(8,128)(2,1)S(1)} %broadcast_select_fusion.2), channel_id=1, source_target_pairs={{0,32},{1,33},{2,34},{3,35},{4,36},{5,37},{6,38},{7,39},{8,40},{9,... | collective-permute-start | bytes 393224 | tf_op jit(solution)/shard_map/ppermute | solution.py:535
  155.7 63.1 %collective-permute-start.3 = (bf16[6,128,512]{2,1,0:T(8,128)(2,1)}, bf16[6,128,512]{2,1,0:T(8,128)(2,1)}, u32[]{:S(2)}, u32[]{:S(2)}) collective-permute-start(bf16[6,128,512]{2,1,0:T(8,128)(2,1)} %collective-permute-done.2.av_l.refs_8_), channel_id=1, source_target_pairs={{0,64},{4,68},{8,72},{12,76},{16,80},{20,84},{24,88},{28,92},{32,9... | collective-permute-start | bytes 2359304 | tf_op jit(solution)/shard_map/ppermute | solution.py:569
  157.3 8.5 %collective-permute-start.22 = (bf16[2,128,512]{2,1,0:T(8,128)(2,1)S(1)}, bf16[2,128,512]{2,1,0:T(8,128)(2,1)S(1)}, u32[]{:S(2)}, u32[]{:S(2)}) collective-permute-start(bf16[2,128,512]{2,1,0:T(8,128)(2,1)S(1)} %get-tuple-element.39), channel_id=1, source_target_pairs={{0,63},{64,127},{128,191},{192,255}} | collective-permute-start | bytes 786440 | tf_op jit(solution)/shard_map/ppermute | solution.py:577
  166.6 40.2 %collective-permute-start.15 = (bf16[2,64,512]{2,1,0:T(8,128)(2,1)S(1)}, bf16[2,64,512]{2,1,0:T(8,128)(2,1)}, u32[]{:S(2)}, u32[]{:S(2)}) collective-permute-start(bf16[2,64,512]{2,1,0:T(8,128)(2,1)S(1)} %broadcast_select_fusion.3.refs_0_), channel_id=1, source_target_pairs={{0,2},{1,3},{2,0},{3,1},{4,6},{5,7},{6,4},{7,5},{8,10},{9,11},{10,... | collective-permute-start | bytes 393224 | tf_op jit(solution)/shard_map/ppermute | solution.py:535
  168.0 38.8 %collective-permute-start.16 = (bf16[2,64,512]{2,1,0:T(8,128)(2,1)S(1)}, bf16[2,64,512]{2,1,0:T(8,128)(2,1)}, u32[]{:S(2)}, u32[]{:S(2)}) collective-permute-start(bf16[2,64,512]{2,1,0:T(8,128)(2,1)S(1)} %broadcast_select_fusion.3.refs_0_), channel_id=1, source_target_pairs={{0,3},{1,2},{2,1},{3,0},{4,7},{5,6},{6,5},{7,4},{8,11},{9,10},{10,... | collective-permute-start | bytes 393224 | tf_op jit(solution)/shard_map/ppermute | solution.py:535
  (31 other events, 984.0 us)

commit v5 on v4

--- a/solution.py
+++ b/solution.py
@@ -81,7 +81,7 @@
 def pack(gids, keys, values, start, count, joined=False, ends=False):
     shapes = [jax.ShapeDtypeStruct((count, BS, W), keys.dtype)] * 2
     if joined:
-        shapes = [jax.ShapeDtypeStruct((2, count, BS, W), keys.dtype)]
+        shapes = [pltpu.VMEM((2, count, BS, W), keys.dtype)]
     if ends:
         shapes += [jax.ShapeDtypeStruct((2, BS, W), keys.dtype)] * 2
     places = count + 2 * ends
@@ -390,43 +390,58 @@
     )(gids, picks, place, queries, *pieces, *opposite, *state)
 
 
-def last_kernel(blocks, gids, picks, g, a_v, b_v, weights, share, acc, out, obuf, out_sem):
+def last_kernel(blocks, gids, picks, g, a_v, b_v, weights, share, acc, out, obuf, order, out_sem):
     places = first_two(gids, blocks)
 
     def store(j):
         rows = pl.ds(pl.multiple_of(j * BS, BS), BS)
         return pltpu.make_async_copy(obuf.at[j], out.at[rows], out_sem.at[j])
 
-    def step(j, carry):
+    def sort(j, counts):
         position = position_of(picks[j, 1], places, blocks)
-
-        def finish(v):
-            mixed = [(dot(weights[j, h], v[:, head(h)]) + acc[j, h]) * share[j, h] for h in range(H)]
-            for h in range(H):
-                obuf[j, :, head(h)] = mixed[h].astype(obuf.dtype)
-
-        @pl.when(position < G_N)
-        def _():
-            finish(g.at[1, jnp.minimum(position, G_N - 1)])
-
-        @pl.when((position >= G_N) & (position < G_N + A_N))
-        def _():
-            finish(a_v.at[jnp.clip(position - G_N, 0, A_N - 1)])
-
-        @pl.when(position >= G_N + A_N)
-        def _():
-            finish(b_v.at[jnp.clip(position - G_N - A_N, 0, B_N - 1)])
-
-        store(j).start()
-        return carry
-
-    lax.fori_loop(0, blocks, step, 0)
+        kind = (position >= G_N).astype(jnp.int32) + (position >= G_N + A_N).astype(jnp.int32)
+        at = jnp.where(kind == 0, counts[0], jnp.where(kind == 1, counts[1], counts[2]))
+        order[kind * blocks + at] = j
+        return tuple(count + (kind == n).astype(jnp.int32) for n, count in enumerate(counts))
+
+    zero = jnp.int32(0)
+    counts = lax.fori_loop(0, blocks, sort, (zero, zero, zero), unroll=True)
+
+    for kind, (values, begin) in enumerate(((g.at[1], 0), (a_v, G_N), (b_v, G_N + A_N))):
+        count = counts[kind]
+
+        def pair(n, carry, kind=kind, values=values, begin=begin, count=count):
+            both = [
+                order[kind * blocks + 2 * n],
+                order[kind * blocks + jnp.minimum(2 * n + 1, count - 1)],
+            ]
+            mixed = []
+            for j in both:
+                at = position_of(picks[j, 1], places, blocks) - begin
+                at = jnp.clip(at, 0, values.shape[0] - 1)
+                mixed.append([dot(weights[j, h], values[at, :, head(h)]) for h in range(H)])
+            done = [
+                [((m + acc[j, h]) * share[j, h]).astype(obuf.dtype) for h, m in enumerate(ms)]
+                for j, ms in zip(both, mixed)
+            ]
+            for j, parts in zip(both, done):
+                for h in range(H):
+                    obuf[j, :, head(h)] = parts[h]
+            store(both[0]).start()
+
+            @pl.when(both[1] != both[0])
+            def _():
+                store(both[1]).start()
+
+            return carry
+
+        lax.fori_loop(0, lax.div(count + 1, 2), pair, 0)
 
     def drain(j, carry):
         store(j).wait()
         return carry
 
-    lax.fori_loop(0, blocks, drain, 0)
+    lax.fori_loop(0, blocks, drain, 0, unroll=True)
 
 
 def last(gids, picks, parts, weights, share, acc, like):
@@ -439,6 +454,7 @@
         out_specs=ANY,
         scratch_shapes=[
             pltpu.VMEM((blocks, BS, W), like.dtype),
+            pltpu.SMEM((3 * blocks,), jnp.int32),
             pltpu.SemaphoreType.DMA((blocks,)),
         ],
         compiler_params=pltpu.CompilerParams(vmem_limit_bytes=LAST_VMEM),

time: 229 us -> 224 us (0.978)
    unnamed x53 -> x51, local copies, waits for them, and re-layouts: 12.6 us -> 11.2 us
where the time goes in v5:
time: 224 us; the launch traced here: 220 us
  waiting for transfers between devices  99.4 us (44%)
  Pallas kernels  57.7 us (26%)
  starting transfers between devices  51 us (23%)
  local copies, waits for them, and re-layouts  11.3 us (5%)
    ppermute x7, waiting for transfers between devices, to_left(): return lax.ppermute(v, 'blk', left)  48.1 us
    ppermute x8, waiting for transfers between devices, to_right(): return lax.ppermute(v, 'blk', right)  36.2 us
    ppermute x10, starting transfers between devices, swap(): return lax.ppermute(value, ALL, [(i, i ^ bits) for i in range(count)])  16.8 us
    pallas_call x1, Pallas kernels, near(): pl.pallas_call(functools.partial(near_kernel, blocks), out_shape=state_of...  16.2 us
    pallas_call x1, Pallas kernels, window(): pl.pallas_call(functools.partial(window_kernel, blocks), out_shape=state_...  13.1 us
    ppermute x7, starting transfers between devices, to_left(): return lax.ppermute(v, 'blk', left)  13.1 us
    ppermute x8, starting transfers between devices, to_right(): return lax.ppermute(v, 'blk', right)  12.1 us
    pallas_call x1, Pallas kernels, score(): pl.pallas_call(functools.partial(score_kernel, blocks), out_shape=[jax.Sh...  12.1 us
  transfers between devices with their start and end apart: 29, of which 11 were waited for; matrix products, arithmetic and copies ran while one was open for 0% of the time, Pallas kernels for 23%

profile of v5, /device:TPU:2, one launch (start us, length us, event | category | flops | bytes accessed | tf_op | source)
XLA Modules:
  0.0 220.5 jit_solution(6597142741597909522)
XLA Ops:
  0.0 2.0 pack.3.g
  4.4 3.2 %pack.4 = (bf16[6,128,512]{2,1,0:T(8,128)(2,1)}, bf16[6,128,512]{2,1,0:T(8,128)(2,1)}, bf16[2,128,512]{2,1,0:T(8,128)(2,1)}, bf16[2,128,512]{2,1,0:T(8,128)(2,1)}) custom-call(s32[2]{0:T(128)} %gids.15, bf16[16,128,512]{2,1,0:T(8,128)(2,1)} %bitcast.33, bf16[16,128,512]{2,1,0:T(8,128)(2,1)} %bitcast.36), custom_call_target="tpu_custom_call" | custom-call | bytes 4194304 | tf_op jit(solution)/shard_map/pack/pallas_call | solution.py:88
  8.9 8.1 %collective-permute-done.g_l.refs_5_ = bf16[2,2,128,512]{3,2,1,0:T(8,128)(2,1)S(1)} collective-permute-done((bf16[2,2,128,512]{3,2,1,0:T(8,128)(2,1)S(1)}, bf16[2,2,128,512]{3,2,1,0:T(8,128)(2,1)S(1)}, u32[]{:S(2)}, u32[]{:S(2)}) %collective-permute-start) | collective-permute-done | bytes 524320 | tf_op jit(solution)/shard_map/ppermute | solution.py:585
  18.5 25.3 %collective-permute-done.1.g_o.refs_4_.g = bf16[2,2,128,512]{3,2,1,0:T(8,128)(2,1)S(1)} collective-permute-done((bf16[2,2,128,512]{3,2,1,0:T(8,128)(2,1)S(1)}, bf16[2,2,128,512]{3,2,1,0:T(8,128)(2,1)S(1)}, u32[]{:S(2)}, u32[]{:S(2)}) %collective-permute-start.1) | collective-permute-done | bytes 524320 | tf_op jit(solution)/shard_map/ppermute | solution.py:585
  56.7 2.8 %collective-permute-start.10 = (bf16[2,64,512]{2,1,0:T(8,128)(2,1)S(1)}, bf16[2,64,512]{2,1,0:T(8,128)(2,1)S(1)}, u32[]{:S(2)}, u32[]{:S(2)}) collective-permute-start(bf16[2,64,512]{2,1,0:T(8,128)(2,1)S(1)} %select_select_fusion), channel_id=1, source_target_pairs={{0,4},{1,5},{2,6},{3,7},{4,0},{5,1},{6,2},{7,3},{8,12},{9,13},{10,... | collective-permute-start | bytes 393224 | tf_op jit(solution)/shard_map/ppermute | solution.py:551
  59.4 3.3 %pack.5 = (bf16[8,128,512]{2,1,0:T(8,128)(2,1)}, bf16[8,128,512]{2,1,0:T(8,128)(2,1)}) custom-call(s32[2]{0:T(128)} %gids.15, bf16[16,128,512]{2,1,0:T(8,128)(2,1)} %bitcast.34, bf16[16,128,512]{2,1,0:T(8,128)(2,1)} %bitcast.37), custom_call_target="tpu_custom_call" | custom-call | bytes 4194304 | tf_op jit(solution)/shard_map/pack/pallas_call | solution.py:88
  64.4 2.7 %collective-permute-start.25 = (bf16[8,128,512]{2,1,0:T(8,128)(2,1)}, bf16[8,128,512]{2,1,0:T(8,128)(2,1)S(1)}, u32[]{:S(2)}, u32[]{:S(2)}) collective-permute-start(bf16[8,128,512]{2,1,0:T(8,128)(2,1)} %get-tuple-element.37), channel_id=1, source_target_pairs={{0,64},{4,68},{8,72},{12,76},{16,80},{20,84},{24,88},{28,92},{32,9... | collective-permute-start | bytes 3145736 | tf_op jit(solution)/shard_map/ppermute | solution.py:585
  69.0 2.7 %collective-permute-done.2.av_l.refs_8_ = bf16[6,128,512]{2,1,0:T(8,128)(2,1)} collective-permute-done((bf16[6,128,512]{2,1,0:T(8,128)(2,1)}, bf16[6,128,512]{2,1,0:T(8,128)(2,1)}, u32[]{:S(2)}, u32[]{:S(2)}) %collective-permute-start.2) | collective-permute-done | bytes 786464 | tf_op jit(solution)/shard_map/ppermute | solution.py:585
  71.7 3.1 %collective-permute-start.11 = (bf16[2,64,512]{2,1,0:T(8,128)(2,1)S(1)}, bf16[2,64,512]{2,1,0:T(8,128)(2,1)S(1)}, u32[]{:S(2)}, u32[]{:S(2)}) collective-permute-start(bf16[2,64,512]{2,1,0:T(8,128)(2,1)S(1)} %broadcast_select_fusion), channel_id=1, source_target_pairs={{0,8},{1,9},{2,10},{3,11},{4,12},{5,13},{6,14},{7,15},{8,0},{9,1},... | collective-permute-start | bytes 393224 | tf_op jit(solution)/shard_map/ppermute | solution.py:551
  75.7 3.0 %collective-permute-start.24 = (bf16[6,128,512]{2,1,0:T(8,128)(2,1)S(1)}, bf16[6,128,512]{2,1,0:T(8,128)(2,1)S(1)}, u32[]{:S(2)}, u32[]{:S(2)}) collective-permute-start(bf16[6,128,512]{2,1,0:T(8,128)(2,1)S(1)} %copy-done.24), channel_id=1, source_target_pairs={{0,192},{4,196},{8,200},{12,204},{16,208},{20,212},{24,216},{28,22... | collective-permute-start | bytes 2359304 | tf_op jit(solution)/shard_map/ppermute | solution.py:588
  81.9 48.1 %collective-permute-done.24.refs_3_ = bf16[6,128,512]{2,1,0:T(8,128)(2,1)S(1)} collective-permute-done((bf16[6,128,512]{2,1,0:T(8,128)(2,1)S(1)}, bf16[6,128,512]{2,1,0:T(8,128)(2,1)S(1)}, u32[]{:S(2)}, u32[]{:S(2)}) %collective-permute-start.24) | collective-permute-done | bytes 786464 | tf_op jit(solution)/shard_map/ppermute | solution.py:588
  131.0 6.3 %collective-permute-start.12 = (bf16[2,64,512]{2,1,0:T(8,128)(2,1)S(1)}, bf16[2,64,512]{2,1,0:T(8,128)(2,1)S(1)}, u32[]{:S(2)}, u32[]{:S(2)}) collective-permute-start(bf16[2,64,512]{2,1,0:T(8,128)(2,1)S(1)} %broadcast_select_fusion.1), channel_id=1, source_target_pairs={{0,16},{1,17},{2,18},{3,19},{4,20},{5,21},{6,22},{7,23},{8,24},{9,... | collective-permute-start | bytes 393224 | tf_op jit(solution)/shard_map/ppermute | solution.py:551
  139.3 1.9 ends.1
  143.7 2.8 %collective-permute-start.5 = (bf16[8,128,512]{2,1,0:T(8,128)(2,1)}, bf16[8,128,512]{2,1,0:T(8,128)(2,1)}, u32[]{:S(2)}, u32[]{:S(2)}) collective-permute-start(bf16[8,128,512]{2,1,0:T(8,128)(2,1)} %collective-permute-done.4.bv_r.refs_4_), channel_id=1, source_target_pairs={{0,192},{4,196},{8,200},{12,204},{16,208},{20,212},{24,216},{28,22... | collective-permute-start | bytes 3145736 | tf_op jit(solution)/shard_map/ppermute | solution.py:588
  147.6 2.3 %collective-permute-start.13 = (bf16[2,64,512]{2,1,0:T(8,128)(2,1)S(1)}, bf16[2,64,512]{2,1,0:T(8,128)(2,1)S(1)}, u32[]{:S(2)}, u32[]{:S(2)}) collective-permute-start(bf16[2,64,512]{2,1,0:T(8,128)(2,1)S(1)} %broadcast_select_fusion.2), channel_id=1, source_target_pairs={{0,32},{1,33},{2,34},{3,35},{4,36},{5,37},{6,38},{7,39},{8,40},{9,... | collective-permute-start | bytes 393224 | tf_op jit(solution)/shard_map/ppermute | solution.py:551
  149.8 4.9 %collective-permute-done.21.first = bf16[2,128,512]{2,1,0:T(8,128)(2,1)S(1)} collective-permute-done((bf16[2,128,512]{2,1,0:T(8,128)(2,1)S(1)}, bf16[2,128,512]{2,1,0:T(8,128)(2,1)S(1)}, u32[]{:S(2)}, u32[]{:S(2)}) %collective-permute-start.21) | collective-permute-done | bytes 262176 | tf_op jit(solution)/shard_map/ppermute | solution.py:593
  156.3 4.6 %collective-permute-start.22 = (bf16[2,128,512]{2,1,0:T(8,128)(2,1)S(1)}, bf16[2,128,512]{2,1,0:T(8,128)(2,1)S(1)}, u32[]{:S(2)}, u32[]{:S(2)}) collective-permute-start(bf16[2,128,512]{2,1,0:T(8,128)(2,1)S(1)} %get-tuple-element.39), channel_id=1, source_target_pairs={{0,63},{64,127},{128,191},{192,255}} | collective-permute-start | bytes 786440 | tf_op jit(solution)/shard_map/ppermute | solution.py:593
  161.0 3.8 %collective-permute-done.22.last = bf16[2,128,512]{2,1,0:T(8,128)(2,1)S(1)} collective-permute-done((bf16[2,128,512]{2,1,0:T(8,128)(2,1)S(1)}, bf16[2,128,512]{2,1,0:T(8,128)(2,1)S(1)}, u32[]{:S(2)}, u32[]{:S(2)}) %collective-permute-start.22) | collective-permute-done | bytes 262176 | tf_op jit(solution)/shard_map/ppermute | solution.py:593
  170.1 13.1 %window.1 = (f32[16,4,128,128]{3,2,1,0:T(8,128)S(1)}, f32[16,4,128,128]{3,2,1,0:T(8,128)S(1)}, f32[16,4,128,128]{3,2,1,0:T(8,128)S(1)}) custom-call(s32[4]{0:T(128)S(1)} %copy-done.22, s32[16,3]{1,0:T(8,128)S(1)} %copy.14.picks, bf16[2048,512]{1,0:T(8,128)(2,1)} %q_ref.1, bf16[2048,512]{1,0:T(8,128)(2,1)} %keys.1, bf16[2048,512]{1,0:T(8,128)(2,1)} %values.1, ...), custom_call_target="tpu_custom_call" | custom-call | flops 1610612736 | bytes 20971520 | tf_op jit(solution)/shard_map/window/pallas_call | solution.py:203
  183.2 2.0 copy-done.1
  185.2 2.2 copy-done.2
  187.4 16.2 %near.1 = (f32[16,4,128,128]{3,2,1,0:T(8,128)S(1)}, f32[16,4,128,128]{3,2,1,0:T(8,128)S(1)}, f32[16,4,128,128]{3,2,1,0:T(8,128)S(1)}) custom-call(s32[2]{0:T(128)S(1)} %copy-done.20, s32[16,3]{1,0:T(8,128)S(1)} %copy.14.picks, s32[4]{0:T(128)S(1)} %copy-done.22, ...), custom_call_target="tpu_custom_call", output_to_operand_aliasing={{0}: (16, {}), {1}: (17, {}), {2}: (18, {})} | custom-call | flops 1073741824 | bytes 31457280 | tf_op jit(solution)/shard_map/near/pallas_call | solution.py:295
  203.6 12.1 %score.1 = (bf16[16,4,128,128]{3,2,1,0:T(8,128)(2,1)S(1)}, f32[16,4,128,128]{3,2,1,0:T(8,128)S(1)}, f32[16,4,128,128]{3,2,1,0:T(8,128)S(1)}) custom-call(s32[2]{0:T(128)S(1)} %copy-done.20, s32[16,3]{1,0:T(8,128)S(1)} %copy.14.picks, s32[4]{0:T(128)S(1)} %copy-done.22, ...), custom_call_target="tpu_custom_call", output_to_operand_aliasing={{1}: (12, {}), {2}: (13, {})} | custom-call | flops 1342177280 | bytes 29360128 | tf_op jit(solution)/shard_map/score/pallas_call | solution.py:373
  215.7 4.6 %last.1 = bf16[2048,512]{1,0:T(8,128)(2,1)} custom-call(s32[2]{0:T(128)S(1)} %copy-done.20, s32[16,3]{1,0:T(8,128)S(1)} %copy.14.picks, bf16[2,2,128,512]{3,2,1,0:T(8,128)(2,1)S(1)} %copy-done.4, bf16[6,128,512]{2,1,0:T(8,128)(2,1)} %collective-permute-done.3.a_v, bf16[8,128,512]{2,1,0:T(8,128)(2,1)} %collective-permute-done.5.b_v, ...), custom_call_target="tpu_custom_call" | custom-call | flops 268435456 | bytes 10485760 | tf_op jit(solution)/shard_map/last/pallas_call | solution.py:450
  (106 shorter events, 39.0 us)
Async XLA Ops:
  2.0 15.1 %collective-permute-start = (bf16[2,2,128,512]{3,2,1,0:T(8,128)(2,1)S(1)}, bf16[2,2,128,512]{3,2,1,0:T(8,128)(2,1)S(1)}, u32[]{:S(2)}, u32[]{:S(2)}) collective-permute-start(bf16[2,2,128,512]{3,2,1,0:T(8,128)(2,1)S(1)} %pack.3.g), channel_id=1, source_target_pairs={{0,64},{4,68},{8,72},{12,76},{16,80},{20,84},{24,88},{28,92},{32,9... | collective-permute-start | bytes 1572872 | tf_op jit(solution)/shard_map/ppermute | solution.py:585
  3.5 15.0 %collective-permute-start.6 = (bf16[2,2,128,512]{3,2,1,0:T(8,128)(2,1)S(1)}, bf16[2,2,128,512]{3,2,1,0:T(8,128)(2,1)S(1)}, u32[]{:S(2)}, u32[]{:S(2)}) collective-permute-start(bf16[2,2,128,512]{3,2,1,0:T(8,128)(2,1)S(1)} %pack.3.g), channel_id=1, source_target_pairs={{0,192},{4,196},{8,200},{12,204},{16,208},{20,212},{24,216},{28,22... | collective-permute-start | bytes 1572872 | tf_op jit(solution)/shard_map/ppermute | solution.py:588
  7.7 56.8 %collective-permute-start.17 = (bf16[6,128,512]{2,1,0:T(8,128)(2,1)}, bf16[6,128,512]{2,1,0:T(8,128)(2,1)}, u32[]{:S(2)}, u32[]{:S(2)}) collective-permute-start(bf16[6,128,512]{2,1,0:T(8,128)(2,1)} %get-tuple-element.36), channel_id=1, source_target_pairs={{0,64},{4,68},{8,72},{12,76},{16,80},{20,84},{24,88},{28,92},{32,9... | collective-permute-start | bytes 2359304 | tf_op jit(solution)/shard_map/ppermute | solution.py:585
  17.1 26.7 %collective-permute-start.1 = (bf16[2,2,128,512]{3,2,1,0:T(8,128)(2,1)S(1)}, bf16[2,2,128,512]{3,2,1,0:T(8,128)(2,1)S(1)}, u32[]{:S(2)}, u32[]{:S(2)}) collective-permute-start(bf16[2,2,128,512]{3,2,1,0:T(8,128)(2,1)S(1)} %collective-permute-done.g_l.refs_5_), channel_id=1, source_target_pairs={{0,64},{4,68},{8,72},{12,76},{16,80},{20,84},{24,88},{28,92},{32,9... | collective-permute-start | bytes 1572872 | tf_op jit(solution)/shard_map/ppermute | solution.py:585
  45.5 8.4 %collective-permute-start.8 = (bf16[2,64,512]{2,1,0:T(8,128)(2,1)S(1)}, bf16[2,64,512]{2,1,0:T(8,128)(2,1)S(1)}, u32[]{:S(2)}, u32[]{:S(2)}) collective-permute-start(bf16[2,64,512]{2,1,0:T(8,128)(2,1)S(1)} %get-tuple-element.33), channel_id=1, source_target_pairs={{0,2},{1,3},{2,0},{3,1},{4,6},{5,7},{6,4},{7,5},{8,10},{9,11},{10,... | collective-permute-start | bytes 393224 | tf_op jit(solution)/shard_map/ppermute | solution.py:551
  47.0 27.8 %collective-permute-start.23 = (bf16[6,128,512]{2,1,0:T(8,128)(2,1)}, bf16[6,128,512]{2,1,0:T(8,128)(2,1)S(1)}, u32[]{:S(2)}, u32[]{:S(2)}) collective-permute-start(bf16[6,128,512]{2,1,0:T(8,128)(2,1)} %get-tuple-element.36), channel_id=1, source_target_pairs={{0,192},{4,196},{8,200},{12,204},{16,208},{20,212},{24,216},{28,22... | collective-permute-start | bytes 2359304 | tf_op jit(solution)/shard_map/ppermute | solution.py:588
  51.0 20.7 %collective-permute-start.2 = (bf16[6,128,512]{2,1,0:T(8,128)(2,1)}, bf16[6,128,512]{2,1,0:T(8,128)(2,1)}, u32[]{:S(2)}, u32[]{:S(2)}) collective-permute-start(bf16[6,128,512]{2,1,0:T(8,128)(2,1)} %get-tuple-element.28), channel_id=1, source_target_pairs={{0,64},{4,68},{8,72},{12,76},{16,80},{20,84},{24,88},{28,92},{32,9... | collective-permute-start | bytes 2359304 | tf_op jit(solution)/shard_map/ppermute | solution.py:585
  56.7 10.4 %collective-permute-start.10 = (bf16[2,64,512]{2,1,0:T(8,128)(2,1)S(1)}, bf16[2,64,512]{2,1,0:T(8,128)(2,1)S(1)}, u32[]{:S(2)}, u32[]{:S(2)}) collective-permute-start(bf16[2,64,512]{2,1,0:T(8,128)(2,1)S(1)} %select_select_fusion), channel_id=1, source_target_pairs={{0,4},{1,5},{2,6},{3,7},{4,0},{5,1},{6,2},{7,3},{8,12},{9,13},{10,... | collective-permute-start | bytes 393224 | tf_op jit(solution)/shard_map/ppermute | solution.py:551
  62.7 74.5 %collective-permute-start.19 = (bf16[8,128,512]{2,1,0:T(8,128)(2,1)}, bf16[8,128,512]{2,1,0:T(8,128)(2,1)}, u32[]{:S(2)}, u32[]{:S(2)}) collective-permute-start(bf16[8,128,512]{2,1,0:T(8,128)(2,1)} %get-tuple-element.37), channel_id=1, source_target_pairs={{0,192},{4,196},{8,200},{12,204},{16,208},{20,212},{24,216},{28,22... | collective-permute-start | bytes 3145736 | tf_op jit(solution)/shard_map/ppermute | solution.py:588
  64.4 76.8 %collective-permute-start.25 = (bf16[8,128,512]{2,1,0:T(8,128)(2,1)}, bf16[8,128,512]{2,1,0:T(8,128)(2,1)S(1)}, u32[]{:S(2)}, u32[]{:S(2)}) collective-permute-start(bf16[8,128,512]{2,1,0:T(8,128)(2,1)} %get-tuple-element.37), channel_id=1, source_target_pairs={{0,64},{4,68},{8,72},{12,76},{16,80},{20,84},{24,88},{28,92},{32,9... | collective-permute-start | bytes 3145736 | tf_op jit(solution)/shard_map/ppermute | solution.py:585
  67.1 71.4 %collective-permute-start.4 = (bf16[8,128,512]{2,1,0:T(8,128)(2,1)}, bf16[8,128,512]{2,1,0:T(8,128)(2,1)}, u32[]{:S(2)}, u32[]{:S(2)}) collective-permute-start(bf16[8,128,512]{2,1,0:T(8,128)(2,1)} %get-tuple-element.29), channel_id=1, source_target_pairs={{0,192},{4,196},{8,200},{12,204},{16,208},{20,212},{24,216},{28,22... | collective-permute-start | bytes 3145736 | tf_op jit(solution)/shard_map/ppermute | solution.py:588
  71.7 8.7 %collective-permute-start.11 = (bf16[2,64,512]{2,1,0:T(8,128)(2,1)S(1)}, bf16[2,64,512]{2,1,0:T(8,128)(2,1)S(1)}, u32[]{:S(2)}, u32[]{:S(2)}) collective-permute-start(bf16[2,64,512]{2,1,0:T(8,128)(2,1)S(1)} %broadcast_select_fusion), channel_id=1, source_target_pairs={{0,8},{1,9},{2,10},{3,11},{4,12},{5,13},{6,14},{7,15},{8,0},{9,1},... | collective-permute-start | bytes 393224 | tf_op jit(solution)/shard_map/ppermute | solution.py:551
  75.7 54.4 %collective-permute-start.24 = (bf16[6,128,512]{2,1,0:T(8,128)(2,1)S(1)}, bf16[6,128,512]{2,1,0:T(8,128)(2,1)S(1)}, u32[]{:S(2)}, u32[]{:S(2)}) collective-permute-start(bf16[6,128,512]{2,1,0:T(8,128)(2,1)S(1)} %copy-done.24), channel_id=1, source_target_pairs={{0,192},{4,196},{8,200},{12,204},{16,208},{20,212},{24,216},{28,22... | collective-permute-start | bytes 2359304 | tf_op jit(solution)/shard_map/ppermute | solution.py:588
  80.4 66.2 %collective-permute-start.26 = (bf16[8,128,512]{2,1,0:T(8,128)(2,1)}, bf16[8,128,512]{2,1,0:T(8,128)(2,1)S(1)}, u32[]{:S(2)}, u32[]{:S(2)}) collective-permute-start(bf16[8,128,512]{2,1,0:T(8,128)(2,1)} %get-tuple-element.29), channel_id=1, source_target_pairs={{0,64},{4,68},{8,72},{12,76},{16,80},{20,84},{24,88},{28,92},{32,9... | collective-permute-start | bytes 3145736 | tf_op jit(solution)/shard_map/ppermute | solution.py:585
  131.0 12.7 %collective-permute-start.12 = (bf16[2,64,512]{2,1,0:T(8,128)(2,1)S(1)}, bf16[2,64,512]{2,1,0:T(8,128)(2,1)S(1)}, u32[]{:S(2)}, u32[]{:S(2)}) collective-permute-start(bf16[2,64,512]{2,1,0:T(8,128)(2,1)S(1)} %broadcast_select_fusion.1), channel_id=1, source_target_pairs={{0,16},{1,17},{2,18},{3,19},{4,20},{5,21},{6,22},{7,23},{8,24},{9,... | collective-permute-start | bytes 393224 | tf_op jit(solution)/shard_map/ppermute | solution.py:551
  137.3 66.3 %collective-permute-start.20 = (bf16[8,128,512]{2,1,0:T(8,128)(2,1)}, bf16[8,128,512]{2,1,0:T(8,128)(2,1)}, u32[]{:S(2)}, u32[]{:S(2)}) collective-permute-start(bf16[8,128,512]{2,1,0:T(8,128)(2,1)} %collective-permute-done.19.bk_r.refs_2_), channel_id=1, source_target_pairs={{0,192},{4,196},{8,200},{12,204},{16,208},{20,212},{24,216},{28,22... | collective-permute-start | bytes 3145736 | tf_op jit(solution)/shard_map/ppermute | solution.py:588
  138.5 27.1 %collective-permute-start.18 = (bf16[6,128,512]{2,1,0:T(8,128)(2,1)}, bf16[6,128,512]{2,1,0:T(8,128)(2,1)}, u32[]{:S(2)}, u32[]{:S(2)}) collective-permute-start(bf16[6,128,512]{2,1,0:T(8,128)(2,1)} %collective-permute-done.17.ak_l.refs_6_), channel_id=1, source_target_pairs={{0,64},{4,68},{8,72},{12,76},{16,80},{20,84},{24,88},{28,92},{32,9... | collective-permute-start | bytes 2359304 | tf_op jit(solution)/shard_map/ppermute | solution.py:585
  142.2 12.5 %collective-permute-start.21 = (bf16[2,128,512]{2,1,0:T(8,128)(2,1)S(1)}, bf16[2,128,512]{2,1,0:T(8,128)(2,1)S(1)}, u32[]{:S(2)}, u32[]{:S(2)}) collective-permute-start(bf16[2,128,512]{2,1,0:T(8,128)(2,1)S(1)} %get-tuple-element.38), channel_id=1, source_target_pairs={{63,0},{127,64},{191,128},{255,192}} | collective-permute-start | bytes 786440 | tf_op jit(solution)/shard_map/ppermute | solution.py:593
  143.7 72.0 %collective-permute-start.5 = (bf16[8,128,512]{2,1,0:T(8,128)(2,1)}, bf16[8,128,512]{2,1,0:T(8,128)(2,1)}, u32[]{:S(2)}, u32[]{:S(2)}) collective-permute-start(bf16[8,128,512]{2,1,0:T(8,128)(2,1)} %collective-permute-done.4.bv_r.refs_4_), channel_id=1, source_target_pairs={{0,192},{4,196},{8,200},{12,204},{16,208},{20,212},{24,216},{28,22... | collective-permute-start | bytes 3145736 | tf_op jit(solution)/shard_map/ppermute | solution.py:588
  147.6 8.8 %collective-permute-start.13 = (bf16[2,64,512]{2,1,0:T(8,128)(2,1)S(1)}, bf16[2,64,512]{2,1,0:T(8,128)(2,1)S(1)}, u32[]{:S(2)}, u32[]{:S(2)}) collective-permute-start(bf16[2,64,512]{2,1,0:T(8,128)(2,1)S(1)} %broadcast_select_fusion.2), channel_id=1, source_target_pairs={{0,32},{1,33},{2,34},{3,35},{4,36},{5,37},{6,38},{7,39},{8,40},{9,... | collective-permute-start | bytes 393224 | tf_op jit(solution)/shard_map/ppermute | solution.py:551
  154.7 60.9 %collective-permute-start.3 = (bf16[6,128,512]{2,1,0:T(8,128)(2,1)}, bf16[6,128,512]{2,1,0:T(8,128)(2,1)}, u32[]{:S(2)}, u32[]{:S(2)}) collective-permute-start(bf16[6,128,512]{2,1,0:T(8,128)(2,1)} %collective-permute-done.2.av_l.refs_8_), channel_id=1, source_target_pairs={{0,64},{4,68},{8,72},{12,76},{16,80},{20,84},{24,88},{28,92},{32,9... | collective-permute-start | bytes 2359304 | tf_op jit(solution)/shard_map/ppermute | solution.py:585
  156.3 8.5 %collective-permute-start.22 = (bf16[2,128,512]{2,1,0:T(8,128)(2,1)S(1)}, bf16[2,128,512]{2,1,0:T(8,128)(2,1)S(1)}, u32[]{:S(2)}, u32[]{:S(2)}) collective-permute-start(bf16[2,128,512]{2,1,0:T(8,128)(2,1)S(1)} %get-tuple-element.39), channel_id=1, source_target_pairs={{0,63},{64,127},{128,191},{192,255}} | collective-permute-start | bytes 786440 | tf_op jit(solution)/shard_map/ppermute | solution.py:593
  165.6 38.0 %collective-permute-start.15 = (bf16[2,64,512]{2,1,0:T(8,128)(2,1)S(1)}, bf16[2,64,512]{2,1,0:T(8,128)(2,1)S(1)}, u32[]{:S(2)}, u32[]{:S(2)}) collective-permute-start(bf16[2,64,512]{2,1,0:T(8,128)(2,1)S(1)} %broadcast_select_fusion.3.refs_0_), channel_id=1, source_target_pairs={{0,2},{1,3},{2,0},{3,1},{4,6},{5,7},{6,4},{7,5},{8,10},{9,11},{10,... | collective-permute-start | bytes 393224 | tf_op jit(solution)/shard_map/ppermute | solution.py:551
  167.0 36.6 %collective-permute-start.16 = (bf16[2,64,512]{2,1,0:T(8,128)(2,1)S(1)}, bf16[2,64,512]{2,1,0:T(8,128)(2,1)S(1)}, u32[]{:S(2)}, u32[]{:S(2)}) collective-permute-start(bf16[2,64,512]{2,1,0:T(8,128)(2,1)S(1)} %broadcast_select_fusion.3.refs_0_), channel_id=1, source_target_pairs={{0,3},{1,2},{2,1},{3,0},{4,7},{5,6},{6,5},{7,4},{8,11},{9,10},{10,... | collective-permute-start | bytes 393224 | tf_op jit(solution)/shard_map/ppermute | solution.py:551
  (30 other events, 880.0 us)

commit v6 on v5

--- a/solution.py
+++ b/solution.py
@@ -56,7 +56,7 @@
     places = first_two(gids, blocks)
     outs, (buf, in_sem, out_sem) = refs[:-3], refs[-3:]
     if joined:
-        buf = outs[0]
+        outs = (outs[0].at[0], outs[0].at[1])
     wanted = [block_at(start + i, places, blocks) for i in range(count)]
     if ends:
         wanted += [blocks - 1, 0]
@@ -68,8 +68,6 @@
             loads.append((half, i, copy))
     for half, i, load in loads:
         load.wait()
-        if joined:
-            continue
         target = outs[half].at[i] if i < count else outs[2 + i - count].at[half]
         copy = pltpu.make_async_copy(buf.at[half, i], target, out_sem.at[half, i])
         copy.start()
@@ -81,7 +79,7 @@
 def pack(gids, keys, values, start, count, joined=False, ends=False):
     shapes = [jax.ShapeDtypeStruct((count, BS, W), keys.dtype)] * 2
     if joined:
-        shapes = [pltpu.VMEM((2, count, BS, W), keys.dtype)]
+        shapes = [jax.ShapeDtypeStruct((2, count, BS, W), keys.dtype)]
     if ends:
         shapes += [jax.ShapeDtypeStruct((2, BS, W), keys.dtype)] * 2
     places = count + 2 * ends
@@ -89,9 +87,9 @@
         functools.partial(pack_kernel, start, count, joined, ends),
         out_shape=shapes,
         in_specs=[SM, HB, HB],
-        out_specs=[VM if joined else ANY] * len(shapes),
+        out_specs=[ANY] * len(shapes),
         scratch_shapes=[
-            pltpu.VMEM((2, 1 if joined else places, BS, W), keys.dtype),
+            pltpu.VMEM((2, places, BS, W), keys.dtype),
             pltpu.SemaphoreType.DMA((2, places)),
             pltpu.SemaphoreType.DMA((2, places)),
         ],
@@ -405,7 +403,7 @@
         return tuple(count + (kind == n).astype(jnp.int32) for n, count in enumerate(counts))
 
     zero = jnp.int32(0)
-    counts = lax.fori_loop(0, blocks, sort, (zero, zero, zero), unroll=True)
+    counts = lax.fori_loop(0, blocks, sort, (zero, zero, zero))
 
     for kind, (values, begin) in enumerate(((g.at[1], 0), (a_v, G_N), (b_v, G_N + A_N))):
         count = counts[kind]
@@ -441,7 +439,7 @@
         store(j).wait()
         return carry
 
-    lax.fori_loop(0, blocks, drain, 0, unroll=True)
+    lax.fori_loop(0, blocks, drain, 0)
 
 
 def last(gids, picks, parts, weights, share, acc, like):

time: 224 us -> 228 us (1.018)
    unnamed x51 -> x53, local copies, waits for them, and re-layouts: 11.2 us -> 12.6 us
where the time goes in v6:
time: 228 us; the launch traced here: 224 us
  waiting for transfers between devices  100 us (44%)
  Pallas kernels  58.7 us (26%)
  starting transfers between devices  51.1 us (22%)
  local copies, waits for them, and re-layouts  12.6 us (6%)
    ppermute x7, waiting for transfers between devices, to_left(): return lax.ppermute(v, 'blk', left)  48.1 us
    ppermute x8, waiting for transfers between devices, to_right(): return lax.ppermute(v, 'blk', right)  36.3 us
    ppermute x10, starting transfers between devices, swap(): return lax.ppermute(value, ALL, [(i, i ^ bits) for i in range(count)])  16.8 us
    pallas_call x1, Pallas kernels, near(): pl.pallas_call(functools.partial(near_kernel, blocks), out_shape=state_of...  16.2 us
    ppermute x7, starting transfers between devices, to_left(): return lax.ppermute(v, 'blk', left)  13.2 us
    pallas_call x1, Pallas kernels, window(): pl.pallas_call(functools.partial(window_kernel, blocks), out_shape=state_...  13.1 us
    unnamed x53, local copies, waits for them, and re-layouts  12.6 us
    ppermute x8, starting transfers between devices, to_right(): return lax.ppermute(v, 'blk', right)  12.1 us
  transfers between devices with their start and end apart: 29, of which 11 were waited for; matrix products, arithmetic and copies ran while one was open for 0% of the time, Pallas kernels for 23%

profile of v6, /device:TPU:2, one launch (start us, length us, event | category | flops | bytes accessed | tf_op | source)
XLA Modules:
  0.0 223.8 jit_solution(12840576392744787703)
XLA Ops:
  0.0 2.6 %pack.3.g = bf16[2,2,128,512]{3,2,1,0:T(8,128)(2,1)} custom-call(s32[2]{0:T(128)} %gids.15, bf16[16,128,512]{2,1,0:T(8,128)(2,1)} %bitcast.32, bf16[16,128,512]{2,1,0:T(8,128)(2,1)} %bitcast.35), custom_call_target="tpu_custom_call" | custom-call | bytes 1048576 | tf_op jit(solution)/shard_map/pack/pallas_call | solution.py:86
  5.0 3.3 %pack.4 = (bf16[6,128,512]{2,1,0:T(8,128)(2,1)}, bf16[6,128,512]{2,1,0:T(8,128)(2,1)}, bf16[2,128,512]{2,1,0:T(8,128)(2,1)}, bf16[2,128,512]{2,1,0:T(8,128)(2,1)}) custom-call(s32[2]{0:T(128)} %gids.15, bf16[16,128,512]{2,1,0:T(8,128)(2,1)} %bitcast.33, bf16[16,128,512]{2,1,0:T(8,128)(2,1)} %bitcast.36), custom_call_target="tpu_custom_call" | custom-call | bytes 4194304 | tf_op jit(solution)/shard_map/pack/pallas_call | solution.py:86
  9.7 8.3 %collective-permute-done.g_l.refs_5_ = bf16[2,2,128,512]{3,2,1,0:T(8,128)(2,1)S(1)} collective-permute-done((bf16[2,2,128,512]{3,2,1,0:T(8,128)(2,1)}, bf16[2,2,128,512]{3,2,1,0:T(8,128)(2,1)S(1)}, u32[]{:S(2)}, u32[]{:S(2)}) %collective-permute-start) | collective-permute-done | bytes 524320 | tf_op jit(solution)/shard_map/ppermute | solution.py:583
  19.4 25.3 %collective-permute-done.1.g_o.refs_4_.g = bf16[2,2,128,512]{3,2,1,0:T(8,128)(2,1)S(1)} collective-permute-done((bf16[2,2,128,512]{3,2,1,0:T(8,128)(2,1)S(1)}, bf16[2,2,128,512]{3,2,1,0:T(8,128)(2,1)S(1)}, u32[]{:S(2)}, u32[]{:S(2)}) %collective-permute-start.1) | collective-permute-done | bytes 524320 | tf_op jit(solution)/shard_map/ppermute | solution.py:583
  57.6 2.8 %collective-permute-start.10 = (bf16[2,64,512]{2,1,0:T(8,128)(2,1)S(1)}, bf16[2,64,512]{2,1,0:T(8,128)(2,1)S(1)}, u32[]{:S(2)}, u32[]{:S(2)}) collective-permute-start(bf16[2,64,512]{2,1,0:T(8,128)(2,1)S(1)} %select_select_fusion), channel_id=1, source_target_pairs={{0,4},{1,5},{2,6},{3,7},{4,0},{5,1},{6,2},{7,3},{8,12},{9,13},{10,... | collective-permute-start | bytes 393224 | tf_op jit(solution)/shard_map/ppermute | solution.py:549
  60.3 3.3 %pack.5 = (bf16[8,128,512]{2,1,0:T(8,128)(2,1)}, bf16[8,128,512]{2,1,0:T(8,128)(2,1)}) custom-call(s32[2]{0:T(128)} %gids.15, bf16[16,128,512]{2,1,0:T(8,128)(2,1)} %bitcast.34, bf16[16,128,512]{2,1,0:T(8,128)(2,1)} %bitcast.37), custom_call_target="tpu_custom_call" | custom-call | bytes 4194304 | tf_op jit(solution)/shard_map/pack/pallas_call | solution.py:86
  65.3 2.7 %collective-permute-start.25 = (bf16[8,128,512]{2,1,0:T(8,128)(2,1)}, bf16[8,128,512]{2,1,0:T(8,128)(2,1)S(1)}, u32[]{:S(2)}, u32[]{:S(2)}) collective-permute-start(bf16[8,128,512]{2,1,0:T(8,128)(2,1)} %get-tuple-element.37), channel_id=1, source_target_pairs={{0,64},{4,68},{8,72},{12,76},{16,80},{20,84},{24,88},{28,92},{32,9... | collective-permute-start | bytes 3145736 | tf_op jit(solution)/shard_map/ppermute | solution.py:583
  69.8 2.7 %collective-permute-done.2.av_l.refs_8_ = bf16[6,128,512]{2,1,0:T(8,128)(2,1)} collective-permute-done((bf16[6,128,512]{2,1,0:T(8,128)(2,1)}, bf16[6,128,512]{2,1,0:T(8,128)(2,1)}, u32[]{:S(2)}, u32[]{:S(2)}) %collective-permute-start.2) | collective-permute-done | bytes 786464 | tf_op jit(solution)/shard_map/ppermute | solution.py:583
  72.6 3.1 %collective-permute-start.11 = (bf16[2,64,512]{2,1,0:T(8,128)(2,1)S(1)}, bf16[2,64,512]{2,1,0:T(8,128)(2,1)S(1)}, u32[]{:S(2)}, u32[]{:S(2)}) collective-permute-start(bf16[2,64,512]{2,1,0:T(8,128)(2,1)S(1)} %broadcast_select_fusion), channel_id=1, source_target_pairs={{0,8},{1,9},{2,10},{3,11},{4,12},{5,13},{6,14},{7,15},{8,0},{9,1},... | collective-permute-start | bytes 393224 | tf_op jit(solution)/shard_map/ppermute | solution.py:549
  75.7 3.1 %collective-permute-start.24 = (bf16[6,128,512]{2,1,0:T(8,128)(2,1)S(1)}, bf16[6,128,512]{2,1,0:T(8,128)(2,1)S(1)}, u32[]{:S(2)}, u32[]{:S(2)}) collective-permute-start(bf16[6,128,512]{2,1,0:T(8,128)(2,1)S(1)} %copy-done.25), channel_id=1, source_target_pairs={{0,192},{4,196},{8,200},{12,204},{16,208},{20,212},{24,216},{28,22... | collective-permute-start | bytes 2359304 | tf_op jit(solution)/shard_map/ppermute | solution.py:586
  78.7 2.5 %collective-permute-done.11 = bf16[2,64,512]{2,1,0:T(8,128)(2,1)S(1)} collective-permute-done((bf16[2,64,512]{2,1,0:T(8,128)(2,1)S(1)}, bf16[2,64,512]{2,1,0:T(8,128)(2,1)S(1)}, u32[]{:S(2)}, u32[]{:S(2)}) %collective-permute-start.11) | collective-permute-done | bytes 131104 | tf_op jit(solution)/shard_map/ppermute | solution.py:549
  82.8 48.1 %collective-permute-done.24.refs_3_ = bf16[6,128,512]{2,1,0:T(8,128)(2,1)S(1)} collective-permute-done((bf16[6,128,512]{2,1,0:T(8,128)(2,1)S(1)}, bf16[6,128,512]{2,1,0:T(8,128)(2,1)S(1)}, u32[]{:S(2)}, u32[]{:S(2)}) %collective-permute-start.24) | collective-permute-done | bytes 786464 | tf_op jit(solution)/shard_map/ppermute | solution.py:586
  131.8 6.3 %collective-permute-start.12 = (bf16[2,64,512]{2,1,0:T(8,128)(2,1)S(1)}, bf16[2,64,512]{2,1,0:T(8,128)(2,1)S(1)}, u32[]{:S(2)}, u32[]{:S(2)}) collective-permute-start(bf16[2,64,512]{2,1,0:T(8,128)(2,1)S(1)} %broadcast_select_fusion.1), channel_id=1, source_target_pairs={{0,16},{1,17},{2,18},{3,19},{4,20},{5,21},{6,22},{7,23},{8,24},{9,... | collective-permute-start | bytes 393224 | tf_op jit(solution)/shard_map/ppermute | solution.py:549
  144.5 2.8 %collective-permute-start.5 = (bf16[8,128,512]{2,1,0:T(8,128)(2,1)}, bf16[8,128,512]{2,1,0:T(8,128)(2,1)}, u32[]{:S(2)}, u32[]{:S(2)}) collective-permute-start(bf16[8,128,512]{2,1,0:T(8,128)(2,1)} %collective-permute-done.4.bv_r.refs_4_), channel_id=1, source_target_pairs={{0,192},{4,196},{8,200},{12,204},{16,208},{20,212},{24,216},{28,22... | collective-permute-start | bytes 3145736 | tf_op jit(solution)/shard_map/ppermute | solution.py:586
  148.4 2.3 %collective-permute-start.13 = (bf16[2,64,512]{2,1,0:T(8,128)(2,1)S(1)}, bf16[2,64,512]{2,1,0:T(8,128)(2,1)S(1)}, u32[]{:S(2)}, u32[]{:S(2)}) collective-permute-start(bf16[2,64,512]{2,1,0:T(8,128)(2,1)S(1)} %broadcast_select_fusion.2), channel_id=1, source_target_pairs={{0,32},{1,33},{2,34},{3,35},{4,36},{5,37},{6,38},{7,39},{8,40},{9,... | collective-permute-start | bytes 393224 | tf_op jit(solution)/shard_map/ppermute | solution.py:549
  150.7 4.9 %collective-permute-done.21.first = bf16[2,128,512]{2,1,0:T(8,128)(2,1)S(1)} collective-permute-done((bf16[2,128,512]{2,1,0:T(8,128)(2,1)S(1)}, bf16[2,128,512]{2,1,0:T(8,128)(2,1)S(1)}, u32[]{:S(2)}, u32[]{:S(2)}) %collective-permute-start.21) | collective-permute-done | bytes 262176 | tf_op jit(solution)/shard_map/ppermute | solution.py:591
  157.2 4.6 %collective-permute-start.22 = (bf16[2,128,512]{2,1,0:T(8,128)(2,1)S(1)}, bf16[2,128,512]{2,1,0:T(8,128)(2,1)S(1)}, u32[]{:S(2)}, u32[]{:S(2)}) collective-permute-start(bf16[2,128,512]{2,1,0:T(8,128)(2,1)S(1)} %get-tuple-element.39), channel_id=1, source_target_pairs={{0,63},{64,127},{128,191},{192,255}} | collective-permute-start | bytes 786440 | tf_op jit(solution)/shard_map/ppermute | solution.py:591
  161.9 3.8 %collective-permute-done.22.last = bf16[2,128,512]{2,1,0:T(8,128)(2,1)S(1)} collective-permute-done((bf16[2,128,512]{2,1,0:T(8,128)(2,1)S(1)}, bf16[2,128,512]{2,1,0:T(8,128)(2,1)S(1)}, u32[]{:S(2)}, u32[]{:S(2)}) %collective-permute-start.22) | collective-permute-done | bytes 262176 | tf_op jit(solution)/shard_map/ppermute | solution.py:591
  171.0 13.1 %window.1 = (f32[16,4,128,128]{3,2,1,0:T(8,128)S(1)}, f32[16,4,128,128]{3,2,1,0:T(8,128)S(1)}, f32[16,4,128,128]{3,2,1,0:T(8,128)S(1)}) custom-call(s32[4]{0:T(128)S(1)} %copy-done.23, s32[16,3]{1,0:T(8,128)S(1)} %copy.14.picks, bf16[2048,512]{1,0:T(8,128)(2,1)} %q_ref.1, bf16[2048,512]{1,0:T(8,128)(2,1)} %keys.1, bf16[2048,512]{1,0:T(8,128)(2,1)} %values.1, ...), custom_call_target="tpu_custom_call" | custom-call | flops 1610612736 | bytes 20971520 | tf_op jit(solution)/shard_map/window/pallas_call | solution.py:201
  184.1 2.0 copy-done.1
  186.1 2.2 copy-done.2
  190.5 16.2 %near.1 = (f32[16,4,128,128]{3,2,1,0:T(8,128)S(1)}, f32[16,4,128,128]{3,2,1,0:T(8,128)S(1)}, f32[16,4,128,128]{3,2,1,0:T(8,128)S(1)}) custom-call(s32[2]{0:T(128)S(1)} %copy-done.21, s32[16,3]{1,0:T(8,128)S(1)} %copy.14.picks, s32[4]{0:T(128)S(1)} %copy-done.23, ...), custom_call_target="tpu_custom_call", output_to_operand_aliasing={{0}: (16, {}), {1}: (17, {}), {2}: (18, {})} | custom-call | flops 1073741824 | bytes 31457280 | tf_op jit(solution)/shard_map/near/pallas_call | solution.py:293
  206.7 12.0 %score.1 = (bf16[16,4,128,128]{3,2,1,0:T(8,128)(2,1)S(1)}, f32[16,4,128,128]{3,2,1,0:T(8,128)S(1)}, f32[16,4,128,128]{3,2,1,0:T(8,128)S(1)}) custom-call(s32[2]{0:T(128)S(1)} %copy-done.21, s32[16,3]{1,0:T(8,128)S(1)} %copy.14.picks, s32[4]{0:T(128)S(1)} %copy-done.23, ...), custom_call_target="tpu_custom_call", output_to_operand_aliasing={{1}: (12, {}), {2}: (13, {})} | custom-call | flops 1342177280 | bytes 29360128 | tf_op jit(solution)/shard_map/score/pallas_call | solution.py:371
  218.8 4.8 %last.1 = bf16[2048,512]{1,0:T(8,128)(2,1)} custom-call(s32[2]{0:T(128)S(1)} %copy-done.21, s32[16,3]{1,0:T(8,128)S(1)} %copy.14.picks, bf16[2,2,128,512]{3,2,1,0:T(8,128)(2,1)S(1)} %copy-done.4, bf16[6,128,512]{2,1,0:T(8,128)(2,1)} %collective-permute-done.3.a_v, bf16[8,128,512]{2,1,0:T(8,128)(2,1)} %collective-permute-done.5.b_v, ...), custom_call_target="tpu_custom_call" | custom-call | flops 268435456 | bytes 10485760 | tf_op jit(solution)/shard_map/last/pallas_call | solution.py:448
  (108 shorter events, 40.6 us)
Async XLA Ops:
  2.6 15.3 %collective-permute-start = (bf16[2,2,128,512]{3,2,1,0:T(8,128)(2,1)}, bf16[2,2,128,512]{3,2,1,0:T(8,128)(2,1)S(1)}, u32[]{:S(2)}, u32[]{:S(2)}) collective-permute-start(bf16[2,2,128,512]{3,2,1,0:T(8,128)(2,1)} %pack.3.g), channel_id=1, source_target_pairs={{0,64},{4,68},{8,72},{12,76},{16,80},{20,84},{24,88},{28,92},{32,9... | collective-permute-start | bytes 1572872 | tf_op jit(solution)/shard_map/ppermute | solution.py:583
  4.2 15.2 %collective-permute-start.6 = (bf16[2,2,128,512]{3,2,1,0:T(8,128)(2,1)}, bf16[2,2,128,512]{3,2,1,0:T(8,128)(2,1)S(1)}, u32[]{:S(2)}, u32[]{:S(2)}) collective-permute-start(bf16[2,2,128,512]{3,2,1,0:T(8,128)(2,1)} %pack.3.g), channel_id=1, source_target_pairs={{0,192},{4,196},{8,200},{12,204},{16,208},{20,212},{24,216},{28,22... | collective-permute-start | bytes 1572872 | tf_op jit(solution)/shard_map/ppermute | solution.py:586
  8.4 56.9 %collective-permute-start.17 = (bf16[6,128,512]{2,1,0:T(8,128)(2,1)}, bf16[6,128,512]{2,1,0:T(8,128)(2,1)}, u32[]{:S(2)}, u32[]{:S(2)}) collective-permute-start(bf16[6,128,512]{2,1,0:T(8,128)(2,1)} %get-tuple-element.36), channel_id=1, source_target_pairs={{0,64},{4,68},{8,72},{12,76},{16,80},{20,84},{24,88},{28,92},{32,9... | collective-permute-start | bytes 2359304 | tf_op jit(solution)/shard_map/ppermute | solution.py:583
  17.9 26.7 %collective-permute-start.1 = (bf16[2,2,128,512]{3,2,1,0:T(8,128)(2,1)S(1)}, bf16[2,2,128,512]{3,2,1,0:T(8,128)(2,1)S(1)}, u32[]{:S(2)}, u32[]{:S(2)}) collective-permute-start(bf16[2,2,128,512]{3,2,1,0:T(8,128)(2,1)S(1)} %collective-permute-done.g_l.refs_5_), channel_id=1, source_target_pairs={{0,64},{4,68},{8,72},{12,76},{16,80},{20,84},{24,88},{28,92},{32,9... | collective-permute-start | bytes 1572872 | tf_op jit(solution)/shard_map/ppermute | solution.py:583
  46.3 8.4 %collective-permute-start.8 = (bf16[2,64,512]{2,1,0:T(8,128)(2,1)S(1)}, bf16[2,64,512]{2,1,0:T(8,128)(2,1)S(1)}, u32[]{:S(2)}, u32[]{:S(2)}) collective-permute-start(bf16[2,64,512]{2,1,0:T(8,128)(2,1)S(1)} %get-tuple-element.33), channel_id=1, source_target_pairs={{0,2},{1,3},{2,0},{3,1},{4,6},{5,7},{6,4},{7,5},{8,10},{9,11},{10,... | collective-permute-start | bytes 393224 | tf_op jit(solution)/shard_map/ppermute | solution.py:549
  47.9 27.8 %collective-permute-start.23 = (bf16[6,128,512]{2,1,0:T(8,128)(2,1)}, bf16[6,128,512]{2,1,0:T(8,128)(2,1)S(1)}, u32[]{:S(2)}, u32[]{:S(2)}) collective-permute-start(bf16[6,128,512]{2,1,0:T(8,128)(2,1)} %get-tuple-element.36), channel_id=1, source_target_pairs={{0,192},{4,196},{8,200},{12,204},{16,208},{20,212},{24,216},{28,22... | collective-permute-start | bytes 2359304 | tf_op jit(solution)/shard_map/ppermute | solution.py:586
  51.9 20.7 %collective-permute-start.2 = (bf16[6,128,512]{2,1,0:T(8,128)(2,1)}, bf16[6,128,512]{2,1,0:T(8,128)(2,1)}, u32[]{:S(2)}, u32[]{:S(2)}) collective-permute-start(bf16[6,128,512]{2,1,0:T(8,128)(2,1)} %get-tuple-element.28), channel_id=1, source_target_pairs={{0,64},{4,68},{8,72},{12,76},{16,80},{20,84},{24,88},{28,92},{32,9... | collective-permute-start | bytes 2359304 | tf_op jit(solution)/shard_map/ppermute | solution.py:583
  57.6 10.4 %collective-permute-start.10 = (bf16[2,64,512]{2,1,0:T(8,128)(2,1)S(1)}, bf16[2,64,512]{2,1,0:T(8,128)(2,1)S(1)}, u32[]{:S(2)}, u32[]{:S(2)}) collective-permute-start(bf16[2,64,512]{2,1,0:T(8,128)(2,1)S(1)} %select_select_fusion), channel_id=1, source_target_pairs={{0,4},{1,5},{2,6},{3,7},{4,0},{5,1},{6,2},{7,3},{8,12},{9,13},{10,... | collective-permute-start | bytes 393224 | tf_op jit(solution)/shard_map/ppermute | solution.py:549
  63.6 74.5 %collective-permute-start.19 = (bf16[8,128,512]{2,1,0:T(8,128)(2,1)}, bf16[8,128,512]{2,1,0:T(8,128)(2,1)}, u32[]{:S(2)}, u32[]{:S(2)}) collective-permute-start(bf16[8,128,512]{2,1,0:T(8,128)(2,1)} %get-tuple-element.37), channel_id=1, source_target_pairs={{0,192},{4,196},{8,200},{12,204},{16,208},{20,212},{24,216},{28,22... | collective-permute-start | bytes 3145736 | tf_op jit(solution)/shard_map/ppermute | solution.py:586
  65.3 76.8 %collective-permute-start.25 = (bf16[8,128,512]{2,1,0:T(8,128)(2,1)}, bf16[8,128,512]{2,1,0:T(8,128)(2,1)S(1)}, u32[]{:S(2)}, u32[]{:S(2)}) collective-permute-start(bf16[8,128,512]{2,1,0:T(8,128)(2,1)} %get-tuple-element.37), channel_id=1, source_target_pairs={{0,64},{4,68},{8,72},{12,76},{16,80},{20,84},{24,88},{28,92},{32,9... | collective-permute-start | bytes 3145736 | tf_op jit(solution)/shard_map/ppermute | solution.py:583
  68.0 71.4 %collective-permute-start.4 = (bf16[8,128,512]{2,1,0:T(8,128)(2,1)}, bf16[8,128,512]{2,1,0:T(8,128)(2,1)}, u32[]{:S(2)}, u32[]{:S(2)}) collective-permute-start(bf16[8,128,512]{2,1,0:T(8,128)(2,1)} %get-tuple-element.29), channel_id=1, source_target_pairs={{0,192},{4,196},{8,200},{12,204},{16,208},{20,212},{24,216},{28,22... | collective-permute-start | bytes 3145736 | tf_op jit(solution)/shard_map/ppermute | solution.py:586
  72.6 8.7 %collective-permute-start.11 = (bf16[2,64,512]{2,1,0:T(8,128)(2,1)S(1)}, bf16[2,64,512]{2,1,0:T(8,128)(2,1)S(1)}, u32[]{:S(2)}, u32[]{:S(2)}) collective-permute-start(bf16[2,64,512]{2,1,0:T(8,128)(2,1)S(1)} %broadcast_select_fusion), channel_id=1, source_target_pairs={{0,8},{1,9},{2,10},{3,11},{4,12},{5,13},{6,14},{7,15},{8,0},{9,1},... | collective-permute-start | bytes 393224 | tf_op jit(solution)/shard_map/ppermute | solution.py:549
  75.7 55.3 %collective-permute-start.24 = (bf16[6,128,512]{2,1,0:T(8,128)(2,1)S(1)}, bf16[6,128,512]{2,1,0:T(8,128)(2,1)S(1)}, u32[]{:S(2)}, u32[]{:S(2)}) collective-permute-start(bf16[6,128,512]{2,1,0:T(8,128)(2,1)S(1)} %copy-done.25), channel_id=1, source_target_pairs={{0,192},{4,196},{8,200},{12,204},{16,208},{20,212},{24,216},{28,22... | collective-permute-start | bytes 2359304 | tf_op jit(solution)/shard_map/ppermute | solution.py:586
  81.2 66.2 %collective-permute-start.26 = (bf16[8,128,512]{2,1,0:T(8,128)(2,1)}, bf16[8,128,512]{2,1,0:T(8,128)(2,1)S(1)}, u32[]{:S(2)}, u32[]{:S(2)}) collective-permute-start(bf16[8,128,512]{2,1,0:T(8,128)(2,1)} %get-tuple-element.29), channel_id=1, source_target_pairs={{0,64},{4,68},{8,72},{12,76},{16,80},{20,84},{24,88},{28,92},{32,9... | collective-permute-start | bytes 3145736 | tf_op jit(solution)/shard_map/ppermute | solution.py:583
  131.8 12.7 %collective-permute-start.12 = (bf16[2,64,512]{2,1,0:T(8,128)(2,1)S(1)}, bf16[2,64,512]{2,1,0:T(8,128)(2,1)S(1)}, u32[]{:S(2)}, u32[]{:S(2)}) collective-permute-start(bf16[2,64,512]{2,1,0:T(8,128)(2,1)S(1)} %broadcast_select_fusion.1), channel_id=1, source_target_pairs={{0,16},{1,17},{2,18},{3,19},{4,20},{5,21},{6,22},{7,23},{8,24},{9,... | collective-permute-start | bytes 393224 | tf_op jit(solution)/shard_map/ppermute | solution.py:549
  138.1 68.5 %collective-permute-start.20 = (bf16[8,128,512]{2,1,0:T(8,128)(2,1)}, bf16[8,128,512]{2,1,0:T(8,128)(2,1)}, u32[]{:S(2)}, u32[]{:S(2)}) collective-permute-start(bf16[8,128,512]{2,1,0:T(8,128)(2,1)} %collective-permute-done.19.bk_r.refs_2_), channel_id=1, source_target_pairs={{0,192},{4,196},{8,200},{12,204},{16,208},{20,212},{24,216},{28,22... | collective-permute-start | bytes 3145736 | tf_op jit(solution)/shard_map/ppermute | solution.py:586
  139.4 27.1 %collective-permute-start.18 = (bf16[6,128,512]{2,1,0:T(8,128)(2,1)}, bf16[6,128,512]{2,1,0:T(8,128)(2,1)}, u32[]{:S(2)}, u32[]{:S(2)}) collective-permute-start(bf16[6,128,512]{2,1,0:T(8,128)(2,1)} %collective-permute-done.17.ak_l.refs_6_), channel_id=1, source_target_pairs={{0,64},{4,68},{8,72},{12,76},{16,80},{20,84},{24,88},{28,92},{32,9... | collective-permute-start | bytes 2359304 | tf_op jit(solution)/shard_map/ppermute | solution.py:583
  143.1 12.5 %collective-permute-start.21 = (bf16[2,128,512]{2,1,0:T(8,128)(2,1)S(1)}, bf16[2,128,512]{2,1,0:T(8,128)(2,1)S(1)}, u32[]{:S(2)}, u32[]{:S(2)}) collective-permute-start(bf16[2,128,512]{2,1,0:T(8,128)(2,1)S(1)} %get-tuple-element.38), channel_id=1, source_target_pairs={{63,0},{127,64},{191,128},{255,192}} | collective-permute-start | bytes 786440 | tf_op jit(solution)/shard_map/ppermute | solution.py:591
  144.5 74.2 %collective-permute-start.5 = (bf16[8,128,512]{2,1,0:T(8,128)(2,1)}, bf16[8,128,512]{2,1,0:T(8,128)(2,1)}, u32[]{:S(2)}, u32[]{:S(2)}) collective-permute-start(bf16[8,128,512]{2,1,0:T(8,128)(2,1)} %collective-permute-done.4.bv_r.refs_4_), channel_id=1, source_target_pairs={{0,192},{4,196},{8,200},{12,204},{16,208},{20,212},{24,216},{28,22... | collective-permute-start | bytes 3145736 | tf_op jit(solution)/shard_map/ppermute | solution.py:586
  148.4 8.8 %collective-permute-start.13 = (bf16[2,64,512]{2,1,0:T(8,128)(2,1)S(1)}, bf16[2,64,512]{2,1,0:T(8,128)(2,1)S(1)}, u32[]{:S(2)}, u32[]{:S(2)}) collective-permute-start(bf16[2,64,512]{2,1,0:T(8,128)(2,1)S(1)} %broadcast_select_fusion.2), channel_id=1, source_target_pairs={{0,32},{1,33},{2,34},{3,35},{4,36},{5,37},{6,38},{7,39},{8,40},{9,... | collective-permute-start | bytes 393224 | tf_op jit(solution)/shard_map/ppermute | solution.py:549
  155.6 63.1 %collective-permute-start.3 = (bf16[6,128,512]{2,1,0:T(8,128)(2,1)}, bf16[6,128,512]{2,1,0:T(8,128)(2,1)}, u32[]{:S(2)}, u32[]{:S(2)}) collective-permute-start(bf16[6,128,512]{2,1,0:T(8,128)(2,1)} %collective-permute-done.2.av_l.refs_8_), channel_id=1, source_target_pairs={{0,64},{4,68},{8,72},{12,76},{16,80},{20,84},{24,88},{28,92},{32,9... | collective-permute-start | bytes 2359304 | tf_op jit(solution)/shard_map/ppermute | solution.py:583
  157.2 8.5 %collective-permute-start.22 = (bf16[2,128,512]{2,1,0:T(8,128)(2,1)S(1)}, bf16[2,128,512]{2,1,0:T(8,128)(2,1)S(1)}, u32[]{:S(2)}, u32[]{:S(2)}) collective-permute-start(bf16[2,128,512]{2,1,0:T(8,128)(2,1)S(1)} %get-tuple-element.39), channel_id=1, source_target_pairs={{0,63},{64,127},{128,191},{192,255}} | collective-permute-start | bytes 786440 | tf_op jit(solution)/shard_map/ppermute | solution.py:591
  166.5 40.2 %collective-permute-start.15 = (bf16[2,64,512]{2,1,0:T(8,128)(2,1)S(1)}, bf16[2,64,512]{2,1,0:T(8,128)(2,1)}, u32[]{:S(2)}, u32[]{:S(2)}) collective-permute-start(bf16[2,64,512]{2,1,0:T(8,128)(2,1)S(1)} %broadcast_select_fusion.3.refs_0_), channel_id=1, source_target_pairs={{0,2},{1,3},{2,0},{3,1},{4,6},{5,7},{6,4},{7,5},{8,10},{9,11},{10,... | collective-permute-start | bytes 393224 | tf_op jit(solution)/shard_map/ppermute | solution.py:549
  167.9 38.8 %collective-permute-start.16 = (bf16[2,64,512]{2,1,0:T(8,128)(2,1)S(1)}, bf16[2,64,512]{2,1,0:T(8,128)(2,1)}, u32[]{:S(2)}, u32[]{:S(2)}) collective-permute-start(bf16[2,64,512]{2,1,0:T(8,128)(2,1)S(1)} %broadcast_select_fusion.3.refs_0_), channel_id=1, source_target_pairs={{0,3},{1,2},{2,1},{3,0},{4,7},{5,6},{6,5},{7,4},{8,11},{9,10},{10,... | collective-permute-start | bytes 393224 | tf_op jit(solution)/shard_map/ppermute | solution.py:549
  (31 other events, 983.8 us)
